TPU v7x, 256 devices: a whole 4x4x8 slice. The times are simulated.
256 devices in a mesh: branch: 4 (over y_hi, core), dap: 64 (over x, z, y_lo).
Axes of the slice: x: 4, y: 4 (y_hi: 2, y_lo: 2; y = y_hi * 2 + y_lo), z: 8, core: 2. Of those that a mesh axis runs over, the one named last changes fastest.
Arguments:
- alignment: bfloat16 [512, 512, 256], P('dap'), may hold values from -24 to 24
- pair_rep: bfloat16 [512, 512, 128], P('dap', 'branch'), may hold values from -6 to 6
- align_mask: int32 [512, 512], replicated, may hold values from 0 to 1, as said below
- residue_mask: int32 [512], replicated, may hold values from 0 to 1, as said below
- bias_weight: bfloat16 [128, 8], replicated, may hold values from -1 to 1
- row_proj_weight: bfloat16 [4, 256, 256], P(None, None, 'branch'), may hold values from -0.375 to 0.375
- row_out_weight: bfloat16 [256, 256], replicated, may hold values from -1 to 1
- column_proj_weight: bfloat16 [4, 256, 256], P(None, None, 'branch'), may hold values from -0.375 to 0.375
- column_out_weight: bfloat16 [256, 256], replicated, may hold values from -1 to 1
- outer_factor_weight: bfloat16 [256, 64], replicated, may hold values from -0.375 to 0.375
- outer_out: bfloat16 [1024, 128], replicated, may hold values from -0.375 to 0.375
Outputs:
- updated_alignment: bfloat16 [512, 512, 256], P(None, 'dap')
- pair_out: bfloat16 [512, 512, 128], P('dap', 'branch')
Inputs may be any that keep to these rules, and one draw needn't show every extreme that they name: `align_mask`: the first alignment is all ones; in every other alignment the ones form one contiguous run of residues that is never empty. `residue_mask`: ones on a leading run of residues and zeros after it; both values occur.
All inputs are finite; a program needn't handle non-finite values.
Results may differ from a plain program's by a relative error of at most 0.0085.
Values may be sent and summed in bfloat16 or wider, within the bound.
A program may use at most 128 MiB of HBM per device.

v0:
```python
import math

import jax
import jax.numpy as jnp
from jax import lax
from jax.sharding import PartitionSpec as P

ATTN_HEAD_COUNT = 8
HEAD_CHANNELS = 32
FACTOR_CHANNELS = 32


norm_eps = 1e-05
count_eps = 0.001


def layer_normalize(values):
    centre = jnp.mean(values, axis=-1, keepdims=True)
    centred = values - centre
    spread = jnp.mean(centred * centred, axis=-1, keepdims=True)
    return centred * lax.rsqrt(spread + norm_eps)


def attend_heads(inputs, key_mask, proj_weight, out_weight, score_bias):
    batch = inputs.shape[0]
    length = inputs.shape[1]
    local_width = proj_weight.shape[2]
    local_heads = local_width // HEAD_CHANNELS
    normed = layer_normalize(inputs.astype(jnp.float32)).astype(jnp.bfloat16)
    projected = jnp.einsum("blc,kcd->kbld", normed, proj_weight, preferred_element_type=jnp.float32)
    triple = (
        projected[:3].astype(jnp.bfloat16).reshape(3, batch, length, local_heads, HEAD_CHANNELS)
    )
    gating = jax.nn.sigmoid(projected[3])

    def attend_one(operands):
        queries, key_rows, value_rows, mask_row = operands
        scores = jnp.einsum(
            "ihd,jhd->hij", queries, key_rows, preferred_element_type=jnp.float32
        ) / math.sqrt(HEAD_CHANNELS)
        if score_bias is not None:
            scores = scores + score_bias.astype(jnp.float32)
        raised = jnp.exp(scores) * mask_row[None, None, :]
        weights = (raised / jnp.sum(raised, axis=-1, keepdims=True)).astype(jnp.bfloat16)
        return jnp.einsum("hij,jhd->ihd", weights, value_rows, preferred_element_type=jnp.float32)

    attended_rows = lax.map(attend_one, (triple[0], triple[1], triple[2], key_mask))
    heads_out = (attended_rows.reshape(batch, length, local_width) * gating).astype(jnp.bfloat16)
    gathered = lax.all_gather(heads_out, "branch", axis=2, tiled=True)
    update = jnp.einsum("blf,fc->blc", gathered, out_weight, preferred_element_type=jnp.float32)
    return (inputs.astype(jnp.float32) + update).astype(jnp.bfloat16)


def per_device(
    alignment,
    pair_rep,
    align_mask,
    residue_mask,
    bias_weight,
    row_proj_weight,
    row_out_weight,
    column_proj_weight,
    column_out_weight,
    outer_factor_weight,
    outer_out,
):
    branch_count = lax.axis_size("branch")
    dap_count = lax.axis_size("dap")
    branch_index = lax.axis_index("branch")
    dap_index = lax.axis_index("dap")
    seq_dev = alignment.shape[0]
    res_dev = pair_rep.shape[0]
    quarter = pair_rep.shape[1]
    total_seqs = align_mask.shape[0]
    local_heads = ATTN_HEAD_COUNT // branch_count
    float_mask = align_mask.astype(jnp.float32)
    res_float = residue_mask.astype(jnp.float32)
    pair_normed = layer_normalize(pair_rep.astype(jnp.float32)).astype(jnp.bfloat16)
    bias_block = jnp.einsum(
        "ijc,ch->hij", pair_normed, bias_weight, preferred_element_type=jnp.float32
    ).astype(jnp.bfloat16)
    bias_wide = lax.all_gather(bias_block, "branch", axis=2, tiled=True)
    bias_full = lax.all_gather(bias_wide, "dap", axis=1, tiled=True)
    pair_score_bias = lax.dynamic_slice_in_dim(
        bias_full, branch_index * local_heads, local_heads, 0
    )
    sequence_row_mask = lax.dynamic_slice_in_dim(float_mask, dap_index * seq_dev, seq_dev, 0)
    row_alignment = attend_heads(
        alignment, sequence_row_mask, row_proj_weight, row_out_weight, pair_score_bias
    )
    send_mask = sequence_row_mask.astype(jnp.bfloat16)
    blocked_rows = row_alignment.reshape(seq_dev, dap_count, res_dev, row_alignment.shape[2])
    blocked_mask = send_mask.reshape(seq_dev, dap_count, res_dev)
    moved_rows = lax.all_to_all(blocked_rows, "dap", split_axis=1, concat_axis=0, tiled=True)
    moved_mask = lax.all_to_all(blocked_mask, "dap", split_axis=1, concat_axis=0, tiled=True)
    seq_total = moved_rows.shape[0]
    items = moved_rows.shape[2]
    flat_rows = moved_rows.reshape(seq_total, items, moved_rows.shape[3])
    flat_mask = moved_mask.reshape(seq_total, items)
    transposed_rows = jnp.swapaxes(flat_rows, 0, 1)
    key_mask = jnp.swapaxes(flat_mask, 0, 1).astype(jnp.float32)
    attended_rows = attend_heads(
        transposed_rows, key_mask, column_proj_weight, column_out_weight, None
    )
    column_alignment = jnp.swapaxes(attended_rows, 0, 1)
    outer_mean_normed = layer_normalize(column_alignment.astype(jnp.float32)).astype(jnp.bfloat16)
    projected = jnp.einsum(
        "src,ce->sre", outer_mean_normed, outer_factor_weight, preferred_element_type=jnp.float32
    )
    factor_pairs = (projected * flat_mask.astype(jnp.float32)[:, :, None]).astype(jnp.bfloat16)
    column_alignment, factor_pairs = (column_alignment, factor_pairs)
    blocked_out = column_alignment.reshape(seq_total, 1, items, column_alignment.shape[2])
    blocked_factors = factor_pairs.reshape(seq_total, 1, items, factor_pairs.shape[2])
    updated_alignment = blocked_out.reshape(total_seqs, res_dev, blocked_out.shape[3])
    factor_pairs = blocked_factors.reshape(total_seqs, res_dev, blocked_factors.shape[3])
    left_side = factor_pairs[:, :, :FACTOR_CHANNELS]
    right_local = factor_pairs[:, :, FACTOR_CHANNELS:]
    col_start = branch_index * quarter
    row_start = dap_index * res_dev
    mask_rows = lax.dynamic_slice_in_dim(align_mask, row_start, res_dev, 1).astype(jnp.bfloat16)
    mask_cols = lax.dynamic_slice_in_dim(align_mask, col_start, quarter, 1).astype(jnp.bfloat16)
    counts = jnp.einsum("si,sj->ij", mask_rows, mask_cols, preferred_element_type=jnp.float32)
    live_rows = lax.dynamic_slice_in_dim(res_float, row_start, res_dev, 0)
    live_cols = lax.dynamic_slice_in_dim(res_float, col_start, quarter, 0)
    outer_weight = outer_out.astype(jnp.float32)
    right_all = lax.all_gather(right_local, "dap", axis=1, tiled=True)
    right_mine = lax.dynamic_slice_in_dim(right_all, col_start, quarter, 1)
    outer_sums = jnp.einsum(
        "sic,sje->ijce", left_side, right_mine, preferred_element_type=jnp.float32
    )
    outer_sums = outer_sums.reshape(res_dev, quarter, FACTOR_CHANNELS * FACTOR_CHANNELS)
    update = jnp.einsum("ijf,fz->ijz", outer_sums, outer_weight, precision=lax.Precision.HIGHEST)
    live = live_rows[:, None] * live_cols[None, :]
    update = update / (counts[:, :, None] + count_eps) * live[:, :, None]
    pair_out = (pair_rep.astype(jnp.float32) + update).astype(jnp.bfloat16)
    return (updated_alignment, pair_out)


def solution(mesh):
    placed = (
        P("dap", None, None),
        P("dap", "branch", None),
        P(),
        P(),
        P(),
        P(None, None, "branch"),
        P(),
        P(None, None, "branch"),
        P(),
        P(),
        P(),
    )
    return jax.shard_map(
        per_device,
        mesh=mesh,
        in_specs=placed,
        out_specs=(P(None, "dap", None), P("dap", "branch", None)),
        check_vma=False,
    )
```

profile of v0, /device:TPU:32, one launch (start us, length us, event | category | flops | bytes accessed | tf_op | source)
XLA Modules:
  0.0 911.8 jit_solution(9711300610161135919)
XLA Ops:
  11.2 7.2 all_gather.15
  22.9 3.1 fusion.89
  27.3 296.0 %all-gather.5.cloned.1.call-done = bf16[8,512,512]{2,0,1:T(8,128)(2,1)} async-done(((bf16[8,8,512]{2,0,1:T(8,128)(2,1)}), bf16[8,512,512]{2,0,1:T(8,128)(2,1)}) %all-gather.5.cloned.1.call-update) | async-done | bytes 4194320 | tf_op jit(solution)/shard_map/all_gather | solution.py:83
  323.3 3.3 constant_dynamic-slice_fusion.3
  329.1 27.4 %while.20 = (s32[]{:T(128)}, f32[8,512,2,32]{1,3,2,0:T(8,128)}, bf16[8,512,2,32]{1,3,2,0:T(8,128)(2,1)}, bf16[8,512,2,32]{1,3,2,0:T(8,128)(2,1)}, bf16[8,512,2,3...) while((s32[]{:T(128)}, f32[8,512,2,32]{1,3,2,0:T(8,128)}, ...), condition=%wide.region_6.7_spmd, body=%wide.region_4.6_spmd.sunk | while | flops 70256128 | bytes 7675993 | solution.py:47
  356.5 2.8 fusion.69
  360.2 7.8 all-to-all-start.1
  368.0 19.6 %all-gather.7.cloned.1.call-done = bf16[8,512,256]{1,2,0:T(8,128)(2,1)} async-done(((bf16[8,512,64]{1,2,0:T(8,128)(2,1)}), bf16[8,512,256]{1,2,0:T(8,128)(2,1)}) %all-gather.7.cloned.1.call-update) | async-done | bytes 2097168 | tf_op jit(solution)/shard_map/all_gather | solution.py:49
  391.6 9.9 %all-to-all-start = ((bf16[8,64,8,256]{3,2,0,1:T(8,128)(2,1)}), bf16[8,64,8,256]{3,2,0,1:T(8,128)(2,1)S(1)}, u32[]{:S(2)}, u32[]{:S(2)}) async-start(bf16[8,64,8,256]{3,2,0,1:T(8,128)(2,1)} %copy.57), calls=%async_computation | async-start | bytes 4194304 | tf_op jit(solution)/shard_map/all_to_all | solution.py:94
  401.9 50.2 %all-to-all-done = bf16[8,64,8,256]{3,2,0,1:T(8,128)(2,1)S(1)} async-done(((bf16[8,64,8,256]{3,2,0,1:T(8,128)(2,1)}), bf16[8,64,8,256]{3,2,0,1:T(8,128)(2,1)S(1)}, u32[]{:S(2)}, u32[]{:S(2)}) %all-to-all-start) | async-done | bytes 2097184 | tf_op jit(solution)/shard_map/all_to_all | solution.py:94
  454.5 2.8 reduce_sum.94
  457.6 3.2 multiply_reduce_fusion
  461.1 2.9 fusion.38
  464.0 3.0 fusion.90
  467.3 9.2 %while.21 = (s32[]{:T(128)}, f32[8,512,2,32]{1,3,2,0:T(8,128)S(1)}, bf16[8,512,2,32]{1,3,2,0:T(8,128)(2,1)S(1)}, bf16[8,512,2,32]{1,3,2,0:T(8,128)(2,1)S(1)}, bf...) while((s32[]{:T(128)}, f32[8,512,2,32]{1,3,2,0:T(8,128)S(1)}, ...), condition=%wide.region_11.12_spmd, body=%wide.region_9.11_spmd.sunk | while | flops 70777856 | bytes 4540497 | solution.py:47
  478.9 5.3 copy.66
  484.3 20.5 %all-gather.9.cloned.1.call-done = bf16[8,512,256]{1,2,0:T(8,128)(2,1)} async-done(((bf16[8,512,64]{1,2,0:T(8,128)(2,1)}), bf16[8,512,256]{1,2,0:T(8,128)(2,1)}) %all-gather.9.cloned.1.call-update) | async-done | bytes 2097168 | tf_op jit(solution)/shard_map/all_gather | solution.py:49
  504.7 3.9 convert_reduce_fusion.1
  512.4 3.1 copy.71
  515.5 367.1 %all-gather.11.cloned.1.call-done = bf16[512,512,32]{0,2,1:T(8,128)(2,1)} async-done(((bf16[512,8,32]{0,2,1:T(8,128)(2,1)}), bf16[512,512,32]{0,2,1:T(8,128)(2,1)}) %all-gather.11.cloned.1.call-update) | async-done | bytes 16777232 | tf_op jit(solution)/shard_map/all_gather | solution.py:126
  882.5 4.7 constant_dynamic-slice_fusion.2
  887.2 7.9 copy.84
  895.1 3.4 fusion.35
  901.0 4.3 fusion.57
  (117 shorter events, 65.6 us)
Async XLA Ops:
  7.2 893.8 %copy-start = (bf16[1024,128]{1,0:T(8,128)(2,1)S(1)}, bf16[1024,128]{1,0:T(8,128)(2,1)}, u32[]{:S(2)}) copy-start(bf16[1024,128]{1,0:T(8,128)(2,1)} %param.25) | copy-start | bytes 786436
  7.2 14.3 %copy-start.1 = (bf16[8,512,256]{2,1,0:T(8,128)(2,1)S(1)}, bf16[8,512,256]{2,1,0:T(8,128)(2,1)}, u32[]{:S(2)}) copy-start(bf16[8,512,256]{2,1,0:T(8,128)(2,1)} %param.15) | copy-start | bytes 6291460
  7.2 316.1 %all-gather.5.cloned.1.call-start = ((), (), s32[]{:S(2)}) async-start(), calls=%async_computation.2 | async-start | bytes 4259840 | tf_op jit(solution)/shard_map/all_gather | solution.py:83
  18.5 369.2 %all-gather.7.cloned.1.call-start = ((), (), s32[]{:S(2)}) async-start(), calls=%async_computation.3 | async-start | bytes 2621440 | tf_op jit(solution)/shard_map/all_gather | solution.py:49
  19.3 3.6 copy-start.4
  356.5 31.2 %copy-start.2 = (bf16[8,512,256]{2,1,0:T(8,128)(2,1)S(1)}, bf16[8,512,256]{2,1,0:T(8,128)(2,1)}, u32[]{:S(2)}) copy-start(bf16[8,512,256]{2,1,0:T(8,128)(2,1)} %param.15) | copy-start | bytes 6291460
  356.5 31.2 %copy-start.6 = (bf16[256,256]{1,0:T(8,128)(2,1)S(1)}, bf16[256,256]{1,0:T(8,128)(2,1)}, u32[]{:S(2)}) copy-start(bf16[256,256]{1,0:T(8,128)(2,1)} %param.21) | copy-start | bytes 393220
  360.2 31.4 %all-to-all-start.1 = ((bf16[8,64,8]{2,0,1:T(8,128)(2,1)}), bf16[8,64,8]{2,0,1:T(8,128)(2,1)S(1)}, u32[]{:S(2)}, u32[]{:S(2)}) async-start(bf16[8,64,8]{2,0,1:T(8,128)(2,1)} %copy.63), calls=%async_computation.1 | async-start | bytes 262144 | tf_op jit(solution)/shard_map/all_to_all | solution.py:95
  391.6 60.4 %all-to-all-start = ((bf16[8,64,8,256]{3,2,0,1:T(8,128)(2,1)}), bf16[8,64,8,256]{3,2,0,1:T(8,128)(2,1)S(1)}, u32[]{:S(2)}, u32[]{:S(2)}) async-start(bf16[8,64,8,256]{3,2,0,1:T(8,128)(2,1)} %copy.57), calls=%async_computation | async-start | bytes 4194304 | tf_op jit(solution)/shard_map/all_to_all | solution.py:94
  401.5 103.2 %all-gather.9.cloned.1.call-start = ((), (), s32[]{:S(2)}) async-start(), calls=%async_computation.4 | async-start | bytes 2621440 | tf_op jit(solution)/shard_map/all_gather | solution.py:49
  461.0 2.9 copy-start.7
  478.9 403.7 %all-gather.11.cloned.1.call-start = ((), (), s32[]{:S(2)}) async-start(), calls=%async_computation.5 | async-start | bytes 17039360 | tf_op jit(solution)/shard_map/all_gather | solution.py:126
  478.9 25.8 %copy-start.5 = (bf16[256,256]{1,0:T(8,128)(2,1)S(1)}, bf16[256,256]{1,0:T(8,128)(2,1)}, u32[]{:S(2)}) copy-start(bf16[256,256]{1,0:T(8,128)(2,1)} %param.23) | copy-start | bytes 393220
  508.6 0.8 copy-start.9
  509.4 1.5 copy-start.8
  898.6 2.4 copy-start.3
Sparse Core Ops, SparseCore 0:
  18.6 304.6 all-gather.4
  359.4 28.1 all-gather.6
  479.0 25.6 all-gather.8
  511.0 371.5 all-gather.10
where the time goes:
time: 914 us; the launch traced here: 912 us
  waiting for transfers between devices  753 us (82%)
  matrix products  59.9 us (7%)
  local copies, waits for them, and re-layouts  35 us (4%)
  other arithmetic  24 us (3%)
  starting transfers between devices  18.1 us (2%)
  between operations  14.1 us (2%)
    all_gather x1, waiting for transfers between devices, per_device(): right_all = lax.all_gather(right_local, 'dap', axis=1, tiled=True)  367 us
    all_gather x1, waiting for transfers between devices, per_device(): bias_full = lax.all_gather(bias_wide, 'dap', axis=1, tiled=True)  296 us
    all_to_all x1, waiting for transfers between devices, per_device(): lax.all_to_all(blocked_rows, 'dap', split_axis=1, concat_axis=0, tiled=True)  50.2 us
    all_gather x2, waiting for transfers between devices, attend_heads(): gathered = lax.all_gather(heads_out, 'branch', axis=2, tiled=True)  40 us
    dot_general x16, matrix products, attend_one(): jnp.einsum('hij,jhd->ihd', weights, value_rows, preferred_element_type=jn...  19.5 us
  transfers between devices with their start and end apart: 6, of which 5 were waited for; matrix products, arithmetic and copies ran while one was open for 3% of the time, Pallas kernels for 0%

commit v1 on v0

v1 whole, which is shorter than its diff:
```python
import functools
import math

import jax
import jax.numpy as jnp
from jax import lax
from jax.experimental import pallas as pl
from jax.experimental.pallas import tpu as pltpu
from jax.sharding import PartitionSpec as P

HEADS = 8
HEAD = 32
FACTOR = 32
norm_eps = 1e-05
count_eps = 0.001
SCALE = 1.0 / math.sqrt(HEAD)
F32 = jnp.float32
BF16 = jnp.bfloat16
MESH = pl.DeviceIdType.MESH
VMEM_LIMIT = 60 * 1024 * 1024
SEQS = 512
TILE = 128
NT = (((1,), (1,)), ((), ()))
TN = (((0,), (1,)), ((), ()))


def normalize(values):
    centre = jnp.mean(values, axis=-1, keepdims=True)
    centred = values - centre
    spread = jnp.mean(centred * centred, axis=-1, keepdims=True)
    return centred * lax.rsqrt(spread + norm_eps)


def dot(a, b, dims=(((1,), (0,)), ((), ()))):
    return lax.dot_general(a, b, dims, preferred_element_type=F32)


def lane_block(rows, index):
    lanes = lax.broadcasted_iota(jnp.int32, (rows, 128), 1)
    return (lanes // HEAD == index).astype(F32)


def attend(q_s, k_s, g_s, rhs_s, o_s, bias_of, mask_of):
    def run(stable):
        def tile(step, extremes):
            rows = pl.ds(pl.multiple_of(step * TILE, TILE), TILE)
            q = q_s[rows, :]
            total = None
            for n in range(4):
                qn = q * lane_block(TILE, n).astype(BF16)
                scores = dot(qn, k_s[...], NT) * SCALE
                if bias_of is not None:
                    scores = scores + bias_of(step, n)
                if stable:
                    scores = jnp.where(mask_of(n) > 0.0, scores, -1e30)
                    scores = scores - jnp.max(scores, axis=1, keepdims=True)
                raised = jnp.exp(scores).astype(BF16)
                part = dot(raised, rhs_s[n * SEQS : (n + 1) * SEQS, :])
                total = part if total is None else total + part
            sums = total[:, 128:]
            o_s[rows, :] = total[:, :128] / sums * g_s[rows, :]
            low, high = extremes
            folded = sums.reshape(TILE // 8, 8, 128)
            return jnp.minimum(low, jnp.min(folded, axis=0)), jnp.maximum(
                high, jnp.max(folded, axis=0)
            )

        start = (jnp.full((8, 128), 1.0, F32), jnp.full((8, 128), 1.0, F32))
        return lax.fori_loop(0, SEQS // TILE, tile, start)

    low, high = run(False)
    fine = jnp.logical_and(jnp.min(low) > 1e-30, jnp.max(high) < 1e30)

    @pl.when(jnp.logical_not(fine))
    def _():
        run(True)


def fill_rhs(rhs_s, values, mask):
    for n in range(4):
        block = mask * lane_block(SEQS, n)
        rhs_s[n * SEQS : (n + 1) * SEQS, :128] = (values * block).astype(BF16)
        rhs_s[n * SEQS : (n + 1) * SEQS, 128:] = block.astype(BF16)


def bias_kernel(pair_ref, weight_ref, out_ref):
    rows, cols, width = pair_ref.shape
    x = pair_ref[...].astype(F32).reshape(rows * cols, width)
    normed = normalize(x).astype(BF16)
    res = dot(weight_ref[...], normed, TN)
    for i in range(rows):
        out_ref[:, i, :] = res[:, i * cols : (i + 1) * cols].astype(BF16)


def row_kernel(
    x_ref, w_ref, bias_ref, maskcol_ref, maskrow_ref, out_ref, q_s, k_s, g_s, rhs_s, o_s, buf
):
    pair = pl.program_id(0)
    normed = [normalize(x_ref[p].astype(F32)).astype(BF16) for p in range(2)]
    both = jnp.concatenate(normed, axis=1)
    q_s[...] = dot(both, w_ref[:, :128]).astype(BF16)
    k_s[...] = dot(both, w_ref[:, 128:256]).astype(BF16)
    values = dot(both, w_ref[:, 256:384]).astype(BF16).astype(F32)
    fill_rhs(rhs_s, values, maskcol_ref[0].astype(F32))
    g_s[...] = jax.nn.sigmoid(dot(both, w_ref[:, 384:]))

    def bias_of(step, n):
        pieces = []
        for b in range(4):
            piece = bias_ref[pl.ds(step * (TILE // 8), TILE // 8), b, n % 2]
            pieces.append(piece.astype(F32).reshape(TILE, 128))
        return jnp.concatenate(pieces, axis=1)

    attend(q_s, k_s, g_s, rhs_s, o_s, bias_of, lambda n: maskrow_ref[0, n // 2 : n // 2 + 1, :])
    for k in range(2):
        buf[pl.ds(pair * 2 + k, 256, stride=8), :] = o_s[pl.ds(k, 256, stride=2), :]

    @pl.when(pair == pl.num_programs(0) - 1)
    def _():
        out_ref[...] = buf[...].reshape(256, 8, 128).astype(BF16)


def column_kernel(
    a_ref,
    res_ref,
    wrow_ref,
    wcol_ref,
    wout_ref,
    wfac_ref,
    maskcol_ref,
    maskrow_ref,
    upd_ref,
    left_ref,
    right_ref,
    x_s,
    msa_s,
    n_s,
    q_s,
    k_s,
    g_s,
    rhs_s,
    o_s,
    heads_s,
):
    k = pl.program_id(0)

    @pl.when(k == 0)
    def _():
        pieces = [a_ref[:, b].astype(F32).reshape(SEQS, 128).astype(BF16) for b in range(4)]
        x = dot(jnp.concatenate(pieces, axis=1), wrow_ref[...])
        for j in range(4):
            x_s[j] = x[:, j * 128 : (j + 1) * 128]

    mine = [x_s[j, pl.ds(k, 256, stride=2), :] for j in range(4)]
    rows = jnp.concatenate(
        [jnp.concatenate(mine[:2], axis=1), jnp.concatenate(mine[2:], axis=1)], axis=0
    )
    msa = (rows + res_ref[0].astype(F32)).astype(BF16).astype(F32)
    msa_s[...] = msa
    n_s[...] = normalize(msa).astype(BF16)
    for group in range(2):
        lanes = slice(group * 128, group * 128 + 128)

        def project(part):
            at = part * 256 + group * 128
            return dot(n_s[...], wcol_ref[:, at : at + 128])

        q_s[...] = project(0).astype(BF16)
        k_s[...] = project(1).astype(BF16)
        values = project(2).astype(BF16).astype(F32)
        fill_rhs(rhs_s, values, maskcol_ref[0].astype(F32))
        g_s[...] = jax.nn.sigmoid(project(3))
        attend(q_s, k_s, g_s, rhs_s, o_s, None, lambda n: maskrow_ref[0])
        heads_s[:, lanes] = o_s[...].astype(BF16)
    updated = (msa_s[...] + dot(heads_s[...], wout_ref[...])).astype(BF16)
    upd_ref[0] = updated
    outer = normalize(updated.astype(F32)).astype(BF16)
    factors = dot(wfac_ref[...], outer, TN) * maskrow_ref[0]
    left_ref[0] = factors[:FACTOR].astype(BF16)
    right_ref[0] = factors[FACTOR:].astype(BF16)


def place():
    branch = lax.axis_index("branch")
    dap = lax.axis_index("dap")
    return dict(
        branch=branch,
        dap=dap,
        y_hi=branch // 2,
        core=branch % 2,
        x=dap // 16,
        z=(dap // 2) % 8,
        y_lo=dap % 2,
    )


def outer_kernel(
    left_ref,
    right_ref,
    upd_ref,
    weight_ref,
    gather_ref,
    pair_ref,
    l_s,
    lp_s,
    r_s,
    perm_s,
    wide_s,
    lhs_s,
    send_s,
    l_send,
    l_recv,
    r_send,
    r_recv,
    f_send,
    f_recv,
    u_send,
    u_recv,
    p_send,
    p_recv,
):
    at = place()
    branch, dap, y_hi, core = at["branch"], at["dap"], at["y_hi"], at["core"]
    x, z, y_lo = at["x"], at["z"], at["y_lo"]
    barrier = pltpu.get_barrier_semaphore()

    def greet(index, _):
        other_b = index // 8
        other_d = (index // 2) % 4 * 16 + z * 2 + index % 2
        other = jnp.logical_or(other_b != branch, other_d != dap)

        @pl.when(other)
        def _():
            pl.semaphore_signal(barrier, 1, device_id=(other_b, other_d), device_id_type=MESH)

        return 0

    lax.fori_loop(0, 32, greet, 0)

    def greet_line(index, _):
        other_z = index // 2

        @pl.when(other_z != z)
        def _():
            pl.semaphore_signal(
                barrier,
                1,
                device_id=(y_hi * 2 + index % 2, x * 16 + other_z * 2 + y_lo),
                device_id_type=MESH,
            )

        return 0

    lax.fori_loop(0, 16, greet_line, 0)
    pl.semaphore_wait(barrier, 31 + 14)

    def send(src, dst, send_sem, recv_sem, to):
        other = jnp.logical_or(to[0] != branch, to[1] != dap)

        @pl.when(other)
        def _():
            pltpu.make_async_remote_copy(
                src, dst, send_sem, recv_sem, device_id=to, device_id_type=MESH
            ).start()

        @pl.when(jnp.logical_not(other))
        def _():
            pltpu.make_async_copy(src, dst, recv_sem).start()

    def sent(src, send_sem, to):
        other = jnp.logical_or(to[0] != branch, to[1] != dap)

        @pl.when(other)
        def _():
            pltpu.make_async_copy(src, src, send_sem).wait()

    def arrived(dst, recv_sem):
        pltpu.make_async_copy(dst, dst, recv_sem).wait()

    def to_left(slot):
        return ((slot % 4) // 2 * 2 + y_lo, slot // 4 * 16 + z * 2 + slot % 2)

    def to_right(slot):
        return (branch, x * 16 + slot * 2 + y_lo)

    def to_branch(slot):
        return (slot, dap)

    def to_pair(slot):
        return (x, slot * 16 + z * 2 + core)

    partner = (y_hi * 2 + 1 - core, dap)
    my_left = x * 4 + branch
    for slot in range(8):
        send(right_ref, r_s.at[z, core], r_send.at[slot], r_recv.at[z, core], to_right(slot))
    for slot in range(16):
        send(left_ref, l_s.at[my_left], l_send.at[slot], l_recv.at[my_left], to_left(slot))
    for slot in range(4):
        send(upd_ref, gather_ref.at[branch], u_send.at[slot], u_recv.at[branch], to_branch(slot))

    wide_s[...] = jnp.zeros_like(wide_s)

    def widen(c, _):
        block = weight_ref[pl.ds(pl.multiple_of(c * 32, 32), 32), :]
        for j in range(4):
            rows = pl.ds(pl.multiple_of(c * 128 + j * 32, 32), 32)
            wide_s[rows, j * 128 : (j + 1) * 128] = block
        return 0

    lax.fori_loop(0, 32, widen, 0)

    def permute(c, _):
        source = lax.broadcasted_iota(jnp.int32, (32, 1024), 1)
        wanted = lax.broadcasted_iota(jnp.int32, (32, 1024), 0) * 32 + c
        rows = pl.ds(pl.multiple_of(c * 32, 32), 32)
        perm_s[rows, :] = (source == wanted).astype(F32).astype(BF16)
        return 0

    lax.fori_loop(0, 32, permute, 0)

    for slot in range(8):
        arrived(r_s.at[slot, core], r_recv.at[slot, core])
        pltpu.make_async_remote_copy(
            r_s.at[slot, core],
            r_s.at[slot, core],
            f_send.at[slot],
            f_recv.at[slot],
            device_id=partner,
            device_id_type=MESH,
        ).start()
    for slot in range(16):
        arrived(l_s.at[slot], l_recv.at[slot])
    lefts = l_s[...].reshape(1024, SEQS)

    def reorder(c, _):
        rows = pl.ds(pl.multiple_of(c * 128, 128), 128)
        lp_s[rows, :] = dot(perm_s[rows, :], lefts).astype(BF16)
        return 0

    lax.fori_loop(0, 8, reorder, 0)
    for slot in range(8):
        arrived(r_s.at[slot, 1 - core], f_recv.at[slot])
    rights = r_s[...].reshape(1024, SEQS)

    for cp in range(16):
        block = dot(lp_s[cp * 64 : (cp + 1) * 64, :], rights, NT)
        for c2 in range(2):
            tiles = [
                block[c2 * 32 + xi * 8 : c2 * 32 + xi * 8 + 8, jg * 128 : jg * 128 + 128]
                for xi in range(4)
                for jg in range(8)
            ]
            lanes = (cp * 2 + c2) * 128
            lhs_s[:, lanes : lanes + 128] = jnp.concatenate(tiles, axis=0).astype(BF16)
    for xi in range(4):
        update = dot(lhs_s[xi * 64 : (xi + 1) * 64, :], wide_s[...])
        send_s[xi] = update.reshape(8, 8, 512).astype(BF16)
    for slot in range(4):
        send(
            send_s.at[slot],
            pair_ref.at[y_hi * 2 + y_lo],
            p_send.at[slot],
            p_recv.at[y_hi * 2 + y_lo],
            to_pair(slot),
        )
    for slot in range(8):
        sent(right_ref, r_send.at[slot], to_right(slot))
        pltpu.make_async_copy(r_s.at[slot, core], r_s.at[slot, core], f_send.at[slot]).wait()
    for slot in range(16):
        sent(left_ref, l_send.at[slot], to_left(slot))
    for slot in range(4):
        sent(upd_ref, u_send.at[slot], to_branch(slot))
        sent(send_s.at[slot], p_send.at[slot], to_pair(slot))
        arrived(gather_ref.at[slot], u_recv.at[slot])
        arrived(pair_ref.at[slot], p_recv.at[slot])


def whole(shape):
    return pl.BlockSpec(shape, lambda *_: (0,) * len(shape))


def per_device(
    alignment,
    pair_rep,
    align_mask,
    residue_mask,
    bias_weight,
    row_proj_weight,
    row_out_weight,
    column_proj_weight,
    column_out_weight,
    outer_factor_weight,
    outer_out,
):
    branch = lax.axis_index("branch")
    dap = lax.axis_index("dap")
    vmem = pltpu.VMEM
    params = pltpu.CompilerParams(vmem_limit_bytes=VMEM_LIMIT)

    bias_block = pl.pallas_call(
        bias_kernel,
        out_shape=jax.ShapeDtypeStruct((HEADS, 8, 128), BF16),
        compiler_params=params,
        name="pair_bias",
    )(pair_rep, bias_weight)
    spread = jnp.broadcast_to(bias_block.reshape(1, 4, 2, 8, 128), (64, 4, 2, 8, 128))
    bias = lax.all_to_all(
        spread.reshape(256, 2, 8, 128), ("dap", "branch"), split_axis=0, concat_axis=0, tiled=True
    ).reshape(64, 4, 2, 8, 128)

    by_owner = alignment.reshape(8, 64, 4, 2, 256)
    mine = lax.dynamic_slice_in_dim(by_owner, branch, 1, 2)[:, :, 0]
    mine = jnp.transpose(mine.reshape(4, 2, 64, 2, 256), (2, 3, 1, 0, 4))
    moved = lax.all_to_all(mine, "dap", split_axis=0, concat_axis=0, tiled=True)
    residual = jnp.transpose(moved, (1, 2, 0, 3, 4)).reshape(2, SEQS, 256)

    wcol = jnp.broadcast_to(column_proj_weight[None], (4, 4, 256, 64))
    wcol = lax.all_to_all(wcol, "branch", split_axis=0, concat_axis=0, tiled=True)
    wcol = jnp.transpose(wcol, (2, 1, 0, 3)).reshape(256, 1024)

    half = jnp.transpose(row_proj_weight, (1, 0, 2))
    none = jnp.zeros_like(half)
    wrow = jnp.concatenate(
        [jnp.concatenate([half, none], axis=2), jnp.concatenate([none, half], axis=2)], axis=0
    ).reshape(512, 512)
    out_half = row_out_weight.reshape(4, 64, 256)
    out_none = jnp.zeros_like(out_half)
    wrow_out = jnp.concatenate(
        [
            jnp.concatenate([out_half, out_none], axis=2),
            jnp.concatenate([out_none, out_half], axis=2),
        ],
        axis=1,
    ).reshape(512, 512)

    seq_mask = lax.dynamic_slice_in_dim(align_mask, dap * 8, 8, 0).astype(F32)
    row_mask = seq_mask.reshape(4, 2, SEQS)
    row_maskcol = jnp.repeat(jnp.transpose(row_mask, (0, 2, 1)), 64, axis=2).astype(BF16)
    res_mask = lax.dynamic_slice_in_dim(align_mask, dap * 8 + branch * 2, 2, 1).astype(F32)
    res_mask = jnp.transpose(res_mask.reshape(256, 2, 2), (2, 1, 0)).reshape(2, 1, SEQS)
    col_maskcol = jnp.broadcast_to(res_mask.reshape(2, SEQS, 1), (2, SEQS, 128)).astype(BF16)

    attend_scratch = [
        vmem((SEQS, 128), BF16),
        vmem((SEQS, 128), BF16),
        vmem((SEQS, 128), F32),
        vmem((4 * SEQS, 256), BF16),
        vmem((SEQS, 128), F32),
    ]
    heads = pl.pallas_call(
        row_kernel,
        grid=(4,),
        in_specs=[
            pl.BlockSpec((2, SEQS, 256), lambda i: (i, 0, 0)),
            whole((512, 512)),
            whole((64, 4, 2, 8, 128)),
            pl.BlockSpec((1, SEQS, 128), lambda i: (i, 0, 0)),
            pl.BlockSpec((1, 2, SEQS), lambda i: (i, 0, 0)),
        ],
        out_specs=whole((256, 8, 128)),
        out_shape=jax.ShapeDtypeStruct((256, 8, 128), BF16),
        scratch_shapes=attend_scratch + [vmem((2048, 128), F32)],
        compiler_params=params,
        name="row_attention",
    )(alignment, wrow, bias, row_maskcol, row_mask)
    got = lax.all_to_all(heads, ("dap", "branch"), split_axis=0, concat_axis=0, tiled=True)

    updated, left, right = pl.pallas_call(
        column_kernel,
        grid=(2,),
        in_specs=[
            whole((64, 4, 8, 128)),
            pl.BlockSpec((1, SEQS, 256), lambda i: (i, 0, 0)),
            whole((512, 512)),
            whole((256, 1024)),
            whole((256, 256)),
            whole((256, 64)),
            pl.BlockSpec((1, SEQS, 128), lambda i: (i, 0, 0)),
            pl.BlockSpec((1, 1, SEQS), lambda i: (i, 0, 0)),
        ],
        out_specs=(
            pl.BlockSpec((1, SEQS, 256), lambda i: (i, 0, 0)),
            pl.BlockSpec((1, FACTOR, SEQS), lambda i: (i, 0, 0)),
            pl.BlockSpec((1, FACTOR, SEQS), lambda i: (i, 0, 0)),
        ),
        out_shape=(
            jax.ShapeDtypeStruct((2, SEQS, 256), BF16),
            jax.ShapeDtypeStruct((2, FACTOR, SEQS), BF16),
            jax.ShapeDtypeStruct((2, FACTOR, SEQS), BF16),
        ),
        scratch_shapes=[
            vmem((4, SEQS, 128), F32),
            vmem((SEQS, 256), F32),
            vmem((SEQS, 256), BF16),
        ]
        + attend_scratch
        + [vmem((SEQS, 256), BF16)],
        compiler_params=params,
        name="column_attention",
    )(
        got.reshape(64, 4, 8, 128),
        residual,
        wrow_out,
        wcol,
        column_out_weight,
        outer_factor_weight,
        col_maskcol,
        res_mask,
    )

    dma = pltpu.SemaphoreType.DMA
    gathered, pairs = pl.pallas_call(
        outer_kernel,
        in_specs=[pl.BlockSpec(memory_space=vmem)] * 4,
        out_specs=(pl.BlockSpec(memory_space=vmem),) * 2,
        out_shape=(
            jax.ShapeDtypeStruct((4, 2 * SEQS, 256), BF16),
            jax.ShapeDtypeStruct((4, 8, 8, 512), BF16),
        ),
        scratch_shapes=[
            vmem((16, 64, SEQS), BF16),
            vmem((1024, SEQS), BF16),
            vmem((8, 2, 64, SEQS), BF16),
            vmem((1024, 1024), BF16),
            vmem((4096, 512), BF16),
            vmem((256, 4096), BF16),
            vmem((4, 8, 8, 512), BF16),
            dma((16,)),
            dma((16,)),
            dma((8,)),
            dma((8, 2)),
            dma((8,)),
            dma((8,)),
            dma((4,)),
            dma((4,)),
            dma((4,)),
            dma((4,)),
        ],
        compiler_params=pltpu.CompilerParams(
            vmem_limit_bytes=VMEM_LIMIT, collective_id=0, has_side_effects=True
        ),
        name="outer_product",
    )(
        left.reshape(2 * FACTOR, SEQS),
        right.reshape(2 * FACTOR, SEQS),
        updated.reshape(2 * SEQS, 256),
        outer_out,
    )

    rows = jnp.transpose(gathered.reshape(4, 2, 2, 256, 256), (3, 2, 0, 1, 4))
    updated_alignment = rows.reshape(SEQS, 8, 256)

    mask_rows = lax.dynamic_slice_in_dim(align_mask, dap * 8, 8, 1).astype(BF16)
    mask_cols = lax.dynamic_slice_in_dim(align_mask, branch * 128, 128, 1).astype(BF16)
    counts = jnp.einsum("si,sj->ij", mask_rows, mask_cols, preferred_element_type=F32)
    res_float = residue_mask.astype(F32)
    live_rows = lax.dynamic_slice_in_dim(res_float, dap * 8, 8, 0)
    live_cols = lax.dynamic_slice_in_dim(res_float, branch * 128, 128, 0)
    factor = live_rows[:, None] * live_cols[None, :] / (counts + count_eps)
    update = jnp.transpose(pairs.reshape(2, 2, 8, 8, 4, 128), (3, 2, 1, 0, 4, 5))
    update = update.reshape(8, 128, 128).astype(F32)
    pair_out = (pair_rep.astype(F32) + update * factor[:, :, None]).astype(BF16)
    return (updated_alignment, pair_out)


def solution(mesh):
    placed = (
        P("dap", None, None),
        P("dap", "branch", None),
        P(),
        P(),
        P(),
        P(None, None, "branch"),
        P(),
        P(None, None, "branch"),
        P(),
        P(),
        P(),
    )
    return jax.shard_map(
        per_device,
        mesh=mesh,
        in_specs=placed,
        out_specs=(P(None, "dap", None), P("dap", "branch", None)),
        check_vma=False,
    )
```

time: 914 us -> 195 us (0.21)
  waiting for transfers between devices: 753 us -> 49.2 us
  Pallas kernels: 0 us -> 84.3 us
  matrix products: 59.9 us -> 0.28 us
  other arithmetic: 24 us -> 2 us
  starting transfers between devices: 18.1 us -> 33.2 us
  between operations: 14.1 us -> 0.86 us
  local copies, waits for them, and re-layouts: 35 us -> 23.3 us
    all_gather x4 -> x0, waiting for transfers between devices: 703 us -> none  [the longest x1 367 us: per_device(): right_all = lax.all_gather(right_local, 'dap', axis=1, tiled=True)]
    pallas_call x0 -> x4, Pallas kernels: none -> 84.3 us  [the longest x1 47.7 us: per_device(): pl.pallas_call(outer_kernel, in_specs=[pl.BlockSpec(memory_space=vmem)] *...]
    dot_general x41 -> x1, matrix products: 59.9 us -> 0.28 us  [per_device(): jnp.einsum('si,sj->ij', mask_rows, mask_cols, preferred_element_type=F32)]
    all_to_all x2 -> x4, starting transfers between devices: 17.7 us -> 33.2 us  [the longest x1 11.9 us: per_device(): lax.all_to_all(spread.reshape(256, 2, 8, 128), ('dap', 'branch'), split_a...]
    reduce_sum x7 -> x0, other arithmetic: 12.7 us -> none  [the longest x4 6.38 us: layer_normalize(): spread = jnp.mean(centred * centred, axis=-1, keepdims=True)]
    convert_element_type x7 -> x6, other arithmetic: 11.2 us -> 1.12 us  [the longest x1 0.91 us: per_device(): pair_out = (pair_rep.astype(F32) + update * factor[:, :, None]).astype(BF16)]
    all_to_all x2 -> x4, waiting for transfers between devices: 50.2 us -> 49.2 us  [the longest x1 26.8 us: per_device(): lax.all_to_all(spread.reshape(256, 2, 8, 128), ('dap', 'branch'), split_a...]
  transfers between devices with their start and end apart: 6 -> 4, of which waited for: 5 -> 3; matrix products, arithmetic and copies ran while one was open for 3% -> 7% of each run, Pallas kernels for 0% -> 10%
where the time goes in v1:
time: 195 us; the launch traced here: 193 us
  Pallas kernels  84.3 us (43%)
  waiting for transfers between devices  49.2 us (25%)
  starting transfers between devices  33.2 us (17%)
  local copies, waits for them, and re-layouts  23.3 us (12%)
  other arithmetic  2 us (1%)
    pallas_call x1, Pallas kernels, per_device(): pl.pallas_call(outer_kernel, in_specs=[pl.BlockSpec(memory_space=vmem)] *...  47.7 us
    all_to_all x1, waiting for transfers between devices, per_device(): lax.all_to_all(spread.reshape(256, 2, 8, 128), ('dap', 'branch'), split_a...  26.8 us
    pallas_call x1, Pallas kernels, per_device(): pl.pallas_call(row_kernel, grid=(4,), in_specs=[pl.BlockSpec((2, SEQS, 25...  17.8 us
    pallas_call x1, Pallas kernels, per_device(): pl.pallas_call(column_kernel, grid=(2,), in_specs=[whole((64, 4, 8, 128))...  16.8 us
    all_to_all x1, waiting for transfers between devices, per_device(): lax.all_to_all(heads, ('dap', 'branch'), split_axis=0, concat_axis=0, til...  15.6 us
    all_to_all x1, starting transfers between devices, per_device(): lax.all_to_all(spread.reshape(256, 2, 8, 128), ('dap', 'branch'), split_a...  11.9 us
    all_to_all x1, starting transfers between devices, per_device(): lax.all_to_all(heads, ('dap', 'branch'), split_axis=0, concat_axis=0, til...  11.5 us
    all_to_all x1, waiting for transfers between devices, per_device(): lax.all_to_all(wcol, 'branch', split_axis=0, concat_axis=0, tiled=True)  6.85 us
  transfers between devices with their start and end apart: 4, of which 3 were waited for; matrix products, arithmetic and copies ran while one was open for 7% of the time, Pallas kernels for 10%

profile of v1, /device:TPU:32, one launch (start us, length us, event | category | flops | bytes accessed | tf_op | source)
XLA Modules:
  0.0 193.1 jit_solution(11549818091174833137)
XLA Ops:
  0.6 1.7 broadcast_in_dim.13
  2.4 4.6 %all-to-all-start.3 = ((bf16[4,4,256,64]{2,3,1,0:T(8,128)(2,1)}), bf16[4,4,256,64]{2,3,1,0:T(8,128)(2,1)S(1)}, u32[]{:S(2)}, u32[]{:S(2)}) async-start(bf16[4,4,256,64]{2,3,1,0:T(8,128)(2,1)} %broadcast_in_dim.13), calls=%async_computation.3 | async-start | bytes 1048576 | tf_op jit(solution)/shard_map/all_to_all | solution.py:418
  7.0 1.4 copy.42.weight_ref
  8.4 2.1 %pair_bias.1 = bf16[8,8,128]{2,1,0:T(8,128)(2,1)} custom-call(bf16[8,128,128]{2,1,0:T(8,128)(2,1)} %pair_ref.1, bf16[128,8]{1,0:T(8,128)(2,1)} %copy.42.weight_ref), custom_call_target="tpu_custom_call" | custom-call | tf_op jit(solution)/shard_map/pair_bias/pallas_call | solution.py:400
  10.4 6.9 %all-to-all-done.3 = bf16[4,4,256,64]{2,3,1,0:T(8,128)(2,1)S(1)} async-done(((bf16[4,4,256,64]{2,3,1,0:T(8,128)(2,1)}), bf16[4,4,256,64]{2,3,1,0:T(8,128)(2,1)S(1)}, u32[]{:S(2)}, u32[]{:S(2)}) %all-to-all-start.3) | async-done | bytes 524320 | tf_op jit(solution)/shard_map/all_to_all | solution.py:418
  17.3 2.0 %broadcast_in_dim.11 = bf16[64,4,2,8,128]{4,3,2,1,0:T(8,128)(2,1)} broadcast(bf16[4,2,8,128]{3,2,1,0:T(8,128)(2,1)} %bitcast.52), dimensions={1,2,3,4} | broadcast | bytes 1064960 | tf_op jit(solution)/shard_map/broadcast_in_dim | solution.py:406
  19.3 11.9 %all-to-all-start = ((bf16[256,2,8,128]{3,2,1,0:T(8,128)(2,1)}), bf16[256,2,8,128]{3,2,1,0:T(8,128)(2,1)S(1)}, u32[]{:S(2)}, u32[]{:S(2)}) async-start(bf16[256,2,8,128]{3,2,1,0:T(8,128)(2,1)} %bitcast.3), calls=%async_computation | async-start | bytes 2097152 | tf_op jit(solution)/shard_map/all_to_all | solution.py:407
  31.2 2.5 %copy.44 = bf16[8,512,256]{2,0,1:T(8,128)(2,1)} copy(bf16[8,512,256]{2,1,0:T(8,128)(2,1)S(1)} %copy-done) | data formatting | bytes 4194304 | tf_op args[0]
  33.7 1.2 constant_dynamic-slice_fusion
  35.0 1.4 copy.46
  36.4 26.8 %all-to-all-done = bf16[256,2,8,128]{3,2,1,0:T(8,128)(2,1)S(1)} async-done(((bf16[256,2,8,128]{3,2,1,0:T(8,128)(2,1)}), bf16[256,2,8,128]{3,2,1,0:T(8,128)(2,1)S(1)}, u32[]{:S(2)}, u32[]{:S(2)}) %all-to-all-start) | async-done | bytes 1048608 | tf_op jit(solution)/shard_map/all_to_all | solution.py:407
  63.1 5.2 %all-to-all-start.2 = ((bf16[64,2,2,4,256]{4,1,2,3,0:T(2,128)(2,1)}), bf16[64,2,2,4,256]{4,1,2,3,0:T(2,128)(2,1)S(1)}, u32[]{:S(2)}, u32[]{:S(2)}) async-start(bf16[64,2,2,4,256]{4,1,2,3,0:T(2,128)(2,1)} %copy.46), calls=%async_computation.2 | async-start | bytes 1048576 | tf_op jit(solution)/shard_map/all_to_all | solution.py:414
  68.5 1.0 copy.43.maskcol_ref
  69.5 1.0 copy.54.w_ref
  70.5 17.8 %row_attention.1 = bf16[256,8,128]{2,1,0:T(8,128)(2,1)} custom-call(bf16[8,512,256]{2,1,0:T(8,128)(2,1)} %x_ref.1, bf16[512,512]{1,0:T(8,128)(2,1)} %copy.54.w_ref, bf16[64,4,2,8,128]{4,3,2,1,0:T(8,128)(2,1)} %bitcast.36, bf16[4,512,128]{2,1,0:T(8,128)(2,1)} %copy.43.maskcol_ref, f32[4,2,512]{2,1,0:T(2,128)} %copy-done.8), custom_call_target="tpu_custom_call" | custom-call | tf_op jit(solution)/shard_map/row_attention/pallas_call | solution.py:450
  88.3 11.5 %all-to-all-start.1 = ((bf16[256,8,128]{2,1,0:T(8,128)(2,1)}), bf16[256,8,128]{2,1,0:T(8,128)(2,1)S(1)}, u32[]{:S(2)}, u32[]{:S(2)}) async-start(bf16[256,8,128]{2,1,0:T(8,128)(2,1)} %row_attention.1), calls=%async_computation.1 | async-start | bytes 1048576 | tf_op jit(solution)/shard_map/all_to_all | solution.py:466
  102.9 1.0 copy.50.wcol_ref
  104.1 0.9 reshape.77.res_ref
  105.0 15.6 %all-to-all-done.1 = bf16[256,8,128]{2,1,0:T(8,128)(2,1)S(1)} async-done(((bf16[256,8,128]{2,1,0:T(8,128)(2,1)}), bf16[256,8,128]{2,1,0:T(8,128)(2,1)S(1)}, u32[]{:S(2)}, u32[]{:S(2)}) %all-to-all-start.1) | async-done | bytes 524320 | tf_op jit(solution)/shard_map/all_to_all | solution.py:466
  120.6 0.9 broadcast_in_dim.14.maskcol_ref
  121.5 16.8 %column_attention.1 = (bf16[2,512,256]{2,1,0:T(8,128)(2,1)}, bf16[2,32,512]{2,1,0:T(8,128)(2,1)}, bf16[2,32,512]{2,1,0:T(8,128)(2,1)}) custom-call(bf16[64,4,8,128]{3,2,1,0:T(8,128)(2,1)} %bitcast.39, bf16[2,512,256]{2,1,0:T(8,128)(2,1)} %reshape.77.res_ref, bf16[512,512]{1,0:T(8,128)(2,1)} %bitcast.38, bf16[256,1024]{1,0:T(8,128)(2,1)} %copy.50.wcol_ref, ...), custom_call_target="tpu_custom_call" | custom-call | tf_op jit(solution)/shard_map/column_attention/pallas_call | solution.py:468
  138.3 47.7 %outer_product.1 = (bf16[4,1024,256]{2,1,0:T(8,128)(2,1)}, bf16[4,8,8,512]{3,2,1,0:T(8,128)(2,1)}) custom-call(bf16[64,512]{1,0:T(8,128)(2,1)} %bitcast.53, bf16[64,512]{1,0:T(8,128)(2,1)} %bitcast.54, bf16[1024,256]{1,0:T(8,128)(2,1)} %bitcast.48, bf16[1024,128]{1,0:T(8,128)(2,1)} %weight_ref.2), custom_call_target="tpu_custom_call" | custom-call | tf_op jit(solution)/shard_map/outer_product/pallas_call | solution.py:512
  186.0 3.7 %copy.52 = bf16[256,2,4,2,256]{4,3,2,1,0:T(2,128)(2,1)S(1)} copy(bf16[256,2,4,2,256]{4,0,1,3,2:T(8,128)(2,1)} %bitcast.41) | data formatting | bytes 4194304 | tf_op jit(solution)/shard_map/transpose | solution.py:550
  189.8 2.2 %reshape.87 = bf16[512,8,256]{2,1,0:T(8,128)(2,1)} reshape(bf16[256,2,4,2,256]{4,3,2,1,0:T(2,128)(2,1)S(1)} %copy.52) | data formatting | bytes 4194304 | tf_op jit(solution)/shard_map/reshape | solution.py:551
  (49 shorter events, 4.6 us)
Async XLA Ops:
  2.4 28.8 %copy-start = (bf16[8,512,256]{2,1,0:T(8,128)(2,1)S(1)}, bf16[8,512,256]{2,1,0:T(8,128)(2,1)}, u32[]{:S(2)}) copy-start(bf16[8,512,256]{2,1,0:T(8,128)(2,1)} %x_ref.1) | copy-start | bytes 6291460
  2.4 14.9 %all-to-all-start.3 = ((bf16[4,4,256,64]{2,3,1,0:T(8,128)(2,1)}), bf16[4,4,256,64]{2,3,1,0:T(8,128)(2,1)S(1)}, u32[]{:S(2)}, u32[]{:S(2)}) async-start(bf16[4,4,256,64]{2,3,1,0:T(8,128)(2,1)} %broadcast_in_dim.13), calls=%async_computation.3 | async-start | bytes 1048576 | tf_op jit(solution)/shard_map/all_to_all | solution.py:418
  17.3 2.0 %copy-start.3 = (bf16[4,4,256,64]{2,3,1,0:T(8,128)(2,1)}, bf16[4,4,256,64]{2,3,1,0:T(8,128)(2,1)S(1)}, u32[]{:S(2)}) copy-start(bf16[4,4,256,64]{2,3,1,0:T(8,128)(2,1)S(1)} %all-to-all-done.3) | copy-start | bytes 1572868
  19.3 43.8 %all-to-all-start = ((bf16[256,2,8,128]{3,2,1,0:T(8,128)(2,1)}), bf16[256,2,8,128]{3,2,1,0:T(8,128)(2,1)S(1)}, u32[]{:S(2)}, u32[]{:S(2)}) async-start(bf16[256,2,8,128]{3,2,1,0:T(8,128)(2,1)} %bitcast.3), calls=%async_computation | async-start | bytes 2097152 | tf_op jit(solution)/shard_map/all_to_all | solution.py:407
  33.7 34.7 %copy-start.6 = (s32[512,512]{1,0:T(8,128)S(1)}, s32[512,512]{1,0:T(8,128)}, u32[]{:S(2)}) copy-start(s32[512,512]{1,0:T(8,128)} %param.13) | copy-start | bytes 3145732
  35.0 34.5 %copy-start.9 = (bf16[4,256,64]{1,2,0:T(8,128)(2,1)S(1)}, bf16[4,256,64]{1,2,0:T(8,128)(2,1)}, u32[]{:S(2)}) copy-start(bf16[4,256,64]{1,2,0:T(8,128)(2,1)} %param.16) | copy-start | bytes 393220
  63.1 7.4 %copy-start.1 = (bf16[256,2,8,128]{3,2,1,0:T(8,128)(2,1)}, bf16[256,2,8,128]{3,2,1,0:T(8,128)(2,1)S(1)}, u32[]{:S(2)}) copy-start(bf16[256,2,8,128]{3,2,1,0:T(8,128)(2,1)S(1)} %all-to-all-done) | copy-start | bytes 3145732
  63.1 25.2 %all-to-all-start.2 = ((bf16[64,2,2,4,256]{4,1,2,3,0:T(2,128)(2,1)}), bf16[64,2,2,4,256]{4,1,2,3,0:T(2,128)(2,1)S(1)}, u32[]{:S(2)}, u32[]{:S(2)}) async-start(bf16[64,2,2,4,256]{4,1,2,3,0:T(2,128)(2,1)} %copy.46), calls=%async_computation.2 | async-start | bytes 1048576 | tf_op jit(solution)/shard_map/all_to_all | solution.py:414
  68.4 2.1 %copy-start.8 = (f32[4,2,512]{2,1,0:T(2,128)}, f32[4,2,512]{2,1,0:T(2,128)S(1)}, u32[]{:S(2)}) copy-start(f32[4,2,512]{2,1,0:T(2,128)S(1)} %reshape.74.maskrow_ref) | copy-start | bytes 49156
  70.5 30.3 %copy-start.11 = (bf16[256,64]{0,1:T(8,128)(2,1)S(1)}, bf16[256,64]{0,1:T(8,128)(2,1)}, u32[]{:S(2)}) copy-start(bf16[256,64]{0,1:T(8,128)(2,1)} %param.20) | copy-start | bytes 98308
  70.5 31.0 %copy-start.12 = (s32[512]{0:T(512)S(1)}, s32[512]{0:T(512)}, u32[]{:S(2)}) copy-start(s32[512]{0:T(512)} %param.14) | copy-start | bytes 6148
  70.5 31.1 %copy-start.10 = (bf16[256,256]{1,0:T(8,128)(2,1)S(1)}, bf16[256,256]{1,0:T(8,128)(2,1)}, u32[]{:S(2)}) copy-start(bf16[256,256]{1,0:T(8,128)(2,1)} %param.17) | copy-start | bytes 393220
  88.3 14.5 %copy-start.4 = (bf16[4,4,256,64]{2,3,1,0:T(8,128)(2,1)S(1)}, bf16[4,4,256,64]{2,3,1,0:T(8,128)(2,1)}, u32[]{:S(2)}) copy-start(bf16[4,4,256,64]{2,3,1,0:T(8,128)(2,1)} %copy-done.3) | copy-start | bytes 1572868
  88.3 32.3 %all-to-all-start.1 = ((bf16[256,8,128]{2,1,0:T(8,128)(2,1)}), bf16[256,8,128]{2,1,0:T(8,128)(2,1)S(1)}, u32[]{:S(2)}, u32[]{:S(2)}) async-start(bf16[256,8,128]{2,1,0:T(8,128)(2,1)} %row_attention.1), calls=%async_computation.1 | async-start | bytes 1048576 | tf_op jit(solution)/shard_map/all_to_all | solution.py:466
  120.6 0.9 copy-start.2
  189.7 2.2 %copy-start.7 = (bf16[4,8,8,512]{3,2,1,0:T(8,128)(2,1)S(1)}, bf16[4,8,8,512]{3,2,1,0:T(8,128)(2,1)}, u32[]{:S(2)}) copy-start(bf16[4,8,8,512]{3,2,1,0:T(8,128)(2,1)} %get-tuple-element.11) | copy-start | bytes 786436
  189.8 2.4 %copy-start.5 = (bf16[8,128,128]{2,1,0:T(8,128)(2,1)S(1)}, bf16[8,128,128]{2,1,0:T(8,128)(2,1)}, u32[]{:S(2)}) copy-start(bf16[8,128,128]{2,1,0:T(8,128)(2,1)} %pair_ref.1) | copy-start | bytes 786436

commit v2 on v1

--- a/solution.py
+++ b/solution.py
@@ -13,13 +13,14 @@
 FACTOR = 32
 norm_eps = 1e-05
 count_eps = 0.001
-SCALE = 1.0 / math.sqrt(HEAD)
+LOG2E = math.log2(math.e)
+QUERY_SCALE = LOG2E / math.sqrt(HEAD)
 F32 = jnp.float32
 BF16 = jnp.bfloat16
 MESH = pl.DeviceIdType.MESH
 VMEM_LIMIT = 60 * 1024 * 1024
 SEQS = 512
-TILE = 128
+TILE = 256
 NT = (((1,), (1,)), ((), ()))
 TN = (((0,), (1,)), ((), ()))
 
@@ -35,9 +36,9 @@
     return lax.dot_general(a, b, dims, preferred_element_type=F32)
 
 
-def lane_block(rows, index):
-    lanes = lax.broadcasted_iota(jnp.int32, (rows, 128), 1)
-    return (lanes // HEAD == index).astype(F32)
+def lane_block(index):
+    lanes = lax.broadcasted_iota(jnp.int32, (1, 128), 1)
+    return (lanes // HEAD == index).astype(F32).astype(BF16)
 
 
 def attend(q_s, k_s, g_s, rhs_s, o_s, bias_of, mask_of):
@@ -47,14 +48,13 @@
             q = q_s[rows, :]
             total = None
             for n in range(4):
-                qn = q * lane_block(TILE, n).astype(BF16)
-                scores = dot(qn, k_s[...], NT) * SCALE
+                scores = dot(q * lane_block(n), k_s[...], NT)
                 if bias_of is not None:
                     scores = scores + bias_of(step, n)
                 if stable:
                     scores = jnp.where(mask_of(n) > 0.0, scores, -1e30)
                     scores = scores - jnp.max(scores, axis=1, keepdims=True)
-                raised = jnp.exp(scores).astype(BF16)
+                raised = jnp.exp2(scores).astype(BF16)
                 part = dot(raised, rhs_s[n * SEQS : (n + 1) * SEQS, :])
                 total = part if total is None else total + part
             sums = total[:, 128:]
@@ -76,40 +76,204 @@
         run(True)
 
 
-def fill_rhs(rhs_s, values, mask):
+def fill_values(rhs_s, values, mask):
+    masked = values * mask
     for n in range(4):
-        block = mask * lane_block(SEQS, n)
-        rhs_s[n * SEQS : (n + 1) * SEQS, :128] = (values * block).astype(BF16)
-        rhs_s[n * SEQS : (n + 1) * SEQS, 128:] = block.astype(BF16)
-
-
-def bias_kernel(pair_ref, weight_ref, out_ref):
+        rhs_s[n * SEQS : (n + 1) * SEQS, :128] = masked * lane_block(n)
+
+
+def fill_ones(rhs_s, mask):
+    for n in range(4):
+        rhs_s[n * SEQS : (n + 1) * SEQS, 128:] = mask * lane_block(n)
+
+
+def place():
+    branch = lax.axis_index("branch")
+    dap = lax.axis_index("dap")
+    return dict(
+        branch=branch,
+        dap=dap,
+        y_hi=branch // 2,
+        core=branch % 2,
+        x=dap // 16,
+        z=(dap // 2) % 8,
+        y_lo=dap % 2,
+    )
+
+
+def signal(semaphore, to):
+    pl.semaphore_signal(semaphore, 1, device_id=to, device_id_type=MESH)
+
+
+def remote(src, dst, send_sem, recv_sem, to):
+    pltpu.make_async_remote_copy(
+        src, dst, send_sem, recv_sem, device_id=to, device_id_type=MESH
+    ).start()
+
+
+def arrived(dst, semaphore):
+    pltpu.make_async_copy(dst, dst, semaphore).wait()
+
+
+def bias_kernel(
+    pair_ref,
+    weight_ref,
+    wcol_ref,
+    bias_ref,
+    wall_ref,
+    block_s,
+    p_send,
+    p_recv,
+    up_send,
+    down_send,
+    z_recv,
+    w_send,
+    w_recv,
+):
+    at = place()
+    branch, dap, x, z, y_lo = at["branch"], at["dap"], at["x"], at["z"], at["y_lo"]
+    barrier = pltpu.get_barrier_semaphore()
+
+    def to_plane(slot):
+        return (slot % 4, slot // 8 * 16 + z * 2 + slot // 4 % 2)
+
+    def line(other_z):
+        return (branch, x * 16 + other_z * 2 + y_lo)
+
+    mine = x * 8 + y_lo * 4 + branch
+
+    def greet(slot, _):
+        @pl.when(slot != mine)
+        def _():
+            signal(barrier, to_plane(slot))
+
+        return 0
+
+    lax.fori_loop(0, 32, greet, 0)
+
+    def greet_line(other_z, _):
+        @pl.when(other_z != z)
+        def _():
+            signal(barrier, line(other_z))
+
+        return 0
+
+    lax.fori_loop(0, 8, greet_line, 0)
+
     rows, cols, width = pair_ref.shape
-    x = pair_ref[...].astype(F32).reshape(rows * cols, width)
-    normed = normalize(x).astype(BF16)
+    values = pair_ref[...].astype(F32).reshape(rows * cols, width)
+    normed = normalize(values).astype(BF16)
     res = dot(weight_ref[...], normed, TN)
     for i in range(rows):
-        out_ref[:, i, :] = res[:, i * cols : (i + 1) * cols].astype(BF16)
+        tile = res[:, i * cols : (i + 1) * cols].astype(BF16)
+        block_s[:, :, i, :] = tile.reshape(4, 2, cols)
+    pl.semaphore_wait(barrier, 31 + 7)
+
+    def post(slot, _):
+        target = bias_ref.at[z, :, x, y_lo, branch]
+
+        @pl.when(slot != mine)
+        def _():
+            remote(block_s.at[slot % 4], target, p_send.at[slot], p_recv.at[mine], to_plane(slot))
+
+        @pl.when(slot == mine)
+        def _():
+            pltpu.make_async_copy(block_s.at[branch], target, p_recv.at[mine]).start()
+
+        return 0
+
+    lax.fori_loop(0, 32, post, 0)
+    across = (lax.rem(branch + 2, 4), dap)
+    partner = (branch // 2 * 2 + 1 - branch % 2, dap)
+    far = lax.rem(branch + 2, 4)
+    remote(wcol_ref, wall_ref.at[branch], w_send.at[0], w_recv.at[0], partner)
+    remote(wcol_ref, wall_ref.at[branch], w_send.at[1], w_recv.at[1], across)
+    own = pltpu.make_async_copy(wcol_ref, wall_ref.at[branch], w_recv.at[3])
+    own.start()
+
+    def collect(slot, _):
+        arrived(bias_ref.at[z, :, slot // 8, slot // 4 % 2, slot % 4], p_recv.at[slot])
+        return 0
+
+    lax.fori_loop(0, 32, collect, 0)
+
+    def chunk(other_z, c):
+        return bias_ref.at[other_z, c // 2, pl.ds(c % 2 * 2, 2)]
+
+    up, down = lax.rem(z + 1, 8), lax.rem(z + 7, 8)
+
+    def pass_up(t, c):
+        source = lax.rem(z + 8 - t, 8)
+        region = chunk(source, c)
+        remote(region, region, up_send.at[t, c], z_recv.at[source, c], line(up))
+
+    def pass_down(t, c):
+        source = lax.rem(z + t, 8)
+        region = chunk(source, c)
+        remote(region, region, down_send.at[t, c], z_recv.at[source, c], line(down))
+
+    for c in range(4):
+        pass_up(0, c)
+        pass_down(0, c)
+    for t in range(1, 4):
+        for c in range(4):
+            below, above = lax.rem(z + 8 - t, 8), lax.rem(z + t, 8)
+            arrived(chunk(below, c), z_recv.at[below, c])
+            if t < 3 or c < 2:
+                pass_up(t, c)
+            arrived(chunk(above, c), z_recv.at[above, c])
+            if t < 3 or c >= 2:
+                pass_down(t, c)
+    arrived(wall_ref.at[far], w_recv.at[1])
+    remote(wall_ref.at[far], wall_ref.at[far], w_send.at[2], w_recv.at[2], partner)
+    opposite = lax.rem(z + 4, 8)
+    for c in range(4):
+        arrived(chunk(opposite, c), z_recv.at[opposite, c])
+    for t in range(4):
+        for c in range(4):
+            if t < 3 or c < 2:
+                arrived(chunk(z, c), up_send.at[t, c])
+            if t < 3 or c >= 2:
+                arrived(chunk(z, c), down_send.at[t, c])
+
+    def drain(slot, _):
+        @pl.when(slot != mine)
+        def _():
+            arrived(block_s.at[0], p_send.at[slot])
+
+        return 0
+
+    lax.fori_loop(0, 32, drain, 0)
+    own.wait()
+    for n in range(3):
+        arrived(wcol_ref, w_send.at[n])
+    arrived(wcol_ref, w_recv.at[0])
+    arrived(wcol_ref, w_recv.at[2])
 
 
 def row_kernel(
-    x_ref, w_ref, bias_ref, maskcol_ref, maskrow_ref, out_ref, q_s, k_s, g_s, rhs_s, o_s, buf
+    x_ref, w_ref, bias_ref, maskcol_ref, maskrow_ref, out_ref, q_s, k_s, g_s, rhs_s, o_s, buf, bias_s
 ):
     pair = pl.program_id(0)
     normed = [normalize(x_ref[p].astype(F32)).astype(BF16) for p in range(2)]
     both = jnp.concatenate(normed, axis=1)
-    q_s[...] = dot(both, w_ref[:, :128]).astype(BF16)
-    k_s[...] = dot(both, w_ref[:, 128:256]).astype(BF16)
-    values = dot(both, w_ref[:, 256:384]).astype(BF16).astype(F32)
-    fill_rhs(rhs_s, values, maskcol_ref[0].astype(F32))
-    g_s[...] = jax.nn.sigmoid(dot(both, w_ref[:, 384:]))
+    projected = dot(both, w_ref[...])
+    q_s[...] = (projected[:, :128] * QUERY_SCALE).astype(BF16)
+    k_s[...] = projected[:, 128:256].astype(BF16)
+    fill_values(rhs_s, projected[:, 256:384].astype(BF16), maskcol_ref[0])
+    fill_ones(rhs_s, maskcol_ref[0])
+    g_s[...] = jax.nn.sigmoid(projected[:, 384:])
+
+    @pl.when(pair == 0)
+    def _():
+        for x in range(4):
+            for h in range(2):
+                for b in range(4):
+                    piece = bias_ref[:, h, x, :, b].astype(F32).reshape(128, 128)
+                    bias_s[h, x * 128 : x * 128 + 128, b * 128 : b * 128 + 128] = piece * LOG2E
 
     def bias_of(step, n):
-        pieces = []
-        for b in range(4):
-            piece = bias_ref[pl.ds(step * (TILE // 8), TILE // 8), b, n % 2]
-            pieces.append(piece.astype(F32).reshape(TILE, 128))
-        return jnp.concatenate(pieces, axis=1)
+        return bias_s[n % 2, pl.ds(pl.multiple_of(step * TILE, TILE), TILE), :]
 
     attend(q_s, k_s, g_s, rhs_s, o_s, bias_of, lambda n: maskrow_ref[0, n // 2 : n // 2 + 1, :])
     for k in range(2):
@@ -158,6 +322,7 @@
     msa = (rows + res_ref[0].astype(F32)).astype(BF16).astype(F32)
     msa_s[...] = msa
     n_s[...] = normalize(msa).astype(BF16)
+    fill_ones(rhs_s, maskcol_ref[0])
     for group in range(2):
         lanes = slice(group * 128, group * 128 + 128)
 
@@ -165,10 +330,9 @@
             at = part * 256 + group * 128
             return dot(n_s[...], wcol_ref[:, at : at + 128])
 
-        q_s[...] = project(0).astype(BF16)
+        q_s[...] = (project(0) * QUERY_SCALE).astype(BF16)
         k_s[...] = project(1).astype(BF16)
-        values = project(2).astype(BF16).astype(F32)
-        fill_rhs(rhs_s, values, maskcol_ref[0].astype(F32))
+        fill_values(rhs_s, project(2).astype(BF16), maskcol_ref[0])
         g_s[...] = jax.nn.sigmoid(project(3))
         attend(q_s, k_s, g_s, rhs_s, o_s, None, lambda n: maskrow_ref[0])
         heads_s[:, lanes] = o_s[...].astype(BF16)
@@ -178,20 +342,6 @@
     factors = dot(wfac_ref[...], outer, TN) * maskrow_ref[0]
     left_ref[0] = factors[:FACTOR].astype(BF16)
     right_ref[0] = factors[FACTOR:].astype(BF16)
-
-
-def place():
-    branch = lax.axis_index("branch")
-    dap = lax.axis_index("dap")
-    return dict(
-        branch=branch,
-        dap=dap,
-        y_hi=branch // 2,
-        core=branch % 2,
-        x=dap // 16,
-        z=(dap // 2) % 8,
-        y_lo=dap % 2,
-    )
 
 
 def outer_kernel(
@@ -208,8 +358,12 @@
     wide_s,
     lhs_s,
     send_s,
+    relay_s,
     l_send,
     l_recv,
+    up_send,
+    down_send,
+    x_recv,
     r_send,
     r_recv,
     f_send,
@@ -225,13 +379,11 @@
     barrier = pltpu.get_barrier_semaphore()
 
     def greet(index, _):
-        other_b = index // 8
-        other_d = (index // 2) % 4 * 16 + z * 2 + index % 2
-        other = jnp.logical_or(other_b != branch, other_d != dap)
-
-        @pl.when(other)
-        def _():
-            pl.semaphore_signal(barrier, 1, device_id=(other_b, other_d), device_id_type=MESH)
+        to = (index // 8, (index // 2) % 4 * 16 + z * 2 + index % 2)
+
+        @pl.when(jnp.logical_or(to[0] != branch, to[1] != dap))
+        def _():
+            signal(barrier, to)
 
         return 0
 
@@ -242,61 +394,71 @@
 
         @pl.when(other_z != z)
         def _():
-            pl.semaphore_signal(
-                barrier,
-                1,
-                device_id=(y_hi * 2 + index % 2, x * 16 + other_z * 2 + y_lo),
-                device_id_type=MESH,
-            )
+            signal(barrier, (y_hi * 2 + index % 2, x * 16 + other_z * 2 + y_lo))
 
         return 0
 
     lax.fori_loop(0, 16, greet_line, 0)
     pl.semaphore_wait(barrier, 31 + 14)
 
+    def elsewhere(to):
+        return jnp.logical_or(to[0] != branch, to[1] != dap)
+
     def send(src, dst, send_sem, recv_sem, to):
-        other = jnp.logical_or(to[0] != branch, to[1] != dap)
+        other = elsewhere(to)
 
         @pl.when(other)
         def _():
-            pltpu.make_async_remote_copy(
-                src, dst, send_sem, recv_sem, device_id=to, device_id_type=MESH
-            ).start()
+            remote(src, dst, send_sem, recv_sem, to)
 
         @pl.when(jnp.logical_not(other))
         def _():
             pltpu.make_async_copy(src, dst, recv_sem).start()
 
     def sent(src, send_sem, to):
-        other = jnp.logical_or(to[0] != branch, to[1] != dap)
-
-        @pl.when(other)
-        def _():
-            pltpu.make_async_copy(src, src, send_sem).wait()
-
-    def arrived(dst, recv_sem):
-        pltpu.make_async_copy(dst, dst, recv_sem).wait()
+        @pl.when(elsewhere(to))
+        def _():
+            arrived(src, send_sem)
 
     def to_left(slot):
-        return ((slot % 4) // 2 * 2 + y_lo, slot // 4 * 16 + z * 2 + slot % 2)
+        return (slot // 2 * 2 + y_lo, x * 16 + z * 2 + slot % 2)
 
     def to_right(slot):
         return (branch, x * 16 + slot * 2 + y_lo)
 
-    def to_branch(slot):
-        return (slot, dap)
-
     def to_pair(slot):
         return (x, slot * 16 + z * 2 + core)
 
+    def x_line(other_x):
+        return (branch, other_x * 16 + z * 2 + y_lo)
+
+    def y_line(step):
+        other = lax.rem(y_hi * 2 + y_lo + step, 4)
+        return (other // 2 * 2 + core, x * 16 + z * 2 + other % 2)
+
     partner = (y_hi * 2 + 1 - core, dap)
-    my_left = x * 4 + branch
+    far = lax.rem(branch + 2, 4)
+    for slot in range(4):
+        send(left_ref, l_s.at[x, branch], l_send.at[slot], l_recv.at[branch], to_left(slot))
     for slot in range(8):
         send(right_ref, r_s.at[z, core], r_send.at[slot], r_recv.at[z, core], to_right(slot))
-    for slot in range(16):
-        send(left_ref, l_s.at[my_left], l_send.at[slot], l_recv.at[my_left], to_left(slot))
-    for slot in range(4):
-        send(upd_ref, gather_ref.at[branch], u_send.at[slot], u_recv.at[branch], to_branch(slot))
+
+    def rows_of(way, piece):
+        return pl.ds(way * 512 + piece * 256, 256)
+
+    steps = (1, 3)
+    for piece in range(2):
+        for way in range(2):
+            remote(
+                upd_ref.at[rows_of(way, piece)],
+                relay_s.at[way, piece],
+                u_send.at[0, way, piece],
+                u_recv.at[0, way, piece],
+                y_line(steps[way]),
+            )
+    remote(upd_ref, gather_ref.at[branch], u_send.at[3, 0, 0], u_recv.at[3, 0, 0], partner)
+    own = pltpu.make_async_copy(upd_ref, gather_ref.at[branch], u_recv.at[3, 0, 1])
+    own.start()
 
     wide_s[...] = jnp.zeros_like(wide_s)
 
@@ -318,43 +480,67 @@
 
     lax.fori_loop(0, 32, permute, 0)
 
+    above, below = lax.rem(x + 1, 4), lax.rem(x + 3, 4)
+
+    def half(other_x, h):
+        return l_s.at[other_x, pl.ds(h * 2, 2)]
+
+    def pass_x(origin, h, send_sem, to):
+        region = half(origin, h)
+        remote(region, region, send_sem, x_recv.at[origin, h], x_line(to))
+
+    for slot in range(4):
+        arrived(l_s.at[x, slot], l_recv.at[slot])
+    for h in range(2):
+        pass_x(x, h, up_send.at[h], above)
+        pass_x(x, 1 - h, down_send.at[1 - h], below)
+
+    def relay(way, piece):
+        region = relay_s.at[way, piece]
+        arrived(region, u_recv.at[0, way, piece])
+        to = y_line(steps[way])
+        remote(
+            region,
+            gather_ref.at[lax.rem(to[0] + 2, 4), rows_of(way, piece)],
+            u_send.at[1, way, piece],
+            u_recv.at[1, way, piece],
+            to,
+        )
+
+    for way in range(2):
+        relay(way, 0)
     for slot in range(8):
         arrived(r_s.at[slot, core], r_recv.at[slot, core])
-        pltpu.make_async_remote_copy(
-            r_s.at[slot, core],
-            r_s.at[slot, core],
-            f_send.at[slot],
-            f_recv.at[slot],
-            device_id=partner,
-            device_id_type=MESH,
-        ).start()
-    for slot in range(16):
-        arrived(l_s.at[slot], l_recv.at[slot])
+        remote(r_s.at[slot, core], r_s.at[slot, core], f_send.at[slot], f_recv.at[slot], partner)
+    arrived(half(below, 0), x_recv.at[below, 0])
+    pass_x(below, 0, up_send.at[2], above)
+    arrived(half(above, 1), x_recv.at[above, 1])
+    pass_x(above, 1, down_send.at[2], below)
+    for way in range(2):
+        relay(way, 1)
+    arrived(half(below, 1), x_recv.at[below, 1])
+    arrived(half(above, 0), x_recv.at[above, 0])
+    opposite = lax.rem(x + 2, 4)
+    for h in range(2):
+        arrived(half(opposite, h), x_recv.at[opposite, h])
     lefts = l_s[...].reshape(1024, SEQS)
-
-    def reorder(c, _):
-        rows = pl.ds(pl.multiple_of(c * 128, 128), 128)
-        lp_s[rows, :] = dot(perm_s[rows, :], lefts).astype(BF16)
-        return 0
-
-    lax.fori_loop(0, 8, reorder, 0)
+    lp_s[...] = dot(perm_s[...], lefts).astype(BF16)
     for slot in range(8):
         arrived(r_s.at[slot, 1 - core], f_recv.at[slot])
-    rights = r_s[...].reshape(1024, SEQS)
-
-    for cp in range(16):
-        block = dot(lp_s[cp * 64 : (cp + 1) * 64, :], rights, NT)
-        for c2 in range(2):
-            tiles = [
-                block[c2 * 32 + xi * 8 : c2 * 32 + xi * 8 + 8, jg * 128 : jg * 128 + 128]
-                for xi in range(4)
-                for jg in range(8)
-            ]
-            lanes = (cp * 2 + c2) * 128
-            lhs_s[:, lanes : lanes + 128] = jnp.concatenate(tiles, axis=0).astype(BF16)
-    for xi in range(4):
-        update = dot(lhs_s[xi * 64 : (xi + 1) * 64, :], wide_s[...])
-        send_s[xi] = update.reshape(8, 8, 512).astype(BF16)
+
+    def contract(jc, _):
+        rights = r_s[pl.ds(jc * 2, 2)].reshape(256, SEQS)
+        block = dot(lp_s[...], rights, NT)
+        for c in range(32):
+            for xi in range(4):
+                rows = slice(c * 32 + xi * 8, c * 32 + xi * 8 + 8)
+                tile = jnp.concatenate([block[rows, :128], block[rows, 128:]], axis=0)
+                lhs_s[xi, jc, :, c * 128 : c * 128 + 128] = tile.astype(BF16)
+        return 0
+
+    lax.fori_loop(0, 4, contract, 0)
+    update = dot(lhs_s[...].reshape(256, 4096), wide_s[...])
+    send_s[...] = update.reshape(4, 8, 8, 512).astype(BF16)
     for slot in range(4):
         send(
             send_s.at[slot],
@@ -363,15 +549,29 @@
             p_recv.at[y_hi * 2 + y_lo],
             to_pair(slot),
         )
+    for piece in range(2):
+        for way in range(2):
+            region = gather_ref.at[far, rows_of(way, piece)]
+            arrived(region, u_recv.at[1, way, piece])
+            remote(region, region, u_send.at[2, way, piece], u_recv.at[2, way, piece], partner)
     for slot in range(8):
         sent(right_ref, r_send.at[slot], to_right(slot))
-        pltpu.make_async_copy(r_s.at[slot, core], r_s.at[slot, core], f_send.at[slot]).wait()
-    for slot in range(16):
+        arrived(right_ref, f_send.at[slot])
+    for slot in range(4):
         sent(left_ref, l_send.at[slot], to_left(slot))
+        sent(send_s.at[slot], p_send.at[slot], to_pair(slot))
+    for n in range(3):
+        arrived(half(x, 0), up_send.at[n])
+        arrived(half(x, 0), down_send.at[n])
+    for way in range(2):
+        for piece in range(2):
+            for stage in range(3):
+                arrived(relay_s.at[way, piece], u_send.at[stage, way, piece])
+            arrived(relay_s.at[way, piece], u_recv.at[2, way, piece])
+    arrived(upd_ref, u_send.at[3, 0, 0])
+    arrived(upd_ref, u_recv.at[3, 0, 0])
+    own.wait()
     for slot in range(4):
-        sent(upd_ref, u_send.at[slot], to_branch(slot))
-        sent(send_s.at[slot], p_send.at[slot], to_pair(slot))
-        arrived(gather_ref.at[slot], u_recv.at[slot])
         arrived(pair_ref.at[slot], p_recv.at[slot])
 
 
@@ -397,26 +597,38 @@
     vmem = pltpu.VMEM
     params = pltpu.CompilerParams(vmem_limit_bytes=VMEM_LIMIT)
 
-    bias_block = pl.pallas_call(
+    dma = pltpu.SemaphoreType.DMA
+    wcol_mine = jnp.transpose(column_proj_weight, (1, 0, 2)).reshape(256, 256)
+    bias, wcol = pl.pallas_call(
         bias_kernel,
-        out_shape=jax.ShapeDtypeStruct((HEADS, 8, 128), BF16),
-        compiler_params=params,
+        in_specs=[pl.BlockSpec(memory_space=vmem)] * 3,
+        out_specs=(pl.BlockSpec(memory_space=vmem),) * 2,
+        out_shape=(
+            jax.ShapeDtypeStruct((8, 2, 4, 2, 4, 8, 128), BF16),
+            jax.ShapeDtypeStruct((4, 256, 256), BF16),
+        ),
+        scratch_shapes=[
+            vmem((4, 2, 8, 128), BF16),
+            dma((32,)),
+            dma((32,)),
+            dma((4, 4)),
+            dma((4, 4)),
+            dma((8, 4)),
+            dma((3,)),
+            dma((4,)),
+        ],
+        compiler_params=pltpu.CompilerParams(
+            vmem_limit_bytes=VMEM_LIMIT, collective_id=1, has_side_effects=True
+        ),
         name="pair_bias",
-    )(pair_rep, bias_weight)
-    spread = jnp.broadcast_to(bias_block.reshape(1, 4, 2, 8, 128), (64, 4, 2, 8, 128))
-    bias = lax.all_to_all(
-        spread.reshape(256, 2, 8, 128), ("dap", "branch"), split_axis=0, concat_axis=0, tiled=True
-    ).reshape(64, 4, 2, 8, 128)
+    )(pair_rep, bias_weight, wcol_mine)
+    wcol = jnp.transpose(wcol.reshape(4, 256, 4, 64), (1, 2, 0, 3)).reshape(256, 1024)
 
     by_owner = alignment.reshape(8, 64, 4, 2, 256)
     mine = lax.dynamic_slice_in_dim(by_owner, branch, 1, 2)[:, :, 0]
     mine = jnp.transpose(mine.reshape(4, 2, 64, 2, 256), (2, 3, 1, 0, 4))
     moved = lax.all_to_all(mine, "dap", split_axis=0, concat_axis=0, tiled=True)
     residual = jnp.transpose(moved, (1, 2, 0, 3, 4)).reshape(2, SEQS, 256)
-
-    wcol = jnp.broadcast_to(column_proj_weight[None], (4, 4, 256, 64))
-    wcol = lax.all_to_all(wcol, "branch", split_axis=0, concat_axis=0, tiled=True)
-    wcol = jnp.transpose(wcol, (2, 1, 0, 3)).reshape(256, 1024)
 
     half = jnp.transpose(row_proj_weight, (1, 0, 2))
     none = jnp.zeros_like(half)
@@ -453,13 +665,13 @@
         in_specs=[
             pl.BlockSpec((2, SEQS, 256), lambda i: (i, 0, 0)),
             whole((512, 512)),
-            whole((64, 4, 2, 8, 128)),
+            whole((8, 2, 4, 2, 4, 8, 128)),
             pl.BlockSpec((1, SEQS, 128), lambda i: (i, 0, 0)),
             pl.BlockSpec((1, 2, SEQS), lambda i: (i, 0, 0)),
         ],
         out_specs=whole((256, 8, 128)),
         out_shape=jax.ShapeDtypeStruct((256, 8, 128), BF16),
-        scratch_shapes=attend_scratch + [vmem((2048, 128), F32)],
+        scratch_shapes=attend_scratch + [vmem((2048, 128), F32), vmem((2, SEQS, SEQS), F32)],
         compiler_params=params,
         name="row_attention",
     )(alignment, wrow, bias, row_maskcol, row_mask)
@@ -508,7 +720,6 @@
         res_mask,
     )
 
-    dma = pltpu.SemaphoreType.DMA
     gathered, pairs = pl.pallas_call(
         outer_kernel,
         in_specs=[pl.BlockSpec(memory_space=vmem)] * 4,
@@ -518,21 +729,25 @@
             jax.ShapeDtypeStruct((4, 8, 8, 512), BF16),
         ),
         scratch_shapes=[
-            vmem((16, 64, SEQS), BF16),
+            vmem((4, 4, 64, SEQS), BF16),
             vmem((1024, SEQS), BF16),
             vmem((8, 2, 64, SEQS), BF16),
             vmem((1024, 1024), BF16),
             vmem((4096, 512), BF16),
-            vmem((256, 4096), BF16),
+            vmem((4, 4, 16, 4096), BF16),
             vmem((4, 8, 8, 512), BF16),
-            dma((16,)),
-            dma((16,)),
+            vmem((2, 2, 256, 256), BF16),
+            dma((4,)),
+            dma((4,)),
+            dma((3,)),
+            dma((3,)),
+            dma((4, 2)),
             dma((8,)),
             dma((8, 2)),
             dma((8,)),
             dma((8,)),
-            dma((4,)),
-            dma((4,)),
+            dma((4, 2, 2)),
+            dma((4, 2, 2)),
             dma((4,)),
             dma((4,)),
         ],

time: 195 us -> 155 us (0.79)
  waiting for transfers between devices: 49.2 us -> 15.4 us
  starting transfers between devices: 33.2 us -> 21.9 us
  Pallas kernels: 84.3 us -> 93.7 us
  local copies, waits for them, and re-layouts: 23.3 us -> 19 us
    all_to_all x2 -> x0, waiting for transfers between devices: 33.6 us -> none  [the longest x1 26.8 us: per_device(): lax.all_to_all(spread.reshape(256, 2, 8, 128), ('dap', 'branch'), split_a...]
    pallas_call x1, Pallas kernels: 2.07 us -> 30.8 us  [per_device(): pl.pallas_call(bias_kernel, in_specs=[pl.BlockSpec(memory_space=vmem)] *...]
    all_to_all x2 -> x0, starting transfers between devices: 16.5 us -> none  [the longest x1 11.9 us: per_device(): lax.all_to_all(spread.reshape(256, 2, 8, 128), ('dap', 'branch'), split_a...]
    pallas_call x1, Pallas kernels: 47.7 us -> 33.4 us  [per_device(): pl.pallas_call(outer_kernel, in_specs=[pl.BlockSpec(memory_space=vmem)] *...]
    all_to_all x1, starting transfers between devices: 5.2 us -> 12.6 us  [per_device(): moved = lax.all_to_all(mine, 'dap', split_axis=0, concat_axis=0, tiled=True)]
    broadcast_in_dim x2 -> x0, local copies, waits for them, and re-layouts: 3.72 us -> none  [the longest x1 1.97 us: per_device(): jnp.broadcast_to(bias_block.reshape(1, 4, 2, 8, 128), (64, 4, 2, 8, 128))]
    pallas_call x1, Pallas kernels: 17.8 us -> 14.9 us  [per_device(): pl.pallas_call(row_kernel, grid=(4,), in_specs=[pl.BlockSpec((2, SEQS, 25...]
    all_to_all x1, starting transfers between devices: 11.5 us -> 9.26 us  [per_device(): lax.all_to_all(heads, ('dap', 'branch'), split_axis=0, concat_axis=0, til...]
  transfers between devices with their start and end apart: 4 -> 2, of which waited for: 3 -> 1; matrix products, arithmetic and copies ran while one was open for 7% -> 6% of each run, Pallas kernels for 10% -> 30%
where the time goes in v2:
time: 155 us; the launch traced here: 153 us
  Pallas kernels  93.7 us (60%)
  starting transfers between devices  21.9 us (14%)
  local copies, waits for them, and re-layouts  19 us (12%)
  waiting for transfers between devices  15.4 us (10%)
  other arithmetic  2.01 us (1%)
    pallas_call x1, Pallas kernels, per_device(): pl.pallas_call(outer_kernel, in_specs=[pl.BlockSpec(memory_space=vmem)] *...  33.4 us
    pallas_call x1, Pallas kernels, per_device(): pl.pallas_call(bias_kernel, in_specs=[pl.BlockSpec(memory_space=vmem)] *...  30.8 us
    all_to_all x1, waiting for transfers between devices, per_device(): lax.all_to_all(heads, ('dap', 'branch'), split_axis=0, concat_axis=0, til...  15.4 us
    pallas_call x1, Pallas kernels, per_device(): pl.pallas_call(row_kernel, grid=(4,), in_specs=[pl.BlockSpec((2, SEQS, 25...  14.9 us
    pallas_call x1, Pallas kernels, per_device(): pl.pallas_call(column_kernel, grid=(2,), in_specs=[whole((64, 4, 8, 128))...  14.5 us
    all_to_all x1, starting transfers between devices, per_device(): moved = lax.all_to_all(mine, 'dap', split_axis=0, concat_axis=0, tiled=True)  12.6 us
    all_to_all x1, starting transfers between devices, per_device(): lax.all_to_all(heads, ('dap', 'branch'), split_axis=0, concat_axis=0, til...  9.26 us
    unnamed x28, local copies, waits for them, and re-layouts  4.29 us
  transfers between devices with their start and end apart: 2, of which 1 were waited for; matrix products, arithmetic and copies ran while one was open for 6% of the time, Pallas kernels for 30%

profile of v2, /device:TPU:32, one launch (start us, length us, event | category | flops | bytes accessed | tf_op | source)
XLA Modules:
  0.0 153.1 jit_solution(5552742072337814473)
XLA Ops:
  0.6 2.8 %copy.52 = bf16[8,512,256]{2,0,1:T(8,128)(2,1)S(1)} copy(bf16[8,512,256]{2,1,0:T(8,128)(2,1)} %x_ref.1) | data formatting | bytes 4194304 | tf_op args[0]
  3.7 1.4 copy.54
  5.0 12.6 %all-to-all-start.1 = ((bf16[64,2,2,4,256]{4,1,2,3,0:T(2,128)(2,1)}), bf16[64,2,2,4,256]{4,1,2,3,0:T(2,128)(2,1)S(1)}, u32[]{:S(2)}, u32[]{:S(2)}) async-start(bf16[64,2,2,4,256]{4,1,2,3,0:T(2,128)(2,1)} %copy.54), calls=%async_computation.1 | async-start | bytes 1048576 | tf_op jit(solution)/shard_map/all_to_all | solution.py:630
  17.8 1.0 copy.51.maskcol_ref
  18.8 0.8 copy.50.wcol_ref
  19.5 0.7 copy.49.weight_ref
  20.3 1.0 copy.63.w_ref
  21.3 30.8 %pair_bias.1 = (bf16[8,2,4,2,4,8,128]{6,5,4,3,2,1,0:T(8,128)(2,1)}, bf16[4,256,256]{2,1,0:T(8,128)(2,1)}) custom-call(bf16[8,128,128]{2,1,0:T(8,128)(2,1)} %pair_ref.1, bf16[128,8]{1,0:T(8,128)(2,1)} %copy.49.weight_ref, bf16[256,256]{1,0:T(8,128)(2,1)} %copy.50.wcol_ref), custom_call_target="tpu_custom_call" | custom-call | tf_op jit(solution)/shard_map/pair_bias/pallas_call | solution.py:602
  52.2 14.9 %row_attention.1 = bf16[256,8,128]{2,1,0:T(8,128)(2,1)} custom-call(bf16[8,512,256]{2,1,0:T(8,128)(2,1)} %x_ref.1, bf16[512,512]{1,0:T(8,128)(2,1)} %copy.63.w_ref, bf16[8,2,4,2,4,8,128]{6,5,4,3,2,1,0:T(8,128)(2,1)} %get-tuple-element.9.bias_ref, bf16[4,512,128]{2,1,0:T(8,128)(2,1)} %copy.51.maskcol_ref, f32[4,2,512]{2,1,0:T(2,128)} %copy-done.5), custom_call_target="tpu_custom_call" | custom-call | tf_op jit(solution)/shard_map/row_attention/pallas_call | solution.py:662
  67.1 9.3 %all-to-all-start = ((bf16[256,8,128]{2,1,0:T(8,128)(2,1)}), bf16[256,8,128]{2,1,0:T(8,128)(2,1)S(1)}, u32[]{:S(2)}, u32[]{:S(2)}) async-start(bf16[256,8,128]{2,1,0:T(8,128)(2,1)} %row_attention.1), calls=%async_computation | async-start | bytes 1048576 | tf_op jit(solution)/shard_map/all_to_all | solution.py:678
  76.7 0.6 reshape.79.maskrow_ref
  77.5 1.0 copy.59.wcol_ref
  78.6 0.7 copy.60.wfac_ref
  79.4 0.8 fusion.5
  80.3 0.3 fusion
  80.6 0.2 copy.55
  80.8 0.9 reshape.73.res_ref
  81.8 15.4 %all-to-all-done = bf16[256,8,128]{2,1,0:T(8,128)(2,1)S(1)} async-done(((bf16[256,8,128]{2,1,0:T(8,128)(2,1)}), bf16[256,8,128]{2,1,0:T(8,128)(2,1)S(1)}, u32[]{:S(2)}, u32[]{:S(2)}) %all-to-all-start) | async-done | bytes 524320 | tf_op jit(solution)/shard_map/all_to_all | solution.py:678
  97.1 0.9 broadcast_in_dim.5.maskcol_ref
  98.0 14.5 %column_attention.1 = (bf16[2,512,256]{2,1,0:T(8,128)(2,1)}, bf16[2,32,512]{2,1,0:T(8,128)(2,1)}, bf16[2,32,512]{2,1,0:T(8,128)(2,1)}) custom-call(bf16[64,4,8,128]{3,2,1,0:T(8,128)(2,1)} %bitcast.39, bf16[2,512,256]{2,1,0:T(8,128)(2,1)} %reshape.73.res_ref, bf16[512,512]{1,0:T(8,128)(2,1)} %bitcast.38, bf16[256,1024]{1,0:T(8,128)(2,1)} %copy.59.wcol_ref, ...), custom_call_target="tpu_custom_call" | custom-call | tf_op jit(solution)/shard_map/column_attention/pallas_call | solution.py:680
  112.6 33.4 %outer_product.1 = (bf16[4,1024,256]{2,1,0:T(8,128)(2,1)}, bf16[4,8,8,512]{3,2,1,0:T(8,128)(2,1)}) custom-call(bf16[64,512]{1,0:T(8,128)(2,1)} %bitcast.54, bf16[64,512]{1,0:T(8,128)(2,1)} %bitcast.55, bf16[1024,256]{1,0:T(8,128)(2,1)} %bitcast.49, bf16[1024,128]{1,0:T(8,128)(2,1)} %weight_ref.2), custom_call_target="tpu_custom_call" | custom-call | tf_op jit(solution)/shard_map/outer_product/pallas_call | solution.py:723
  146.0 3.7 %copy.61 = bf16[256,2,4,2,256]{4,3,2,1,0:T(2,128)(2,1)S(1)} copy(bf16[256,2,4,2,256]{4,0,1,3,2:T(8,128)(2,1)} %bitcast.41) | data formatting | bytes 4194304 | tf_op jit(solution)/shard_map/transpose | solution.py:765
  149.8 2.2 %reshape.84 = bf16[512,8,256]{2,1,0:T(8,128)(2,1)} reshape(bf16[256,2,4,2,256]{4,3,2,1,0:T(2,128)(2,1)S(1)} %copy.61) | data formatting | bytes 4194304 | tf_op jit(solution)/shard_map/reshape | solution.py:766
  152.2 0.9 add_convert_fusion
  (43 shorter events, 1.2 us)
Async XLA Ops:
  3.4 14.2 %copy-start.2 = (s32[512,512]{1,0:T(8,128)S(1)}, s32[512,512]{1,0:T(8,128)}, u32[]{:S(2)}) copy-start(s32[512,512]{1,0:T(8,128)} %param.13) | copy-start | bytes 3145732
  3.6 15.1 %copy-start.8 = (bf16[4,256,64]{1,2,0:T(8,128)(2,1)S(1)}, bf16[4,256,64]{1,2,0:T(8,128)(2,1)}, u32[]{:S(2)}) copy-start(bf16[4,256,64]{1,2,0:T(8,128)(2,1)} %param.18) | copy-start | bytes 393220
  3.6 15.9 %copy-start.10 = (bf16[128,8]{0,1:T(8,128)(2,1)S(1)}, bf16[128,8]{0,1:T(8,128)(2,1)}, u32[]{:S(2)}) copy-start(bf16[128,8]{0,1:T(8,128)(2,1)} %param.15) | copy-start | bytes 6148
  3.7 16.6 %copy-start.6 = (bf16[4,256,64]{1,2,0:T(8,128)(2,1)S(1)}, bf16[4,256,64]{1,2,0:T(8,128)(2,1)}, u32[]{:S(2)}) copy-start(bf16[4,256,64]{1,2,0:T(8,128)(2,1)} %param.16) | copy-start | bytes 393220
  5.0 62.1 %all-to-all-start.1 = ((bf16[64,2,2,4,256]{4,1,2,3,0:T(2,128)(2,1)}), bf16[64,2,2,4,256]{4,1,2,3,0:T(2,128)(2,1)S(1)}, u32[]{:S(2)}, u32[]{:S(2)}) async-start(bf16[64,2,2,4,256]{4,1,2,3,0:T(2,128)(2,1)} %copy.54), calls=%async_computation.1 | async-start | bytes 1048576 | tf_op jit(solution)/shard_map/all_to_all | solution.py:630
  17.7 34.5 %copy-start.5 = (f32[4,2,512]{2,1,0:T(2,128)}, f32[4,2,512]{2,1,0:T(2,128)S(1)}, u32[]{:S(2)}) copy-start(f32[4,2,512]{2,1,0:T(2,128)S(1)} %reshape.70.maskrow_ref) | copy-start | bytes 49156
  67.1 10.2 %copy-start.3 = (bf16[4,256,256]{2,1,0:T(8,128)(2,1)S(1)}, bf16[4,256,256]{2,1,0:T(8,128)(2,1)}, u32[]{:S(2)}) copy-start(bf16[4,256,256]{2,1,0:T(8,128)(2,1)} %get-tuple-element.10) | copy-start | bytes 1572868
  67.1 30.0 %all-to-all-start = ((bf16[256,8,128]{2,1,0:T(8,128)(2,1)}), bf16[256,8,128]{2,1,0:T(8,128)(2,1)S(1)}, u32[]{:S(2)}, u32[]{:S(2)}) async-start(bf16[256,8,128]{2,1,0:T(8,128)(2,1)} %row_attention.1), calls=%async_computation | async-start | bytes 1048576 | tf_op jit(solution)/shard_map/all_to_all | solution.py:678
  76.4 2.2 %copy-start.9 = (bf16[256,64]{0,1:T(8,128)(2,1)S(1)}, bf16[256,64]{0,1:T(8,128)(2,1)}, u32[]{:S(2)}) copy-start(bf16[256,64]{0,1:T(8,128)(2,1)} %param.20) | copy-start | bytes 98308
  76.4 2.9 %copy-start.11 = (s32[512]{0:T(512)S(1)}, s32[512]{0:T(512)}, u32[]{:S(2)}) copy-start(s32[512]{0:T(512)} %param.14) | copy-start | bytes 6148
  76.4 3.1 %copy-start.7 = (bf16[256,256]{1,0:T(8,128)(2,1)S(1)}, bf16[256,256]{1,0:T(8,128)(2,1)}, u32[]{:S(2)}) copy-start(bf16[256,256]{1,0:T(8,128)(2,1)} %param.17) | copy-start | bytes 393220
  97.1 0.9 copy-start
  149.8 2.2 %copy-start.4 = (bf16[4,8,8,512]{3,2,1,0:T(8,128)(2,1)S(1)}, bf16[4,8,8,512]{3,2,1,0:T(8,128)(2,1)}, u32[]{:S(2)}) copy-start(bf16[4,8,8,512]{3,2,1,0:T(8,128)(2,1)} %get-tuple-element.15) | copy-start | bytes 786436
  149.8 2.4 %copy-start.1 = (bf16[8,128,128]{2,1,0:T(8,128)(2,1)S(1)}, bf16[8,128,128]{2,1,0:T(8,128)(2,1)}, u32[]{:S(2)}) copy-start(bf16[8,128,128]{2,1,0:T(8,128)(2,1)} %pair_ref.1) | copy-start | bytes 786436

commit v3 on v2

--- a/solution.py
+++ b/solution.py
@@ -115,13 +115,40 @@
     pltpu.make_async_copy(dst, dst, semaphore).wait()
 
 
-def bias_kernel(
+def attend_tile(q, k, rhs_s, lane_masks, extra):
+    total = None
+    for n in range(4):
+        scores = dot(q * lane_masks[n], k, NT) + extra(n)
+        scores = scores - jnp.max(scores, axis=1, keepdims=True)
+        raised = jnp.exp2(scores).astype(BF16)
+        part = dot(raised, rhs_s[n * SEQS : (n + 1) * SEQS, :])
+        total = part if total is None else total + part
+    return total[:, :128] / total[:, 128:]
+
+
+def front_kernel(
     pair_ref,
     weight_ref,
     wcol_ref,
-    bias_ref,
+    x_ref,
+    wrow_ref,
+    off_ref,
+    heads_ref,
+    resid_ref,
     wall_ref,
     block_s,
+    bias_s,
+    wide_s,
+    q_s,
+    k_s,
+    g_s,
+    rhs_s,
+    x_s,
+    res_s,
+    resb_s,
+    o_s,
+    buf_s,
+    out_s,
     p_send,
     p_recv,
     up_send,
@@ -129,10 +156,27 @@
     z_recv,
     w_send,
     w_recv,
+    res_send,
+    res_recv,
+    out_send,
+    out_recv,
 ):
     at = place()
     branch, dap, x, z, y_lo = at["branch"], at["dap"], at["x"], at["z"], at["y_lo"]
     barrier = pltpu.get_barrier_semaphore()
+    me = dap * 4 + branch
+
+    def device(slot):
+        return (slot % 4, slot // 4)
+
+    def greet(slot, _):
+        @pl.when(slot != me)
+        def _():
+            signal(barrier, device(slot))
+
+        return 0
+
+    lax.fori_loop(0, 256, greet, 0)
 
     def to_plane(slot):
         return (slot % 4, slot // 8 * 16 + z * 2 + slot // 4 % 2)
@@ -141,25 +185,6 @@
         return (branch, x * 16 + other_z * 2 + y_lo)
 
     mine = x * 8 + y_lo * 4 + branch
-
-    def greet(slot, _):
-        @pl.when(slot != mine)
-        def _():
-            signal(barrier, to_plane(slot))
-
-        return 0
-
-    lax.fori_loop(0, 32, greet, 0)
-
-    def greet_line(other_z, _):
-        @pl.when(other_z != z)
-        def _():
-            signal(barrier, line(other_z))
-
-        return 0
-
-    lax.fori_loop(0, 8, greet_line, 0)
-
     rows, cols, width = pair_ref.shape
     values = pair_ref[...].astype(F32).reshape(rows * cols, width)
     normed = normalize(values).astype(BF16)
@@ -167,10 +192,10 @@
     for i in range(rows):
         tile = res[:, i * cols : (i + 1) * cols].astype(BF16)
         block_s[:, :, i, :] = tile.reshape(4, 2, cols)
-    pl.semaphore_wait(barrier, 31 + 7)
+    pl.semaphore_wait(barrier, 255)
 
     def post(slot, _):
-        target = bias_ref.at[z, :, x, y_lo, branch]
+        target = bias_s.at[z, :, x, y_lo, branch]
 
         @pl.when(slot != mine)
         def _():
@@ -191,14 +216,44 @@
     own = pltpu.make_async_copy(wcol_ref, wall_ref.at[branch], w_recv.at[3])
     own.start()
 
+    def project(sp, _):
+        normed = []
+        for p in range(2):
+            value = x_ref[sp * 2 + p].astype(F32)
+            for side in range(2):
+                x_s[side] = value[:, side * 128 : side * 128 + 128]
+                for k in range(2):
+                    res_s[side, pl.ds(sp * 4 + k * 2 + p, 64, stride=16), :] = x_s[
+                        side, pl.ds(branch * 2 + k, 64, stride=8), :
+                    ]
+            normed.append(normalize(value).astype(BF16))
+        both = jnp.concatenate(normed, axis=1)
+        projected = dot(both, wrow_ref[...])
+        q_s[sp] = (projected[:, :128] * QUERY_SCALE).astype(BF16)
+        k_s[sp] = projected[:, 128:256].astype(BF16)
+        values = projected[:, 256:384].astype(BF16)
+        g_s[sp] = jax.nn.sigmoid(projected[:, 384:])
+        for n in range(4):
+            rhs_s[sp, n * SEQS : (n + 1) * SEQS, :128] = values * lane_block(n)
+            rhs_s[sp, n * SEQS : (n + 1) * SEQS, 128:] = jnp.broadcast_to(
+                lane_block(n), (SEQS, 128)
+            )
+        return 0
+
+    lax.fori_loop(0, 4, project, 0)
+    for side in range(2):
+        resb_s[:, :, side * 128 : side * 128 + 128] = (
+            res_s[side].reshape(64, 16, 128).astype(BF16)
+        )
+
     def collect(slot, _):
-        arrived(bias_ref.at[z, :, slot // 8, slot // 4 % 2, slot % 4], p_recv.at[slot])
+        arrived(bias_s.at[z, :, slot // 8, slot // 4 % 2, slot % 4], p_recv.at[slot])
         return 0
 
     lax.fori_loop(0, 32, collect, 0)
 
     def chunk(other_z, c):
-        return bias_ref.at[other_z, c // 2, pl.ds(c % 2 * 2, 2)]
+        return bias_s.at[other_z, c // 2, pl.ds(c % 2 * 2, 2)]
 
     up, down = lax.rem(z + 1, 8), lax.rem(z + 7, 8)
 
@@ -226,9 +281,71 @@
                 pass_down(t, c)
     arrived(wall_ref.at[far], w_recv.at[1])
     remote(wall_ref.at[far], wall_ref.at[far], w_send.at[2], w_recv.at[2], partner)
+
+    def post_res(slot, _):
+        target = resid_ref.at[dap]
+
+        @pl.when(slot != dap)
+        def _():
+            remote(resb_s.at[slot], target, res_send, res_recv, (branch, slot))
+
+        @pl.when(slot == dap)
+        def _():
+            pltpu.make_async_copy(resb_s.at[slot], target, res_recv).start()
+
+        return 0
+
+    lax.fori_loop(0, 64, post_res, 0)
     opposite = lax.rem(z + 4, 8)
     for c in range(4):
         arrived(chunk(opposite, c), z_recv.at[opposite, c])
+
+    for xx in range(4):
+        for h in range(2):
+            for b in range(4):
+                piece = bias_s[:, h, xx, :, b].astype(F32).reshape(128, 128)
+                wide_s[h, xx * 128 : xx * 128 + 128, b * 128 : b * 128 + 128] = piece * LOG2E
+
+    def step(t, _):
+        other_x = lax.rem(x + t, 4)
+        span = pl.ds(pl.multiple_of(other_x * 128, 128), 128)
+        masks = [lane_block(n) for n in range(4)]
+
+        def some(u, _):
+            for v in range(2):
+                sp = u * 2 + v
+
+                def extra(n):
+                    return wide_s[n % 2, span, :] + off_ref[sp, pl.ds(n // 2, 1), :]
+
+                out = attend_tile(q_s[sp, span, :], k_s[sp], rhs_s.at[sp], masks, extra)
+                o_s[v] = out * g_s[sp, span, :]
+                for k in range(2):
+                    buf_s[pl.ds(sp * 2 + k, 64, stride=8), :] = o_s[v, pl.ds(k, 64, stride=2), :]
+            return 0
+
+        lax.fori_loop(0, 2, some, 0)
+        base = other_x * 64
+        out_s[pl.ds(base, 64)] = buf_s[...].reshape(64, 8, 128).astype(BF16)
+
+        def post_out(j, _):
+            slot = base + j
+
+            @pl.when(slot != me)
+            def _():
+                remote(out_s.at[slot], heads_ref.at[me], out_send, out_recv, device(slot))
+
+            @pl.when(slot == me)
+            def _():
+                pltpu.make_async_copy(out_s.at[slot], heads_ref.at[me], out_recv).start()
+
+            return 0
+
+        lax.fori_loop(0, 64, post_out, 0)
+        return 0
+
+    lax.fori_loop(0, 4, step, 0)
+
     for t in range(4):
         for c in range(4):
             if t < 3 or c < 2:
@@ -249,39 +366,10 @@
         arrived(wcol_ref, w_send.at[n])
     arrived(wcol_ref, w_recv.at[0])
     arrived(wcol_ref, w_recv.at[2])
-
-
-def row_kernel(
-    x_ref, w_ref, bias_ref, maskcol_ref, maskrow_ref, out_ref, q_s, k_s, g_s, rhs_s, o_s, buf, bias_s
-):
-    pair = pl.program_id(0)
-    normed = [normalize(x_ref[p].astype(F32)).astype(BF16) for p in range(2)]
-    both = jnp.concatenate(normed, axis=1)
-    projected = dot(both, w_ref[...])
-    q_s[...] = (projected[:, :128] * QUERY_SCALE).astype(BF16)
-    k_s[...] = projected[:, 128:256].astype(BF16)
-    fill_values(rhs_s, projected[:, 256:384].astype(BF16), maskcol_ref[0])
-    fill_ones(rhs_s, maskcol_ref[0])
-    g_s[...] = jax.nn.sigmoid(projected[:, 384:])
-
-    @pl.when(pair == 0)
-    def _():
-        for x in range(4):
-            for h in range(2):
-                for b in range(4):
-                    piece = bias_ref[:, h, x, :, b].astype(F32).reshape(128, 128)
-                    bias_s[h, x * 128 : x * 128 + 128, b * 128 : b * 128 + 128] = piece * LOG2E
-
-    def bias_of(step, n):
-        return bias_s[n % 2, pl.ds(pl.multiple_of(step * TILE, TILE), TILE), :]
-
-    attend(q_s, k_s, g_s, rhs_s, o_s, bias_of, lambda n: maskrow_ref[0, n // 2 : n // 2 + 1, :])
-    for k in range(2):
-        buf[pl.ds(pair * 2 + k, 256, stride=8), :] = o_s[pl.ds(k, 256, stride=2), :]
-
-    @pl.when(pair == pl.num_programs(0) - 1)
-    def _():
-        out_ref[...] = buf[...].reshape(256, 8, 128).astype(BF16)
+    arrived(resb_s.at[pl.ds(0, 63)], res_send)
+    arrived(resid_ref, res_recv)
+    arrived(out_s.at[pl.ds(0, 255)], out_send)
+    arrived(heads_ref, out_recv)
 
 
 def column_kernel(
@@ -297,6 +385,7 @@
     left_ref,
     right_ref,
     x_s,
+    res_s,
     msa_s,
     n_s,
     q_s,
@@ -314,12 +403,24 @@
         x = dot(jnp.concatenate(pieces, axis=1), wrow_ref[...])
         for j in range(4):
             x_s[j] = x[:, j * 128 : (j + 1) * 128]
+        for side in range(2):
+            block = res_ref[:, :, side * 128 : side * 128 + 128].astype(F32)
+            res_s[side] = block.reshape(1024, 128)
 
     mine = [x_s[j, pl.ds(k, 256, stride=2), :] for j in range(4)]
     rows = jnp.concatenate(
         [jnp.concatenate(mine[:2], axis=1), jnp.concatenate(mine[2:], axis=1)], axis=0
     )
-    msa = (rows + res_ref[0].astype(F32)).astype(BF16).astype(F32)
+    base = jnp.concatenate(
+        [
+            jnp.concatenate(
+                [res_s[side, pl.ds(k * 2 + p, 256, stride=4), :] for side in range(2)], axis=1
+            )
+            for p in range(2)
+        ],
+        axis=0,
+    )
+    msa = (rows + base).astype(BF16).astype(F32)
     msa_s[...] = msa
     n_s[...] = normalize(msa).astype(BF16)
     fill_ones(rhs_s, maskcol_ref[0])
@@ -598,38 +699,6 @@
     params = pltpu.CompilerParams(vmem_limit_bytes=VMEM_LIMIT)
 
     dma = pltpu.SemaphoreType.DMA
-    wcol_mine = jnp.transpose(column_proj_weight, (1, 0, 2)).reshape(256, 256)
-    bias, wcol = pl.pallas_call(
-        bias_kernel,
-        in_specs=[pl.BlockSpec(memory_space=vmem)] * 3,
-        out_specs=(pl.BlockSpec(memory_space=vmem),) * 2,
-        out_shape=(
-            jax.ShapeDtypeStruct((8, 2, 4, 2, 4, 8, 128), BF16),
-            jax.ShapeDtypeStruct((4, 256, 256), BF16),
-        ),
-        scratch_shapes=[
-            vmem((4, 2, 8, 128), BF16),
-            dma((32,)),
-            dma((32,)),
-            dma((4, 4)),
-            dma((4, 4)),
-            dma((8, 4)),
-            dma((3,)),
-            dma((4,)),
-        ],
-        compiler_params=pltpu.CompilerParams(
-            vmem_limit_bytes=VMEM_LIMIT, collective_id=1, has_side_effects=True
-        ),
-        name="pair_bias",
-    )(pair_rep, bias_weight, wcol_mine)
-    wcol = jnp.transpose(wcol.reshape(4, 256, 4, 64), (1, 2, 0, 3)).reshape(256, 1024)
-
-    by_owner = alignment.reshape(8, 64, 4, 2, 256)
-    mine = lax.dynamic_slice_in_dim(by_owner, branch, 1, 2)[:, :, 0]
-    mine = jnp.transpose(mine.reshape(4, 2, 64, 2, 256), (2, 3, 1, 0, 4))
-    moved = lax.all_to_all(mine, "dap", split_axis=0, concat_axis=0, tiled=True)
-    residual = jnp.transpose(moved, (1, 2, 0, 3, 4)).reshape(2, SEQS, 256)
-
     half = jnp.transpose(row_proj_weight, (1, 0, 2))
     none = jnp.zeros_like(half)
     wrow = jnp.concatenate(
@@ -646,8 +715,8 @@
     ).reshape(512, 512)
 
     seq_mask = lax.dynamic_slice_in_dim(align_mask, dap * 8, 8, 0).astype(F32)
-    row_mask = seq_mask.reshape(4, 2, SEQS)
-    row_maskcol = jnp.repeat(jnp.transpose(row_mask, (0, 2, 1)), 64, axis=2).astype(BF16)
+    offset = ((seq_mask - 1.0) * 1e30).reshape(4, 2, SEQS)
+    wcol_mine = jnp.transpose(column_proj_weight, (1, 0, 2)).reshape(256, 256)
     res_mask = lax.dynamic_slice_in_dim(align_mask, dap * 8 + branch * 2, 2, 1).astype(F32)
     res_mask = jnp.transpose(res_mask.reshape(256, 2, 2), (2, 1, 0)).reshape(2, 1, SEQS)
     col_maskcol = jnp.broadcast_to(res_mask.reshape(2, SEQS, 1), (2, SEQS, 128)).astype(BF16)
@@ -659,30 +728,54 @@
         vmem((4 * SEQS, 256), BF16),
         vmem((SEQS, 128), F32),
     ]
-    heads = pl.pallas_call(
-        row_kernel,
-        grid=(4,),
-        in_specs=[
-            pl.BlockSpec((2, SEQS, 256), lambda i: (i, 0, 0)),
-            whole((512, 512)),
-            whole((8, 2, 4, 2, 4, 8, 128)),
-            pl.BlockSpec((1, SEQS, 128), lambda i: (i, 0, 0)),
-            pl.BlockSpec((1, 2, SEQS), lambda i: (i, 0, 0)),
+    got, residual, wcol = pl.pallas_call(
+        front_kernel,
+        in_specs=[pl.BlockSpec(memory_space=vmem)] * 6,
+        out_specs=(pl.BlockSpec(memory_space=vmem),) * 3,
+        out_shape=(
+            jax.ShapeDtypeStruct((256, 8, 128), BF16),
+            jax.ShapeDtypeStruct((64, 16, 256), BF16),
+            jax.ShapeDtypeStruct((4, 256, 256), BF16),
+        ),
+        scratch_shapes=[
+            vmem((4, 2, 8, 128), BF16),
+            vmem((8, 2, 4, 2, 4, 8, 128), BF16),
+            vmem((2, SEQS, SEQS), F32),
+            vmem((4, SEQS, 128), BF16),
+            vmem((4, SEQS, 128), BF16),
+            vmem((4, SEQS, 128), F32),
+            vmem((4, 4 * SEQS, 256), BF16),
+            vmem((2, SEQS, 128), F32),
+            vmem((2, 1024, 128), F32),
+            vmem((64, 16, 256), BF16),
+            vmem((2, 128, 128), F32),
+            vmem((SEQS, 128), F32),
+            vmem((256, 8, 128), BF16),
+            dma((32,)),
+            dma((32,)),
+            dma((4, 4)),
+            dma((4, 4)),
+            dma((8, 4)),
+            dma((3,)),
+            dma((4,)),
+            dma,
+            dma,
+            dma,
+            dma,
         ],
-        out_specs=whole((256, 8, 128)),
-        out_shape=jax.ShapeDtypeStruct((256, 8, 128), BF16),
-        scratch_shapes=attend_scratch + [vmem((2048, 128), F32), vmem((2, SEQS, SEQS), F32)],
-        compiler_params=params,
+        compiler_params=pltpu.CompilerParams(
+            vmem_limit_bytes=VMEM_LIMIT, collective_id=1, has_side_effects=True
+        ),
         name="row_attention",
-    )(alignment, wrow, bias, row_maskcol, row_mask)
-    got = lax.all_to_all(heads, ("dap", "branch"), split_axis=0, concat_axis=0, tiled=True)
+    )(pair_rep, bias_weight, wcol_mine, alignment, wrow, offset)
+    wcol = jnp.transpose(wcol.reshape(4, 256, 4, 64), (1, 2, 0, 3)).reshape(256, 1024)
 
     updated, left, right = pl.pallas_call(
         column_kernel,
         grid=(2,),
         in_specs=[
             whole((64, 4, 8, 128)),
-            pl.BlockSpec((1, SEQS, 256), lambda i: (i, 0, 0)),
+            whole((64, 16, 256)),
             whole((512, 512)),
             whole((256, 1024)),
             whole((256, 256)),
@@ -702,6 +795,7 @@
         ),
         scratch_shapes=[
             vmem((4, SEQS, 128), F32),
+            vmem((2, 1024, 128), F32),
             vmem((SEQS, 256), F32),
             vmem((SEQS, 256), BF16),
         ]

time: 155 us -> 135 us (0.87)
  starting transfers between devices: 21.9 us -> 0 us
  Pallas kernels: 93.7 us -> 113 us
  waiting for transfers between devices: 15.4 us -> 0 us
  local copies, waits for them, and re-layouts: 19 us -> 14.4 us
  other arithmetic: 2.01 us -> 4.66 us
    all_to_all x2 -> x0, starting transfers between devices: 21.9 us -> none  [the longest x1 12.6 us: per_device(): moved = lax.all_to_all(mine, 'dap', split_axis=0, concat_axis=0, tiled=True)]
    pallas_call x2 -> x1, Pallas kernels: 45.8 us -> 62 us  [per_device(): pl.pallas_call(front_kernel, in_specs=[pl.BlockSpec(memory_space=vmem)] *...]
    all_to_all x2 -> x0, waiting for transfers between devices: 15.4 us -> none  [the longest x1 15.4 us: per_device(): lax.all_to_all(heads, ('dap', 'branch'), split_axis=0, concat_axis=0, til...]
    pallas_call x1, Pallas kernels: 33.4 us -> 36.1 us  [per_device(): pl.pallas_call(outer_kernel, in_specs=[pl.BlockSpec(memory_space=vmem)] *...]
    unnamed x28 -> x19, local copies, waits for them, and re-layouts: 4.29 us -> 1.78 us
    transpose x2 -> x0, local copies, waits for them, and re-layouts: 1.58 us -> none  [the longest x1 1.36 us: per_device(): mine = jnp.transpose(mine.reshape(4, 2, 64, 2, 256), (2, 3, 1, 0, 4))]
  transfers between devices with their start and end apart: 2 -> 0, of which waited for: 1 -> 0; matrix products, arithmetic and copies ran while one was open for 6% -> 0% of each run, Pallas kernels for 30% -> 0%
where the time goes in v3:
time: 135 us; the launch traced here: 133 us
  Pallas kernels  113 us (84%)
  local copies, waits for them, and re-layouts  14.4 us (11%)
  other arithmetic  4.66 us (3%)
    pallas_call x1, Pallas kernels, per_device(): pl.pallas_call(front_kernel, in_specs=[pl.BlockSpec(memory_space=vmem)] *...  62 us
    pallas_call x1, Pallas kernels, per_device(): pl.pallas_call(outer_kernel, in_specs=[pl.BlockSpec(memory_space=vmem)] *...  36.1 us
    pallas_call x1, Pallas kernels, per_device(): pl.pallas_call(column_kernel, grid=(2,), in_specs=[whole((64, 4, 8, 128))...  14.6 us
    transpose x1, local copies, waits for them, and re-layouts, per_device(): rows = jnp.transpose(gathered.reshape(4, 2, 2, 256, 256), (3, 2, 0, 1, 4))  3.75 us

profile of v3, /device:TPU:32, one launch (start us, length us, event | category | flops | bytes accessed | tf_op | source)
XLA Modules:
  0.0 132.9 jit_solution(17658017254351294481)
XLA Ops:
  0.7 1.1 dynamic-slice_convert_fusion.2
  1.8 0.1 copy.26
  1.9 0.9 broadcast_in_dim.2.maskcol_ref
  2.8 0.6 reshape.69.maskrow_ref
  3.5 0.7 add_multiply_fusion
  4.2 0.6 reshape.62.off_ref
  4.8 1.0 fusion.6
  5.8 1.0 copy.31.wrow_ref
  6.8 0.8 copy.23.wcol_ref
  7.6 0.7 copy.22.weight_ref
  8.3 62.0 %row_attention.1 = (bf16[256,8,128]{2,1,0:T(8,128)(2,1)}, bf16[64,16,256]{2,1,0:T(8,128)(2,1)}, bf16[4,256,256]{2,1,0:T(8,128)(2,1)}) custom-call(bf16[8,128,128]{2,1,0:T(8,128)(2,1)} %pair_ref.1, bf16[128,8]{1,0:T(8,128)(2,1)} %copy.22.weight_ref, bf16[256,256]{1,0:T(8,128)(2,1)} %copy.23.wcol_ref, bf16[8,512,256]{2,1,0:T(8,128)(2,1)} %x_ref.1, ...), custom_call_target="tpu_custom_call" | custom-call | tf_op jit(solution)/shard_map/row_attention/pallas_call | solution.py:731
  70.3 1.3 copy.24
  71.7 1.0 copy.27.wcol_ref
  72.7 0.8 fusion.5
  73.6 0.7 copy.28.wfac_ref
  74.3 14.6 %column_attention.1 = (bf16[2,512,256]{2,1,0:T(8,128)(2,1)}, bf16[2,32,512]{2,1,0:T(8,128)(2,1)}, bf16[2,32,512]{2,1,0:T(8,128)(2,1)}) custom-call(bf16[64,4,8,128]{3,2,1,0:T(8,128)(2,1)} %bitcast.36, bf16[64,16,256]{2,1,0:T(8,128)(2,1)} %get-tuple-element.11.res_ref, bf16[512,512]{1,0:T(8,128)(2,1)} %bitcast.29, bf16[256,1024]{1,0:T(8,128)(2,1)} %copy.27.wcol_ref, ...), custom_call_target="tpu_custom_call" | custom-call | tf_op jit(solution)/shard_map/column_attention/pallas_call | solution.py:773
  88.9 36.1 %outer_product.1 = (bf16[4,1024,256]{2,1,0:T(8,128)(2,1)}, bf16[4,8,8,512]{3,2,1,0:T(8,128)(2,1)}) custom-call(bf16[64,512]{1,0:T(8,128)(2,1)} %bitcast.42, bf16[64,512]{1,0:T(8,128)(2,1)} %bitcast.43, bf16[1024,256]{1,0:T(8,128)(2,1)} %bitcast.37, bf16[1024,128]{1,0:T(8,128)(2,1)} %weight_ref.2), custom_call_target="tpu_custom_call" | custom-call | tf_op jit(solution)/shard_map/outer_product/pallas_call | solution.py:817
  125.0 3.7 %copy.29 = bf16[256,2,4,2,256]{4,3,2,1,0:T(2,128)(2,1)S(1)} copy(bf16[256,2,4,2,256]{4,0,1,3,2:T(8,128)(2,1)} %bitcast.31) | data formatting | bytes 4194304 | tf_op jit(solution)/shard_map/transpose | solution.py:859
  128.8 2.2 %reshape.74 = bf16[512,8,256]{2,1,0:T(8,128)(2,1)} reshape(bf16[256,2,4,2,256]{4,3,2,1,0:T(2,128)(2,1)S(1)} %copy.29) | data formatting | bytes 4194304 | tf_op jit(solution)/shard_map/reshape | solution.py:860
  131.1 0.1 copy.30
  131.3 0.1 dynamic_slice.20
  131.4 0.3 fusion
  131.7 0.3 copy-done
  132.0 0.9 add_convert_fusion
  (21 shorter events, 0.2 us)
Async XLA Ops:
  0.6 6.2 %copy-start.4 = (bf16[4,256,64]{1,2,0:T(8,128)(2,1)S(1)}, bf16[4,256,64]{1,2,0:T(8,128)(2,1)}, u32[]{:S(2)}) copy-start(bf16[4,256,64]{1,2,0:T(8,128)(2,1)} %param.18) | copy-start | bytes 393220
  0.6 6.9 %copy-start.6 = (bf16[128,8]{0,1:T(8,128)(2,1)S(1)}, bf16[128,8]{0,1:T(8,128)(2,1)}, u32[]{:S(2)}) copy-start(bf16[128,8]{0,1:T(8,128)(2,1)} %param.15) | copy-start | bytes 6148
  70.3 2.4 %copy-start.3 = (bf16[256,256]{1,0:T(8,128)(2,1)S(1)}, bf16[256,256]{1,0:T(8,128)(2,1)}, u32[]{:S(2)}) copy-start(bf16[256,256]{1,0:T(8,128)(2,1)} %param.17) | copy-start | bytes 393220
  70.3 3.2 %copy-start.5 = (bf16[256,64]{0,1:T(8,128)(2,1)S(1)}, bf16[256,64]{0,1:T(8,128)(2,1)}, u32[]{:S(2)}) copy-start(bf16[256,64]{0,1:T(8,128)(2,1)} %param.20) | copy-start | bytes 98308
  128.8 2.2 %copy-start.2 = (bf16[4,8,8,512]{3,2,1,0:T(8,128)(2,1)S(1)}, bf16[4,8,8,512]{3,2,1,0:T(8,128)(2,1)}, u32[]{:S(2)}) copy-start(bf16[4,8,8,512]{3,2,1,0:T(8,128)(2,1)} %get-tuple-element.17) | copy-start | bytes 786436
  128.8 2.4 %copy-start.7 = (s32[512]{0:T(512)S(1)}, s32[512]{0:T(512)}, u32[]{:S(2)}) copy-start(s32[512]{0:T(512)} %param.14) | copy-start | bytes 6148
  128.8 2.6 %copy-start.1 = (s32[512,512]{1,0:T(8,128)S(1)}, s32[512,512]{1,0:T(8,128)}, u32[]{:S(2)}) copy-start(s32[512,512]{1,0:T(8,128)} %param.13) | copy-start | bytes 3145732
  131.0 0.9 copy-start

commit v4 on v3

--- a/solution.py
+++ b/solution.py
@@ -101,6 +101,12 @@
     )
 
 
+def z_turn(z, turn):
+    reach = (turn + 1) // 2
+    odd = turn % 2
+    return lax.rem(z + odd * reach + (1 - odd) * (8 - reach), 8)
+
+
 def signal(semaphore, to):
     pl.semaphore_signal(semaphore, 1, device_id=to, device_id_type=MESH)
 
@@ -137,6 +143,7 @@
     resid_ref,
     wall_ref,
     block_s,
+    line_s,
     bias_s,
     wide_s,
     q_s,
@@ -149,10 +156,10 @@
     o_s,
     buf_s,
     out_s,
+    ready,
     p_send,
     p_recv,
-    up_send,
-    down_send,
+    z_send,
     z_recv,
     w_send,
     w_recv,
@@ -165,49 +172,67 @@
     branch, dap, x, z, y_lo = at["branch"], at["dap"], at["x"], at["z"], at["y_lo"]
     barrier = pltpu.get_barrier_semaphore()
     me = dap * 4 + branch
-
-    def device(slot):
-        return (slot % 4, slot // 4)
-
-    def greet(slot, _):
-        @pl.when(slot != me)
-        def _():
-            signal(barrier, device(slot))
-
-        return 0
-
-    lax.fori_loop(0, 256, greet, 0)
-
-    def to_plane(slot):
-        return (slot % 4, slot // 8 * 16 + z * 2 + slot // 4 % 2)
+    mine = x * 8 + y_lo * 4 + branch
+
+    def plane_device(other_x, other_y, other_b):
+        return (other_b, other_x * 16 + z * 2 + other_y)
 
     def line(other_z):
         return (branch, x * 16 + other_z * 2 + y_lo)
 
-    mine = x * 8 + y_lo * 4 + branch
+    def in_plane(act):
+        def each(step_x, _):
+            other_x = lax.rem(x + step_x, 4)
+            for step_y in range(2):
+                other_y = lax.rem(y_lo + step_y, 2)
+                for step in range(1, 4):
+                    other_b = lax.rem(branch + step, 4)
+                    act(other_x * 8 + other_y * 4 + other_b, other_x, other_y, other_b)
+
+                @pl.when(jnp.logical_or(other_x != x, other_y != y_lo))
+                def _():
+                    act(other_x * 8 + other_y * 4 + branch, other_x, other_y, branch)
+
+            return 0
+
+        lax.fori_loop(0, 4, each, 0)
+
+    in_plane(lambda slot, *to: signal(barrier, plane_device(*to)))
+    for step in range(1, 8):
+        signal(barrier, line(lax.rem(z + step, 8)))
+
     rows, cols, width = pair_ref.shape
+
+    def pick(sp, _):
+        for p in range(2):
+            for side in range(2):
+                block = x_ref[sp * 2 + p, :, side * 128 : side * 128 + 128]
+                x_s[p * 2 + side] = block.astype(F32)
+            for side in range(2):
+                for k in range(2):
+                    res_s[side, pl.ds(sp * 4 + k * 2 + p, 64, stride=16), :] = x_s[
+                        p * 2 + side, pl.ds(branch * 2 + k, 64, stride=8), :
+                    ]
+        return 0
+
+    lax.fori_loop(0, 4, pick, 0)
+    for side in range(2):
+        resb_s[:, :, side * 128 : side * 128 + 128] = (
+            res_s[side].reshape(64, 16, 128).astype(BF16)
+        )
     values = pair_ref[...].astype(F32).reshape(rows * cols, width)
     normed = normalize(values).astype(BF16)
     res = dot(weight_ref[...], normed, TN)
     for i in range(rows):
         tile = res[:, i * cols : (i + 1) * cols].astype(BF16)
         block_s[:, :, i, :] = tile.reshape(4, 2, cols)
-    pl.semaphore_wait(barrier, 255)
-
-    def post(slot, _):
-        target = bias_s.at[z, :, x, y_lo, branch]
-
-        @pl.when(slot != mine)
-        def _():
-            remote(block_s.at[slot % 4], target, p_send.at[slot], p_recv.at[mine], to_plane(slot))
-
-        @pl.when(slot == mine)
-        def _():
-            pltpu.make_async_copy(block_s.at[branch], target, p_recv.at[mine]).start()
-
-        return 0
-
-    lax.fori_loop(0, 32, post, 0)
+    pl.semaphore_wait(barrier, 31 + 7)
+    for step in range(1, 8):
+        signal(ready, line(lax.rem(z + step, 8)))
+    for turn in range(1, 8):
+        other_z = z_turn(z, turn)
+        remote(block_s, line_s.at[:, z], z_send.at[turn], z_recv.at[z], line(other_z))
+    pltpu.make_async_copy(block_s, line_s.at[:, z], z_recv.at[z]).start()
     across = (lax.rem(branch + 2, 4), dap)
     partner = (branch // 2 * 2 + 1 - branch % 2, dap)
     far = lax.rem(branch + 2, 4)
@@ -219,14 +244,7 @@
     def project(sp, _):
         normed = []
         for p in range(2):
-            value = x_ref[sp * 2 + p].astype(F32)
-            for side in range(2):
-                x_s[side] = value[:, side * 128 : side * 128 + 128]
-                for k in range(2):
-                    res_s[side, pl.ds(sp * 4 + k * 2 + p, 64, stride=16), :] = x_s[
-                        side, pl.ds(branch * 2 + k, 64, stride=8), :
-                    ]
-            normed.append(normalize(value).astype(BF16))
+            normed.append(normalize(x_ref[sp * 2 + p].astype(F32)).astype(BF16))
         both = jnp.concatenate(normed, axis=1)
         projected = dot(both, wrow_ref[...])
         q_s[sp] = (projected[:, :128] * QUERY_SCALE).astype(BF16)
@@ -241,82 +259,79 @@
         return 0
 
     lax.fori_loop(0, 4, project, 0)
-    for side in range(2):
-        resb_s[:, :, side * 128 : side * 128 + 128] = (
-            res_s[side].reshape(64, 16, 128).astype(BF16)
-        )
-
-    def collect(slot, _):
-        arrived(bias_s.at[z, :, slot // 8, slot // 4 % 2, slot % 4], p_recv.at[slot])
+
+    for other_z in range(8):
+        arrived(line_s.at[:, other_z], z_recv.at[other_z])
+    odd = x % 2
+
+    def plane_turn(t):
+        return lax.rem(x + t // 2 * 2, 4) + t % 2 * (1 - 2 * odd)
+
+    def post(t, _):
+        other_x = plane_turn(t)
+        for step_y in range(2):
+            other_y = lax.rem(y_lo + step_y, 2)
+            for step in range(4):
+                other_b = lax.rem(branch + step, 4)
+                source, target = line_s.at[other_b], bias_s.at[x, y_lo, branch]
+                slot = other_x * 8 + other_y * 4 + other_b
+
+                def go():
+                    to = plane_device(other_x, other_y, other_b)
+                    remote(source, target, p_send.at[slot], p_recv.at[mine], to)
+
+                if step:
+                    go()
+                else:
+                    pl.when(slot != mine)(go)
         return 0
 
-    lax.fori_loop(0, 32, collect, 0)
-
-    def chunk(other_z, c):
-        return bias_s.at[other_z, c // 2, pl.ds(c % 2 * 2, 2)]
-
-    up, down = lax.rem(z + 1, 8), lax.rem(z + 7, 8)
-
-    def pass_up(t, c):
-        source = lax.rem(z + 8 - t, 8)
-        region = chunk(source, c)
-        remote(region, region, up_send.at[t, c], z_recv.at[source, c], line(up))
-
-    def pass_down(t, c):
-        source = lax.rem(z + t, 8)
-        region = chunk(source, c)
-        remote(region, region, down_send.at[t, c], z_recv.at[source, c], line(down))
-
-    for c in range(4):
-        pass_up(0, c)
-        pass_down(0, c)
-    for t in range(1, 4):
-        for c in range(4):
-            below, above = lax.rem(z + 8 - t, 8), lax.rem(z + t, 8)
-            arrived(chunk(below, c), z_recv.at[below, c])
-            if t < 3 or c < 2:
-                pass_up(t, c)
-            arrived(chunk(above, c), z_recv.at[above, c])
-            if t < 3 or c >= 2:
-                pass_down(t, c)
+    lax.fori_loop(0, 4, post, 0)
+    pltpu.make_async_copy(line_s.at[branch], bias_s.at[x, y_lo, branch], p_recv.at[mine]).start()
     arrived(wall_ref.at[far], w_recv.at[1])
     remote(wall_ref.at[far], wall_ref.at[far], w_send.at[2], w_recv.at[2], partner)
-
-    def post_res(slot, _):
-        target = resid_ref.at[dap]
-
-        @pl.when(slot != dap)
-        def _():
-            remote(resb_s.at[slot], target, res_send, res_recv, (branch, slot))
-
-        @pl.when(slot == dap)
-        def _():
-            pltpu.make_async_copy(resb_s.at[slot], target, res_recv).start()
-
-        return 0
-
-    lax.fori_loop(0, 64, post_res, 0)
-    opposite = lax.rem(z + 4, 8)
-    for c in range(4):
-        arrived(chunk(opposite, c), z_recv.at[opposite, c])
-
-    for xx in range(4):
+    pl.semaphore_wait(ready, 7)
+
+    def post_res(turn, _):
+        other_z = z_turn(z, turn)
+
+        def each(step_x, _):
+            other_x = lax.rem(x + step_x, 4)
+            for step_y in range(2):
+                other_d = other_x * 16 + other_z * 2 + lax.rem(y_lo + step_y, 2)
+
+                @pl.when(other_d != dap)
+                def _():
+                    source = resb_s.at[other_d]
+                    remote(source, resid_ref.at[dap], res_send, res_recv, (branch, other_d))
+
+            return 0
+
+        return lax.fori_loop(0, 4, each, 0)
+
+    lax.fori_loop(0, 8, post_res, 0)
+    pltpu.make_async_copy(resb_s.at[dap], resid_ref.at[dap], res_recv).start()
+
+    def step(t, _):
+        other_x = plane_turn(t)
+        span = pl.ds(pl.multiple_of(other_x * 128, 128), 128)
+        masks = [lane_block(n) for n in range(4)]
+
+        for slot in range(8):
+            landed = bias_s.at[other_x, slot // 4, slot % 4]
+            arrived(landed, p_recv.at[other_x * 8 + slot])
         for h in range(2):
             for b in range(4):
-                piece = bias_s[:, h, xx, :, b].astype(F32).reshape(128, 128)
-                wide_s[h, xx * 128 : xx * 128 + 128, b * 128 : b * 128 + 128] = piece * LOG2E
-
-    def step(t, _):
-        other_x = lax.rem(x + t, 4)
-        span = pl.ds(pl.multiple_of(other_x * 128, 128), 128)
-        masks = [lane_block(n) for n in range(4)]
+                sides = [bias_s[other_x, y, b, :, h].astype(F32) for y in range(2)]
+                piece = jnp.stack(sides, axis=1).reshape(128, 128)
+                wide_s[h, :, b * 128 : b * 128 + 128] = piece * LOG2E
 
         def some(u, _):
             for v in range(2):
                 sp = u * 2 + v
 
                 def extra(n):
-                    return wide_s[n % 2, span, :] + off_ref[sp, pl.ds(n // 2, 1), :]
+                    return wide_s[n % 2] + off_ref[sp, pl.ds(n // 2, 1), :]
 
                 out = attend_tile(q_s[sp, span, :], k_s[sp], rhs_s.at[sp], masks, extra)
                 o_s[v] = out * g_s[sp, span, :]
@@ -328,39 +343,34 @@
         base = other_x * 64
         out_s[pl.ds(base, 64)] = buf_s[...].reshape(64, 8, 128).astype(BF16)
 
-        def post_out(j, _):
-            slot = base + j
-
-            @pl.when(slot != me)
-            def _():
-                remote(out_s.at[slot], heads_ref.at[me], out_send, out_recv, device(slot))
-
-            @pl.when(slot == me)
-            def _():
-                pltpu.make_async_copy(out_s.at[slot], heads_ref.at[me], out_recv).start()
+        def post_out(turn, _):
+            for step_y in range(2):
+                other_d = other_x * 16 + z_turn(z, turn) * 2 + lax.rem(y_lo + step_y, 2)
+                for step in range(1, 4):
+                    other_b = lax.rem(branch + step, 4)
+                    source = out_s.at[other_d * 4 + other_b]
+                    remote(source, heads_ref.at[me], out_send, out_recv, (other_b, other_d))
+
+                @pl.when(other_d != dap)
+                def _():
+                    source = out_s.at[other_d * 4 + branch]
+                    remote(source, heads_ref.at[me], out_send, out_recv, (branch, other_d))
 
             return 0
 
-        lax.fori_loop(0, 64, post_out, 0)
+        lax.fori_loop(0, 8, post_out, 0)
+
+        @pl.when(t == 0)
+        def _():
+            pltpu.make_async_copy(out_s.at[me], heads_ref.at[me], out_recv).start()
+
         return 0
 
     lax.fori_loop(0, 4, step, 0)
 
-    for t in range(4):
-        for c in range(4):
-            if t < 3 or c < 2:
-                arrived(chunk(z, c), up_send.at[t, c])
-            if t < 3 or c >= 2:
-                arrived(chunk(z, c), down_send.at[t, c])
-
-    def drain(slot, _):
-        @pl.when(slot != mine)
-        def _():
-            arrived(block_s.at[0], p_send.at[slot])
-
-        return 0
-
-    lax.fori_loop(0, 32, drain, 0)
+    for turn in range(1, 8):
+        arrived(block_s, z_send.at[turn])
+    in_plane(lambda slot, *to: arrived(line_s.at[0], p_send.at[slot]))
     own.wait()
     for n in range(3):
         arrived(wcol_ref, w_send.at[n])
@@ -539,9 +549,11 @@
 
     partner = (y_hi * 2 + 1 - core, dap)
     far = lax.rem(branch + 2, 4)
-    for slot in range(4):
+    for step in range(4):
+        slot = lax.rem(y_hi * 2 + y_lo + step, 4)
         send(left_ref, l_s.at[x, branch], l_send.at[slot], l_recv.at[branch], to_left(slot))
-    for slot in range(8):
+    for turn in range(8):
+        slot = z_turn(z, turn)
         send(right_ref, r_s.at[z, core], r_send.at[slot], r_recv.at[z, core], to_right(slot))
 
     def rows_of(way, piece):
@@ -642,7 +654,8 @@
     lax.fori_loop(0, 4, contract, 0)
     update = dot(lhs_s[...].reshape(256, 4096), wide_s[...])
     send_s[...] = update.reshape(4, 8, 8, 512).astype(BF16)
-    for slot in range(4):
+    for step in range(4):
+        slot = lax.rem(x + step, 4)
         send(
             send_s.at[slot],
             pair_ref.at[y_hi * 2 + y_lo],
@@ -739,23 +752,24 @@
         ),
         scratch_shapes=[
             vmem((4, 2, 8, 128), BF16),
-            vmem((8, 2, 4, 2, 4, 8, 128), BF16),
-            vmem((2, SEQS, SEQS), F32),
+            vmem((4, 8, 2, 8, 128), BF16),
+            vmem((4, 2, 4, 8, 2, 8, 128), BF16),
+            vmem((2, 128, SEQS), F32),
             vmem((4, SEQS, 128), BF16),
             vmem((4, SEQS, 128), BF16),
             vmem((4, SEQS, 128), F32),
             vmem((4, 4 * SEQS, 256), BF16),
-            vmem((2, SEQS, 128), F32),
+            vmem((4, SEQS, 128), F32),
             vmem((2, 1024, 128), F32),
             vmem((64, 16, 256), BF16),
             vmem((2, 128, 128), F32),
             vmem((SEQS, 128), F32),
             vmem((256, 8, 128), BF16),
+            pltpu.SemaphoreType.REGULAR,
             dma((32,)),
             dma((32,)),
-            dma((4, 4)),
-            dma((4, 4)),
-            dma((8, 4)),
+            dma((8,)),
+            dma((8,)),
             dma((3,)),
             dma((4,)),
             dma,

time: 135 us -> 127 us (0.941); the launches traced: 133 us -> 127 us
  Pallas kernels: 113 us -> 106 us
    pallas_call x1, Pallas kernels: 62 us -> 53.1 us  [per_device(): pl.pallas_call(front_kernel, in_specs=[pl.BlockSpec(memory_space=vmem)] *...]
    pallas_call x1, Pallas kernels: 36.1 us -> 38.8 us  [per_device(): pl.pallas_call(outer_kernel, in_specs=[pl.BlockSpec(memory_space=vmem)] *...]
where the time goes in v4:
time: 127 us
  Pallas kernels  106 us (83%)
  local copies, waits for them, and re-layouts  14.4 us (11%)
  other arithmetic  4.66 us (4%)
    pallas_call x1, Pallas kernels, per_device(): pl.pallas_call(front_kernel, in_specs=[pl.BlockSpec(memory_space=vmem)] *...  53.1 us
    pallas_call x1, Pallas kernels, per_device(): pl.pallas_call(outer_kernel, in_specs=[pl.BlockSpec(memory_space=vmem)] *...  38.8 us
    pallas_call x1, Pallas kernels, per_device(): pl.pallas_call(column_kernel, grid=(2,), in_specs=[whole((64, 4, 8, 128))...  14.6 us
    transpose x1, local copies, waits for them, and re-layouts, per_device(): rows = jnp.transpose(gathered.reshape(4, 2, 2, 256, 256), (3, 2, 0, 1, 4))  3.75 us

profile of v4, /device:TPU:32, one launch (start us, length us, event | category | flops | bytes accessed | tf_op | source)
XLA Modules:
  0.0 126.6 jit_solution(607984109376600770)
XLA Ops:
  0.7 1.1 dynamic-slice_convert_fusion.2
  1.8 0.1 copy.26
  1.9 0.9 broadcast_in_dim.2.maskcol_ref
  2.8 0.6 reshape.69.maskrow_ref
  3.5 0.7 add_multiply_fusion
  4.2 0.6 reshape.62.off_ref
  4.8 1.0 fusion.6
  5.8 1.0 copy.31.wrow_ref
  6.8 0.8 copy.23.wcol_ref
  7.6 0.7 copy.22.weight_ref
  8.3 53.1 %row_attention.1 = (bf16[256,8,128]{2,1,0:T(8,128)(2,1)}, bf16[64,16,256]{2,1,0:T(8,128)(2,1)}, bf16[4,256,256]{2,1,0:T(8,128)(2,1)}) custom-call(bf16[8,128,128]{2,1,0:T(8,128)(2,1)} %pair_ref.1, bf16[128,8]{1,0:T(8,128)(2,1)} %copy.22.weight_ref, bf16[256,256]{1,0:T(8,128)(2,1)} %copy.23.wcol_ref, bf16[8,512,256]{2,1,0:T(8,128)(2,1)} %x_ref.1, ...), custom_call_target="tpu_custom_call" | custom-call | tf_op jit(solution)/shard_map/row_attention/pallas_call | solution.py:744
  61.4 1.3 %copy.24 = bf16[4,256,256]{1,2,0:T(8,128)(2,1)S(1)} copy(bf16[4,256,256]{2,1,0:T(8,128)(2,1)} %get-tuple-element.12) | data formatting | bytes 1048576 | tf_op jit(solution)/shard_map/row_attention/pallas_call | solution.py:744
  62.8 1.0 copy.27.wcol_ref
  63.8 0.8 fusion.5
  64.6 0.7 copy.28.wfac_ref
  65.4 14.6 %column_attention.1 = (bf16[2,512,256]{2,1,0:T(8,128)(2,1)}, bf16[2,32,512]{2,1,0:T(8,128)(2,1)}, bf16[2,32,512]{2,1,0:T(8,128)(2,1)}) custom-call(bf16[64,4,8,128]{3,2,1,0:T(8,128)(2,1)} %bitcast.36, bf16[64,16,256]{2,1,0:T(8,128)(2,1)} %get-tuple-element.11.res_ref, bf16[512,512]{1,0:T(8,128)(2,1)} %bitcast.29, bf16[256,1024]{1,0:T(8,128)(2,1)} %copy.27.wcol_ref, ...), custom_call_target="tpu_custom_call" | custom-call | tf_op jit(solution)/shard_map/column_attention/pallas_call | solution.py:787
  80.0 38.8 %outer_product.1 = (bf16[4,1024,256]{2,1,0:T(8,128)(2,1)}, bf16[4,8,8,512]{3,2,1,0:T(8,128)(2,1)}) custom-call(bf16[64,512]{1,0:T(8,128)(2,1)} %bitcast.42, bf16[64,512]{1,0:T(8,128)(2,1)} %bitcast.43, bf16[1024,256]{1,0:T(8,128)(2,1)} %bitcast.37, bf16[1024,128]{1,0:T(8,128)(2,1)} %weight_ref.2), custom_call_target="tpu_custom_call" | custom-call | tf_op jit(solution)/shard_map/outer_product/pallas_call | solution.py:831
  118.7 3.7 %copy.29 = bf16[256,2,4,2,256]{4,3,2,1,0:T(2,128)(2,1)S(1)} copy(bf16[256,2,4,2,256]{4,0,1,3,2:T(8,128)(2,1)} %bitcast.31) | data formatting | bytes 4194304 | tf_op jit(solution)/shard_map/transpose | solution.py:873
  122.5 2.2 %reshape.74 = bf16[512,8,256]{2,1,0:T(8,128)(2,1)} reshape(bf16[256,2,4,2,256]{4,3,2,1,0:T(2,128)(2,1)S(1)} %copy.29) | data formatting | bytes 4194304 | tf_op jit(solution)/shard_map/reshape | solution.py:874
  124.8 0.1 copy.30
  125.0 0.1 dynamic_slice.20
  125.1 0.3 fusion
  125.4 0.3 copy-done
  125.7 0.9 add_convert_fusion
  (21 shorter events, 0.2 us)
Async XLA Ops:
  0.6 6.2 %copy-start.4 = (bf16[4,256,64]{1,2,0:T(8,128)(2,1)S(1)}, bf16[4,256,64]{1,2,0:T(8,128)(2,1)}, u32[]{:S(2)}) copy-start(bf16[4,256,64]{1,2,0:T(8,128)(2,1)} %param.18) | copy-start | bytes 393220
  0.6 6.9 %copy-start.6 = (bf16[128,8]{0,1:T(8,128)(2,1)S(1)}, bf16[128,8]{0,1:T(8,128)(2,1)}, u32[]{:S(2)}) copy-start(bf16[128,8]{0,1:T(8,128)(2,1)} %param.15) | copy-start | bytes 6148
  61.4 2.4 %copy-start.3 = (bf16[256,256]{1,0:T(8,128)(2,1)S(1)}, bf16[256,256]{1,0:T(8,128)(2,1)}, u32[]{:S(2)}) copy-start(bf16[256,256]{1,0:T(8,128)(2,1)} %param.17) | copy-start | bytes 393220
  61.4 3.2 %copy-start.5 = (bf16[256,64]{0,1:T(8,128)(2,1)S(1)}, bf16[256,64]{0,1:T(8,128)(2,1)}, u32[]{:S(2)}) copy-start(bf16[256,64]{0,1:T(8,128)(2,1)} %param.20) | copy-start | bytes 98308
  122.5 2.2 %copy-start.2 = (bf16[4,8,8,512]{3,2,1,0:T(8,128)(2,1)S(1)}, bf16[4,8,8,512]{3,2,1,0:T(8,128)(2,1)}, u32[]{:S(2)}) copy-start(bf16[4,8,8,512]{3,2,1,0:T(8,128)(2,1)} %get-tuple-element.17) | copy-start | bytes 786436
  122.5 2.4 %copy-start.7 = (s32[512]{0:T(512)S(1)}, s32[512]{0:T(512)}, u32[]{:S(2)}) copy-start(s32[512]{0:T(512)} %param.14) | copy-start | bytes 6148
  122.5 2.6 %copy-start.1 = (s32[512,512]{1,0:T(8,128)S(1)}, s32[512,512]{1,0:T(8,128)}, u32[]{:S(2)}) copy-start(s32[512,512]{1,0:T(8,128)} %param.13) | copy-start | bytes 3145732
  124.7 0.9 copy-start

commit v5 on v4

--- a/solution.py
+++ b/solution.py
@@ -39,52 +39,6 @@
 def lane_block(index):
     lanes = lax.broadcasted_iota(jnp.int32, (1, 128), 1)
     return (lanes // HEAD == index).astype(F32).astype(BF16)
-
-
-def attend(q_s, k_s, g_s, rhs_s, o_s, bias_of, mask_of):
-    def run(stable):
-        def tile(step, extremes):
-            rows = pl.ds(pl.multiple_of(step * TILE, TILE), TILE)
-            q = q_s[rows, :]
-            total = None
-            for n in range(4):
-                scores = dot(q * lane_block(n), k_s[...], NT)
-                if bias_of is not None:
-                    scores = scores + bias_of(step, n)
-                if stable:
-                    scores = jnp.where(mask_of(n) > 0.0, scores, -1e30)
-                    scores = scores - jnp.max(scores, axis=1, keepdims=True)
-                raised = jnp.exp2(scores).astype(BF16)
-                part = dot(raised, rhs_s[n * SEQS : (n + 1) * SEQS, :])
-                total = part if total is None else total + part
-            sums = total[:, 128:]
-            o_s[rows, :] = total[:, :128] / sums * g_s[rows, :]
-            low, high = extremes
-            folded = sums.reshape(TILE // 8, 8, 128)
-            return jnp.minimum(low, jnp.min(folded, axis=0)), jnp.maximum(
-                high, jnp.max(folded, axis=0)
-            )
-
-        start = (jnp.full((8, 128), 1.0, F32), jnp.full((8, 128), 1.0, F32))
-        return lax.fori_loop(0, SEQS // TILE, tile, start)
-
-    low, high = run(False)
-    fine = jnp.logical_and(jnp.min(low) > 1e-30, jnp.max(high) < 1e30)
-
-    @pl.when(jnp.logical_not(fine))
-    def _():
-        run(True)
-
-
-def fill_values(rhs_s, values, mask):
-    masked = values * mask
-    for n in range(4):
-        rhs_s[n * SEQS : (n + 1) * SEQS, :128] = masked * lane_block(n)
-
-
-def fill_ones(rhs_s, mask):
-    for n in range(4):
-        rhs_s[n * SEQS : (n + 1) * SEQS, 128:] = mask * lane_block(n)
 
 
 def place():
@@ -382,18 +336,17 @@
     arrived(heads_ref, out_recv)
 
 
-def column_kernel(
+def back_kernel(
     a_ref,
     res_ref,
     wrow_ref,
     wcol_ref,
     wout_ref,
     wfac_ref,
-    maskcol_ref,
-    maskrow_ref,
-    upd_ref,
-    left_ref,
-    right_ref,
+    mask_ref,
+    weight_ref,
+    gather_ref,
+    pair_ref,
     x_s,
     res_s,
     msa_s,
@@ -402,66 +355,10 @@
     k_s,
     g_s,
     rhs_s,
-    o_s,
     heads_s,
-):
-    k = pl.program_id(0)
-
-    @pl.when(k == 0)
-    def _():
-        pieces = [a_ref[:, b].astype(F32).reshape(SEQS, 128).astype(BF16) for b in range(4)]
-        x = dot(jnp.concatenate(pieces, axis=1), wrow_ref[...])
-        for j in range(4):
-            x_s[j] = x[:, j * 128 : (j + 1) * 128]
-        for side in range(2):
-            block = res_ref[:, :, side * 128 : side * 128 + 128].astype(F32)
-            res_s[side] = block.reshape(1024, 128)
-
-    mine = [x_s[j, pl.ds(k, 256, stride=2), :] for j in range(4)]
-    rows = jnp.concatenate(
-        [jnp.concatenate(mine[:2], axis=1), jnp.concatenate(mine[2:], axis=1)], axis=0
-    )
-    base = jnp.concatenate(
-        [
-            jnp.concatenate(
-                [res_s[side, pl.ds(k * 2 + p, 256, stride=4), :] for side in range(2)], axis=1
-            )
-            for p in range(2)
-        ],
-        axis=0,
-    )
-    msa = (rows + base).astype(BF16).astype(F32)
-    msa_s[...] = msa
-    n_s[...] = normalize(msa).astype(BF16)
-    fill_ones(rhs_s, maskcol_ref[0])
-    for group in range(2):
-        lanes = slice(group * 128, group * 128 + 128)
-
-        def project(part):
-            at = part * 256 + group * 128
-            return dot(n_s[...], wcol_ref[:, at : at + 128])
-
-        q_s[...] = (project(0) * QUERY_SCALE).astype(BF16)
-        k_s[...] = project(1).astype(BF16)
-        fill_values(rhs_s, project(2).astype(BF16), maskcol_ref[0])
-        g_s[...] = jax.nn.sigmoid(project(3))
-        attend(q_s, k_s, g_s, rhs_s, o_s, None, lambda n: maskrow_ref[0])
-        heads_s[:, lanes] = o_s[...].astype(BF16)
-    updated = (msa_s[...] + dot(heads_s[...], wout_ref[...])).astype(BF16)
-    upd_ref[0] = updated
-    outer = normalize(updated.astype(F32)).astype(BF16)
-    factors = dot(wfac_ref[...], outer, TN) * maskrow_ref[0]
-    left_ref[0] = factors[:FACTOR].astype(BF16)
-    right_ref[0] = factors[FACTOR:].astype(BF16)
-
-
-def outer_kernel(
-    left_ref,
-    right_ref,
-    upd_ref,
-    weight_ref,
-    gather_ref,
-    pair_ref,
+    left_s,
+    right_s,
+    upd_s,
     l_s,
     lp_s,
     r_s,
@@ -481,6 +378,9 @@
     f_recv,
     u_send,
     u_recv,
+    g_send,
+    g_recv,
+    own_sem,
     p_send,
     p_recv,
 ):
@@ -489,28 +389,24 @@
     x, z, y_lo = at["x"], at["z"], at["y_lo"]
     barrier = pltpu.get_barrier_semaphore()
 
-    def greet(index, _):
-        to = (index // 8, (index // 2) % 4 * 16 + z * 2 + index % 2)
-
-        @pl.when(jnp.logical_or(to[0] != branch, to[1] != dap))
-        def _():
-            signal(barrier, to)
+    def greet(step_x, _):
+        other_x = lax.rem(x + step_x, 4)
+        for step_y in range(2):
+            other_d = other_x * 16 + z * 2 + lax.rem(y_lo + step_y, 2)
+            for step in range(1, 4):
+                signal(barrier, (lax.rem(branch + step, 4), other_d))
+
+            @pl.when(other_d != dap)
+            def _():
+                signal(barrier, (branch, other_d))
 
         return 0
 
-    lax.fori_loop(0, 32, greet, 0)
-
-    def greet_line(index, _):
-        other_z = index // 2
-
-        @pl.when(other_z != z)
-        def _():
-            signal(barrier, (y_hi * 2 + index % 2, x * 16 + other_z * 2 + y_lo))
-
-        return 0
-
-    lax.fori_loop(0, 16, greet_line, 0)
-    pl.semaphore_wait(barrier, 31 + 14)
+    lax.fori_loop(0, 4, greet, 0)
+    for step in range(1, 8):
+        other_z = lax.rem(z + step, 8)
+        for other_core in range(2):
+            signal(barrier, (y_hi * 2 + other_core, x * 16 + other_z * 2 + y_lo))
 
     def elsewhere(to):
         return jnp.logical_or(to[0] != branch, to[1] != dap)
@@ -549,29 +445,154 @@
 
     partner = (y_hi * 2 + 1 - core, dap)
     far = lax.rem(branch + 2, 4)
-    for step in range(4):
-        slot = lax.rem(y_hi * 2 + y_lo + step, 4)
-        send(left_ref, l_s.at[x, branch], l_send.at[slot], l_recv.at[branch], to_left(slot))
-    for turn in range(8):
-        slot = z_turn(z, turn)
-        send(right_ref, r_s.at[z, core], r_send.at[slot], r_recv.at[z, core], to_right(slot))
-
-    def rows_of(way, piece):
-        return pl.ds(way * 512 + piece * 256, 256)
-
+    above, below = lax.rem(x + 1, 4), lax.rem(x + 3, 4)
+    opposite = lax.rem(x + 2, 4)
     steps = (1, 3)
-    for piece in range(2):
+
+    def part(way):
+        return pl.ds(way * 256, 256)
+
+    def half(other_x, h, k):
+        return l_s.at[other_x, pl.ds(h * 2, 2), k]
+
+    def pass_x(origin, h, k, send_sem, to):
+        region = half(origin, h, k)
+        remote(region, region, send_sem, x_recv.at[k, origin, h], x_line(to))
+
+    def first(k):
+        for step in range(4):
+            slot = lax.rem(y_hi * 2 + y_lo + step, 4)
+            send(
+                left_s.at[k],
+                l_s.at[x, branch, k],
+                l_send.at[k, slot],
+                l_recv.at[k, branch],
+                to_left(slot),
+            )
+        for turn in range(8):
+            slot = z_turn(z, turn)
+            send(
+                right_s.at[k],
+                r_s.at[z, core, k],
+                r_send.at[k, slot],
+                r_recv.at[k, z],
+                to_right(slot),
+            )
         for way in range(2):
             remote(
-                upd_ref.at[rows_of(way, piece)],
-                relay_s.at[way, piece],
-                u_send.at[0, way, piece],
-                u_recv.at[0, way, piece],
+                upd_s.at[k, part(way)],
+                relay_s.at[way, k],
+                u_send.at[0, way, k],
+                u_recv.at[0, way, k],
                 y_line(steps[way]),
             )
-    remote(upd_ref, gather_ref.at[branch], u_send.at[3, 0, 0], u_recv.at[3, 0, 0], partner)
-    own = pltpu.make_async_copy(upd_ref, gather_ref.at[branch], u_recv.at[3, 0, 1])
-    own.start()
+        remote(upd_s.at[k], gather_ref.at[branch, k], g_send.at[k], g_recv.at[k], partner)
+        pltpu.make_async_copy(upd_s.at[k], gather_ref.at[branch, k], own_sem.at[k]).start()
+
+    def second(k):
+        for slot in range(4):
+            arrived(l_s.at[x, slot, k], l_recv.at[k, slot])
+        for h in range(2):
+            pass_x(x, h, k, up_send.at[k, h], above)
+            pass_x(x, 1 - h, k, down_send.at[k, 1 - h], below)
+        for way in range(2):
+            region = relay_s.at[way, k]
+            arrived(region, u_recv.at[0, way, k])
+            to = y_line(steps[way])
+            remote(
+                region,
+                gather_ref.at[lax.rem(to[0] + 2, 4), k, part(way)],
+                u_send.at[1, way, k],
+                u_recv.at[1, way, k],
+                to,
+            )
+
+    def third(k):
+        for slot in range(8):
+            region = r_s.at[slot, core, k]
+            arrived(region, r_recv.at[k, slot])
+            remote(region, region, f_send.at[k, slot], f_recv.at[k, slot], partner)
+        arrived(half(below, 0, k), x_recv.at[k, below, 0])
+        pass_x(below, 0, k, up_send.at[k, 2], above)
+        arrived(half(above, 1, k), x_recv.at[k, above, 1])
+        pass_x(above, 1, k, down_send.at[k, 2], below)
+
+    def fourth(k):
+        for way in range(2):
+            region = gather_ref.at[far, k, part(way)]
+            arrived(region, u_recv.at[1, way, k])
+            remote(region, region, u_send.at[2, way, k], u_recv.at[2, way, k], partner)
+
+    pieces = [a_ref[:, b].astype(F32).reshape(SEQS, 128).astype(BF16) for b in range(4)]
+    moved = dot(jnp.concatenate(pieces, axis=1), wrow_ref[...])
+    for j in range(4):
+        x_s[j] = moved[:, j * 128 : (j + 1) * 128]
+    for side in range(2):
+        block = res_ref[:, :, side * 128 : side * 128 + 128].astype(F32)
+        res_s[side] = block.reshape(1024, 128)
+    for group in range(2):
+        for n in range(4):
+            rhs_s[group, n * SEQS : (n + 1) * SEQS, 128:] = jnp.broadcast_to(
+                lane_block(n), (SEQS, 128)
+            )
+
+    for k in range(2):
+        mine = [x_s[j, pl.ds(k, 256, stride=2), :] for j in range(4)]
+        rows = jnp.concatenate(
+            [jnp.concatenate(mine[:2], axis=1), jnp.concatenate(mine[2:], axis=1)], axis=0
+        )
+        base = jnp.concatenate(
+            [
+                jnp.concatenate(
+                    [res_s[side, pl.ds(k * 2 + p, 256, stride=4), :] for side in range(2)], axis=1
+                )
+                for p in range(2)
+            ],
+            axis=0,
+        )
+        msa = (rows + base).astype(BF16).astype(F32)
+        msa_s[...] = msa
+        n_s[...] = normalize(msa).astype(BF16)
+        for group in range(2):
+
+            def project(part_index):
+                start = part_index * 256 + group * 128
+                return dot(n_s[...], wcol_ref[:, start : start + 128])
+
+            q_s[group] = (project(0) * QUERY_SCALE).astype(BF16)
+            k_s[group] = project(1).astype(BF16)
+            values = project(2).astype(BF16)
+            g_s[group] = jax.nn.sigmoid(project(3))
+            for n in range(4):
+                rhs_s[group, n * SEQS : (n + 1) * SEQS, :128] = values * lane_block(n)
+        offset = (mask_ref[k] - 1.0) * 1e30
+
+        def tile(t, _):
+            span = pl.ds(pl.multiple_of(t * 128, 128), 128)
+            masks = [lane_block(n) for n in range(4)]
+            for group in range(2):
+                out = attend_tile(
+                    q_s[group, span, :], k_s[group], rhs_s.at[group], masks, lambda n: offset
+                )
+                heads_s[span, group * 128 : group * 128 + 128] = (
+                    out * g_s[group, span, :]
+                ).astype(BF16)
+            if k == 1:
+                pl.when(t == 0)(lambda: second(0))
+                pl.when(t == 2)(lambda: third(0))
+                pl.when(t == 3)(lambda: fourth(0))
+            return 0
+
+        lax.fori_loop(0, 4, tile, 0)
+        updated = (msa_s[...] + dot(heads_s[...], wout_ref[...])).astype(BF16)
+        upd_s[k] = updated
+        outer = normalize(updated.astype(F32)).astype(BF16)
+        factors = dot(wfac_ref[...], outer, TN) * mask_ref[k]
+        left_s[k] = factors[:FACTOR].astype(BF16)
+        right_s[k] = factors[FACTOR:].astype(BF16)
+        if k == 0:
+            pl.semaphore_wait(barrier, 31 + 14)
+        first(k)
 
     wide_s[...] = jnp.zeros_like(wide_s)
 
@@ -583,6 +604,7 @@
         return 0
 
     lax.fori_loop(0, 32, widen, 0)
+    second(1)
 
     def permute(c, _):
         source = lax.broadcasted_iota(jnp.int32, (32, 1024), 1)
@@ -592,54 +614,17 @@
         return 0
 
     lax.fori_loop(0, 32, permute, 0)
-
-    above, below = lax.rem(x + 1, 4), lax.rem(x + 3, 4)
-
-    def half(other_x, h):
-        return l_s.at[other_x, pl.ds(h * 2, 2)]
-
-    def pass_x(origin, h, send_sem, to):
-        region = half(origin, h)
-        remote(region, region, send_sem, x_recv.at[origin, h], x_line(to))
-
-    for slot in range(4):
-        arrived(l_s.at[x, slot], l_recv.at[slot])
-    for h in range(2):
-        pass_x(x, h, up_send.at[h], above)
-        pass_x(x, 1 - h, down_send.at[1 - h], below)
-
-    def relay(way, piece):
-        region = relay_s.at[way, piece]
-        arrived(region, u_recv.at[0, way, piece])
-        to = y_line(steps[way])
-        remote(
-            region,
-            gather_ref.at[lax.rem(to[0] + 2, 4), rows_of(way, piece)],
-            u_send.at[1, way, piece],
-            u_recv.at[1, way, piece],
-            to,
-        )
-
-    for way in range(2):
-        relay(way, 0)
-    for slot in range(8):
-        arrived(r_s.at[slot, core], r_recv.at[slot, core])
-        remote(r_s.at[slot, core], r_s.at[slot, core], f_send.at[slot], f_recv.at[slot], partner)
-    arrived(half(below, 0), x_recv.at[below, 0])
-    pass_x(below, 0, up_send.at[2], above)
-    arrived(half(above, 1), x_recv.at[above, 1])
-    pass_x(above, 1, down_send.at[2], below)
-    for way in range(2):
-        relay(way, 1)
-    arrived(half(below, 1), x_recv.at[below, 1])
-    arrived(half(above, 0), x_recv.at[above, 0])
-    opposite = lax.rem(x + 2, 4)
-    for h in range(2):
-        arrived(half(opposite, h), x_recv.at[opposite, h])
-    lefts = l_s[...].reshape(1024, SEQS)
-    lp_s[...] = dot(perm_s[...], lefts).astype(BF16)
-    for slot in range(8):
-        arrived(r_s.at[slot, 1 - core], f_recv.at[slot])
+    third(1)
+    for k in range(2):
+        arrived(half(below, 1, k), x_recv.at[k, below, 1])
+        arrived(half(above, 0, k), x_recv.at[k, above, 0])
+        for h in range(2):
+            arrived(half(opposite, h, k), x_recv.at[k, opposite, h])
+    lp_s[...] = dot(perm_s[...], l_s[...].reshape(1024, SEQS)).astype(BF16)
+    for k in range(2):
+        for slot in range(8):
+            arrived(r_s.at[slot, 1 - core, k], f_recv.at[k, slot])
+    fourth(1)
 
     def contract(jc, _):
         rights = r_s[pl.ds(jc * 2, 2)].reshape(256, SEQS)
@@ -663,29 +648,24 @@
             p_recv.at[y_hi * 2 + y_lo],
             to_pair(slot),
         )
-    for piece in range(2):
+    for k in range(2):
+        for slot in range(8):
+            sent(right_s.at[k], r_send.at[k, slot], to_right(slot))
+            arrived(right_s.at[k], f_send.at[k, slot])
+        for slot in range(4):
+            sent(left_s.at[k], l_send.at[k, slot], to_left(slot))
+        for n in range(3):
+            arrived(half(x, 0, k), up_send.at[k, n])
+            arrived(half(x, 0, k), down_send.at[k, n])
         for way in range(2):
-            region = gather_ref.at[far, rows_of(way, piece)]
-            arrived(region, u_recv.at[1, way, piece])
-            remote(region, region, u_send.at[2, way, piece], u_recv.at[2, way, piece], partner)
-    for slot in range(8):
-        sent(right_ref, r_send.at[slot], to_right(slot))
-        arrived(right_ref, f_send.at[slot])
+            for stage in range(3):
+                arrived(relay_s.at[way, k], u_send.at[stage, way, k])
+            arrived(relay_s.at[way, k], u_recv.at[2, way, k])
+        arrived(upd_s.at[k], g_send.at[k])
+        arrived(upd_s.at[k], g_recv.at[k])
+        arrived(upd_s.at[k], own_sem.at[k])
     for slot in range(4):
-        sent(left_ref, l_send.at[slot], to_left(slot))
         sent(send_s.at[slot], p_send.at[slot], to_pair(slot))
-    for n in range(3):
-        arrived(half(x, 0), up_send.at[n])
-        arrived(half(x, 0), down_send.at[n])
-    for way in range(2):
-        for piece in range(2):
-            for stage in range(3):
-                arrived(relay_s.at[way, piece], u_send.at[stage, way, piece])
-            arrived(relay_s.at[way, piece], u_recv.at[2, way, piece])
-    arrived(upd_ref, u_send.at[3, 0, 0])
-    arrived(upd_ref, u_recv.at[3, 0, 0])
-    own.wait()
-    for slot in range(4):
         arrived(pair_ref.at[slot], p_recv.at[slot])
 
 
@@ -709,7 +689,6 @@
     branch = lax.axis_index("branch")
     dap = lax.axis_index("dap")
     vmem = pltpu.VMEM
-    params = pltpu.CompilerParams(vmem_limit_bytes=VMEM_LIMIT)
 
     dma = pltpu.SemaphoreType.DMA
     half = jnp.transpose(row_proj_weight, (1, 0, 2))
@@ -732,15 +711,6 @@
     wcol_mine = jnp.transpose(column_proj_weight, (1, 0, 2)).reshape(256, 256)
     res_mask = lax.dynamic_slice_in_dim(align_mask, dap * 8 + branch * 2, 2, 1).astype(F32)
     res_mask = jnp.transpose(res_mask.reshape(256, 2, 2), (2, 1, 0)).reshape(2, 1, SEQS)
-    col_maskcol = jnp.broadcast_to(res_mask.reshape(2, SEQS, 1), (2, SEQS, 128)).astype(BF16)
-
-    attend_scratch = [
-        vmem((SEQS, 128), BF16),
-        vmem((SEQS, 128), BF16),
-        vmem((SEQS, 128), F32),
-        vmem((4 * SEQS, 256), BF16),
-        vmem((SEQS, 128), F32),
-    ]
     got, residual, wcol = pl.pallas_call(
         front_kernel,
         in_specs=[pl.BlockSpec(memory_space=vmem)] * 6,
@@ -784,39 +754,56 @@
     )(pair_rep, bias_weight, wcol_mine, alignment, wrow, offset)
     wcol = jnp.transpose(wcol.reshape(4, 256, 4, 64), (1, 2, 0, 3)).reshape(256, 1024)
 
-    updated, left, right = pl.pallas_call(
-        column_kernel,
-        grid=(2,),
-        in_specs=[
-            whole((64, 4, 8, 128)),
-            whole((64, 16, 256)),
-            whole((512, 512)),
-            whole((256, 1024)),
-            whole((256, 256)),
-            whole((256, 64)),
-            pl.BlockSpec((1, SEQS, 128), lambda i: (i, 0, 0)),
-            pl.BlockSpec((1, 1, SEQS), lambda i: (i, 0, 0)),
-        ],
-        out_specs=(
-            pl.BlockSpec((1, SEQS, 256), lambda i: (i, 0, 0)),
-            pl.BlockSpec((1, FACTOR, SEQS), lambda i: (i, 0, 0)),
-            pl.BlockSpec((1, FACTOR, SEQS), lambda i: (i, 0, 0)),
-        ),
+    gathered, pairs = pl.pallas_call(
+        back_kernel,
+        in_specs=[pl.BlockSpec(memory_space=vmem)] * 8,
+        out_specs=(pl.BlockSpec(memory_space=vmem),) * 2,
         out_shape=(
-            jax.ShapeDtypeStruct((2, SEQS, 256), BF16),
-            jax.ShapeDtypeStruct((2, FACTOR, SEQS), BF16),
-            jax.ShapeDtypeStruct((2, FACTOR, SEQS), BF16),
+            jax.ShapeDtypeStruct((4, 2, SEQS, 256), BF16),
+            jax.ShapeDtypeStruct((4, 8, 8, 512), BF16),
         ),
         scratch_shapes=[
             vmem((4, SEQS, 128), F32),
             vmem((2, 1024, 128), F32),
             vmem((SEQS, 256), F32),
             vmem((SEQS, 256), BF16),
-        ]
-        + attend_scratch
-        + [vmem((SEQS, 256), BF16)],
-        compiler_params=params,
-        name="column_attention",
+            vmem((2, SEQS, 128), BF16),
+            vmem((2, SEQS, 128), BF16),
+            vmem((2, SEQS, 128), F32),
+            vmem((2, 4 * SEQS, 256), BF16),
+            vmem((SEQS, 256), BF16),
+            vmem((2, FACTOR, SEQS), BF16),
+            vmem((2, FACTOR, SEQS), BF16),
+            vmem((2, SEQS, 256), BF16),
+            vmem((4, 4, 2, FACTOR, SEQS), BF16),
+            vmem((1024, SEQS), BF16),
+            vmem((8, 2, 2, FACTOR, SEQS), BF16),
+            vmem((1024, 1024), BF16),
+            vmem((4096, 512), BF16),
+            vmem((4, 4, 16, 4096), BF16),
+            vmem((4, 8, 8, 512), BF16),
+            vmem((2, 2, 256, 256), BF16),
+            dma((2, 4)),
+            dma((2, 4)),
+            dma((2, 3)),
+            dma((2, 3)),
+            dma((2, 4, 2)),
+            dma((2, 8)),
+            dma((2, 8)),
+            dma((2, 8)),
+            dma((2, 8)),
+            dma((3, 2, 2)),
+            dma((3, 2, 2)),
+            dma((2,)),
+            dma((2,)),
+            dma((2,)),
+            dma((4,)),
+            dma((4,)),
+        ],
+        compiler_params=pltpu.CompilerParams(
+            vmem_limit_bytes=VMEM_LIMIT, collective_id=0, has_side_effects=True
+        ),
+        name="column_outer",
     )(
         got.reshape(64, 4, 8, 128),
         residual,
@@ -824,49 +811,7 @@
         wcol,
         column_out_weight,
         outer_factor_weight,
-        col_maskcol,
         res_mask,
-    )
-
-    gathered, pairs = pl.pallas_call(
-        outer_kernel,
-        in_specs=[pl.BlockSpec(memory_space=vmem)] * 4,
-        out_specs=(pl.BlockSpec(memory_space=vmem),) * 2,
-        out_shape=(
-            jax.ShapeDtypeStruct((4, 2 * SEQS, 256), BF16),
-            jax.ShapeDtypeStruct((4, 8, 8, 512), BF16),
-        ),
-        scratch_shapes=[
-            vmem((4, 4, 64, SEQS), BF16),
-            vmem((1024, SEQS), BF16),
-            vmem((8, 2, 64, SEQS), BF16),
-            vmem((1024, 1024), BF16),
-            vmem((4096, 512), BF16),
-            vmem((4, 4, 16, 4096), BF16),
-            vmem((4, 8, 8, 512), BF16),
-            vmem((2, 2, 256, 256), BF16),
-            dma((4,)),
-            dma((4,)),
-            dma((3,)),
-            dma((3,)),
-            dma((4, 2)),
-            dma((8,)),
-            dma((8, 2)),
-            dma((8,)),
-            dma((8,)),
-            dma((4, 2, 2)),
-            dma((4, 2, 2)),
-            dma((4,)),
-            dma((4,)),
-        ],
-        compiler_params=pltpu.CompilerParams(
-            vmem_limit_bytes=VMEM_LIMIT, collective_id=0, has_side_effects=True
-        ),
-        name="outer_product",
-    )(
-        left.reshape(2 * FACTOR, SEQS),
-        right.reshape(2 * FACTOR, SEQS),
-        updated.reshape(2 * SEQS, 256),
         outer_out,
     )
 

time: 127 us -> 122 us (0.961); the launches traced: 127 us -> 120 us
  Pallas kernels: 106 us -> 100 us
    pallas_call x2 -> x1, Pallas kernels: 53.4 us -> 47.3 us  [per_device(): pl.pallas_call(back_kernel, in_specs=[pl.BlockSpec(memory_space=vmem)] *...]
where the time goes in v5:
time: 122 us; the launch traced here: 120 us
  Pallas kernels  100 us (82%)
  local copies, waits for them, and re-layouts  13.2 us (11%)
  other arithmetic  5.63 us (5%)
    pallas_call x1, Pallas kernels, per_device(): pl.pallas_call(front_kernel, in_specs=[pl.BlockSpec(memory_space=vmem)] *...  53.1 us
    pallas_call x1, Pallas kernels, per_device(): pl.pallas_call(back_kernel, in_specs=[pl.BlockSpec(memory_space=vmem)] *...  47.3 us
    transpose x1, local copies, waits for them, and re-layouts, per_device(): rows = jnp.transpose(gathered.reshape(4, 2, 2, 256, 256), (3, 2, 0, 1, 4))  3.75 us

profile of v5, /device:TPU:32, one launch (start us, length us, event | category | flops | bytes accessed | tf_op | source)
XLA Modules:
  0.0 120.3 jit_solution(11008637713424285707)
XLA Ops:
  0.7 1.1 dynamic-slice_convert_fusion.2
  1.8 0.1 copy.26
  1.9 0.6 reshape.58.mask_ref
  2.5 0.7 add_multiply_fusion
  3.2 0.6 reshape.51.off_ref
  3.9 1.0 fusion.6
  4.9 1.0 copy.31.wrow_ref
  5.9 0.8 copy.23.wcol_ref
  6.7 0.7 copy.22.weight_ref
  7.4 53.1 %row_attention.1 = (bf16[256,8,128]{2,1,0:T(8,128)(2,1)}, bf16[64,16,256]{2,1,0:T(8,128)(2,1)}, bf16[4,256,256]{2,1,0:T(8,128)(2,1)}) custom-call(bf16[8,128,128]{2,1,0:T(8,128)(2,1)} %pair_ref.1, bf16[128,8]{1,0:T(8,128)(2,1)} %copy.22.weight_ref, bf16[256,256]{1,0:T(8,128)(2,1)} %copy.23.wcol_ref, bf16[8,512,256]{2,1,0:T(8,128)(2,1)} %x_ref.1, ...), custom_call_target="tpu_custom_call" | custom-call | tf_op jit(solution)/shard_map/row_attention/pallas_call | solution.py:714
  60.5 0.0 copy-start.2
  60.5 1.3 %copy.24 = bf16[4,256,256]{1,2,0:T(8,128)(2,1)S(1)} copy(bf16[4,256,256]{2,1,0:T(8,128)(2,1)} %get-tuple-element.9) | data formatting | bytes 1048576 | tf_op jit(solution)/shard_map/row_attention/pallas_call | solution.py:714
  61.9 1.0 copy.27.wcol_ref
  62.9 0.8 fusion.5
  63.7 0.7 copy.28.wfac_ref
  64.5 47.3 %column_outer.1 = (bf16[4,2,512,256]{3,2,1,0:T(8,128)(2,1)}, bf16[4,8,8,512]{3,2,1,0:T(8,128)(2,1)}) custom-call(bf16[64,4,8,128]{3,2,1,0:T(8,128)(2,1)} %bitcast.29, bf16[64,16,256]{2,1,0:T(8,128)(2,1)} %get-tuple-element.8.res_ref, bf16[512,512]{1,0:T(8,128)(2,1)} %bitcast.22, bf16[256,1024]{1,0:T(8,128)(2,1)} %copy.27.wcol_ref, ...), custom_call_target="tpu_custom_call" | custom-call | tf_op jit(solution)/shard_map/column_outer/pallas_call | solution.py:757
  111.7 1.0 convert_bitcast_fusion
  112.8 0.1 copy.30
  112.9 0.1 dynamic_slice.20
  113.0 0.1 dynamic_slice.21
  113.1 0.3 fusion
  113.4 0.9 add_convert_fusion
  114.3 3.7 %copy.29 = bf16[256,2,4,2,256]{4,3,2,1,0:T(2,128)(2,1)S(1)} copy(bf16[256,2,4,2,256]{4,0,1,3,2:T(8,128)(2,1)} %bitcast.24) | data formatting | bytes 4194304 | tf_op jit(solution)/shard_map/transpose | solution.py:818
  118.0 2.2 %reshape.60 = bf16[512,8,256]{2,1,0:T(8,128)(2,1)} reshape(bf16[256,2,4,2,256]{4,3,2,1,0:T(2,128)(2,1)S(1)} %copy.29) | data formatting | bytes 4194304 | tf_op jit(solution)/shard_map/reshape | solution.py:819
  (15 shorter events, 0.1 us)
Async XLA Ops:
  0.6 5.3 %copy-start.3 = (bf16[4,256,64]{1,2,0:T(8,128)(2,1)S(1)}, bf16[4,256,64]{1,2,0:T(8,128)(2,1)}, u32[]{:S(2)}) copy-start(bf16[4,256,64]{1,2,0:T(8,128)(2,1)} %param.18) | copy-start | bytes 393220
  0.6 6.0 %copy-start.5 = (bf16[128,8]{0,1:T(8,128)(2,1)S(1)}, bf16[128,8]{0,1:T(8,128)(2,1)}, u32[]{:S(2)}) copy-start(bf16[128,8]{0,1:T(8,128)(2,1)} %param.15) | copy-start | bytes 6148
  60.5 2.4 %copy-start.2 = (bf16[256,256]{1,0:T(8,128)(2,1)S(1)}, bf16[256,256]{1,0:T(8,128)(2,1)}, u32[]{:S(2)}) copy-start(bf16[256,256]{1,0:T(8,128)(2,1)} %param.17) | copy-start | bytes 393220
  60.5 3.2 %copy-start.4 = (bf16[256,64]{0,1:T(8,128)(2,1)S(1)}, bf16[256,64]{0,1:T(8,128)(2,1)}, u32[]{:S(2)}) copy-start(bf16[256,64]{0,1:T(8,128)(2,1)} %param.20) | copy-start | bytes 98308
  64.5 48.4 %copy-start.6 = (s32[512]{0:T(512)S(1)}, s32[512]{0:T(512)}, u32[]{:S(2)}) copy-start(s32[512]{0:T(512)} %param.14) | copy-start | bytes 6148
  64.5 48.6 %copy-start.1 = (s32[512,512]{1,0:T(8,128)S(1)}, s32[512,512]{1,0:T(8,128)}, u32[]{:S(2)}) copy-start(s32[512,512]{1,0:T(8,128)} %param.13) | copy-start | bytes 3145732
  64.5 48.9 %copy-start = (bf16[8,128,128]{2,1,0:T(8,128)(2,1)S(1)}, bf16[8,128,128]{2,1,0:T(8,128)(2,1)}, u32[]{:S(2)}) copy-start(bf16[8,128,128]{2,1,0:T(8,128)(2,1)} %pair_ref.1) | copy-start | bytes 786436

commit v6 on v5

--- a/solution.py
+++ b/solution.py
@@ -86,13 +86,17 @@
     return total[:, :128] / total[:, 128:]
 
 
+def beside(first, second):
+    return jnp.concatenate([first.astype(F32), second.astype(F32)], axis=1).astype(BF16)
+
+
 def front_kernel(
     pair_ref,
     weight_ref,
-    wcol_ref,
+    column_ref,
     x_ref,
-    wrow_ref,
-    off_ref,
+    row_ref,
+    mask_ref,
     heads_ref,
     resid_ref,
     wall_ref,
@@ -110,6 +114,11 @@
     o_s,
     buf_s,
     out_s,
+    wcol_ref,
+    wrow_ref,
+    mask_s,
+    off_ref,
+    mask_sem,
     ready,
     p_send,
     p_recv,
@@ -156,6 +165,16 @@
         signal(barrier, line(lax.rem(z + step, 8)))
 
     rows, cols, width = pair_ref.shape
+    mask_rows = mask_ref.at[pl.ds(pl.multiple_of(dap * 8, 8), 8)]
+    fetch = pltpu.make_async_copy(mask_rows, mask_s, mask_sem)
+    fetch.start()
+    empty = jnp.zeros((256, 64), BF16)
+    for t in range(4):
+        lanes = slice(t * 128, t * 128 + 128)
+        wrow_ref[:256, lanes] = beside(row_ref[t], empty)
+        wrow_ref[256:, lanes] = beside(empty, row_ref[t])
+    for t in range(2):
+        wcol_ref[t] = beside(column_ref[2 * t], column_ref[2 * t + 1])
 
     def pick(sp, _):
         for p in range(2):
@@ -174,6 +193,8 @@
         resb_s[:, :, side * 128 : side * 128 + 128] = (
             res_s[side].reshape(64, 16, 128).astype(BF16)
         )
+    fetch.wait()
+    off_ref[...] = (mask_s[...].astype(F32) - 1.0) * 1e30
     values = pair_ref[...].astype(F32).reshape(rows * cols, width)
     normed = normalize(values).astype(BF16)
     res = dot(weight_ref[...], normed, TN)
@@ -285,7 +306,7 @@
                 sp = u * 2 + v
 
                 def extra(n):
-                    return wide_s[n % 2] + off_ref[sp, pl.ds(n // 2, 1), :]
+                    return wide_s[n % 2] + off_ref[pl.ds(sp * 2 + n // 2, 1), :]
 
                 out = attend_tile(q_s[sp, span, :], k_s[sp], rhs_s.at[sp], masks, extra)
                 o_s[v] = out * g_s[sp, span, :]
@@ -356,6 +377,7 @@
     g_s,
     rhs_s,
     heads_s,
+    wcol_s,
     left_s,
     right_s,
     upd_s,
@@ -523,6 +545,14 @@
             arrived(region, u_recv.at[1, way, k])
             remote(region, region, u_send.at[2, way, k], u_recv.at[2, way, k], partner)
 
+    for part_index in range(4):
+        for group in range(2):
+            start = part_index * 256 + group * 128
+            lanes = slice(part_index % 2 * 64, part_index % 2 * 64 + 64)
+            wcol_s[:, start : start + 128] = beside(
+                wcol_ref[2 * group, part_index // 2, :, lanes],
+                wcol_ref[2 * group + 1, part_index // 2, :, lanes],
+            )
     pieces = [a_ref[:, b].astype(F32).reshape(SEQS, 128).astype(BF16) for b in range(4)]
     moved = dot(jnp.concatenate(pieces, axis=1), wrow_ref[...])
     for j in range(4):
@@ -557,7 +587,7 @@
 
             def project(part_index):
                 start = part_index * 256 + group * 128
-                return dot(n_s[...], wcol_ref[:, start : start + 128])
+                return dot(n_s[...], wcol_s[:, start : start + 128])
 
             q_s[group] = (project(0) * QUERY_SCALE).astype(BF16)
             k_s[group] = project(1).astype(BF16)
@@ -691,11 +721,6 @@
     vmem = pltpu.VMEM
 
     dma = pltpu.SemaphoreType.DMA
-    half = jnp.transpose(row_proj_weight, (1, 0, 2))
-    none = jnp.zeros_like(half)
-    wrow = jnp.concatenate(
-        [jnp.concatenate([half, none], axis=2), jnp.concatenate([none, half], axis=2)], axis=0
-    ).reshape(512, 512)
     out_half = row_out_weight.reshape(4, 64, 256)
     out_none = jnp.zeros_like(out_half)
     wrow_out = jnp.concatenate(
@@ -706,19 +731,16 @@
         axis=1,
     ).reshape(512, 512)
 
-    seq_mask = lax.dynamic_slice_in_dim(align_mask, dap * 8, 8, 0).astype(F32)
-    offset = ((seq_mask - 1.0) * 1e30).reshape(4, 2, SEQS)
-    wcol_mine = jnp.transpose(column_proj_weight, (1, 0, 2)).reshape(256, 256)
     res_mask = lax.dynamic_slice_in_dim(align_mask, dap * 8 + branch * 2, 2, 1).astype(F32)
     res_mask = jnp.transpose(res_mask.reshape(256, 2, 2), (2, 1, 0)).reshape(2, 1, SEQS)
     got, residual, wcol = pl.pallas_call(
         front_kernel,
-        in_specs=[pl.BlockSpec(memory_space=vmem)] * 6,
+        in_specs=[pl.BlockSpec(memory_space=vmem)] * 5 + [pl.BlockSpec(memory_space=pl.ANY)],
         out_specs=(pl.BlockSpec(memory_space=vmem),) * 3,
         out_shape=(
             jax.ShapeDtypeStruct((256, 8, 128), BF16),
             jax.ShapeDtypeStruct((64, 16, 256), BF16),
-            jax.ShapeDtypeStruct((4, 256, 256), BF16),
+            jax.ShapeDtypeStruct((4, 2, 256, 128), BF16),
         ),
         scratch_shapes=[
             vmem((4, 2, 8, 128), BF16),
@@ -735,6 +757,11 @@
             vmem((2, 128, 128), F32),
             vmem((SEQS, 128), F32),
             vmem((256, 8, 128), BF16),
+            vmem((2, 256, 128), BF16),
+            vmem((SEQS, SEQS), BF16),
+            vmem((8, SEQS), jnp.int32),
+            vmem((8, SEQS), F32),
+            dma,
             pltpu.SemaphoreType.REGULAR,
             dma((32,)),
             dma((32,)),
@@ -751,8 +778,7 @@
             vmem_limit_bytes=VMEM_LIMIT, collective_id=1, has_side_effects=True
         ),
         name="row_attention",
-    )(pair_rep, bias_weight, wcol_mine, alignment, wrow, offset)
-    wcol = jnp.transpose(wcol.reshape(4, 256, 4, 64), (1, 2, 0, 3)).reshape(256, 1024)
+    )(pair_rep, bias_weight, column_proj_weight, alignment, row_proj_weight, align_mask)
 
     gathered, pairs = pl.pallas_call(
         back_kernel,
@@ -772,6 +798,7 @@
             vmem((2, SEQS, 128), F32),
             vmem((2, 4 * SEQS, 256), BF16),
             vmem((SEQS, 256), BF16),
+            vmem((256, 1024), BF16),
             vmem((2, FACTOR, SEQS), BF16),
             vmem((2, FACTOR, SEQS), BF16),
             vmem((2, SEQS, 256), BF16),

time: 122 us -> 117 us (0.959); the launches traced: 120 us -> 117 us
  other arithmetic: 5.63 us -> 1.93 us
    unnamed x16, local copies, waits for them, and re-layouts: 1.48 us -> 5.94 us
    reshape x4 -> x0, local copies, waits for them, and re-layouts: 3.39 us -> none  [the longest x1 1.01 us: per_device(): jnp.transpose(wcol.reshape(4, 256, 4, 64), (1, 2, 0, 3)).reshape(256, 1024)]
    pallas_call x1 -> x0, local copies, waits for them, and re-layouts: 1.28 us -> none  [per_device(): pl.pallas_call(front_kernel, in_specs=[pl.BlockSpec(memory_space=vmem)] *...]
where the time goes in v6:
time: 117 us
  Pallas kernels  101 us (86%)
  local copies, waits for them, and re-layouts  12.9 us (11%)
  other arithmetic  1.93 us (2%)
    pallas_call x1, Pallas kernels, per_device(): pl.pallas_call(front_kernel, in_specs=[pl.BlockSpec(memory_space=vmem)] *...  53.1 us
    pallas_call x1, Pallas kernels, per_device(): pl.pallas_call(back_kernel, in_specs=[pl.BlockSpec(memory_space=vmem)] *...  47.6 us
    unnamed x16, local copies, waits for them, and re-layouts  5.94 us
    transpose x1, local copies, waits for them, and re-layouts, per_device(): rows = jnp.transpose(gathered.reshape(4, 2, 2, 256, 256), (3, 2, 0, 1, 4))  3.75 us

profile of v6, /device:TPU:32, one launch (start us, length us, event | category | flops | bytes accessed | tf_op | source)
XLA Modules:
  0.0 116.5 jit_solution(6086793338134026047)
XLA Ops:
  0.6 1.4 %copy.13.weight_ref = bf16[128,8]{1,0:T(8,128)(2,1)} copy(bf16[128,8]{0,1:T(8,128)(2,1)} %param.15) | data formatting | bytes 4096 | tf_op args[4]
  2.0 1.7 %copy.14.column_ref = bf16[4,256,64]{2,1,0:T(8,128)(2,1)} copy(bf16[4,256,64]{1,2,0:T(8,128)(2,1)} %param.18) | data formatting | bytes 262144 | tf_op args[7]
  3.8 1.8 %copy.15.row_ref = bf16[4,256,64]{2,1,0:T(8,128)(2,1)} copy(bf16[4,256,64]{1,2,0:T(8,128)(2,1)} %param.16) | data formatting | bytes 262144 | tf_op args[5]
  5.5 53.1 %row_attention.1 = (bf16[256,8,128]{2,1,0:T(8,128)(2,1)}, bf16[64,16,256]{2,1,0:T(8,128)(2,1)}, bf16[4,2,256,128]{3,2,1,0:T(8,128)(2,1)}) custom-call(bf16[8,128,128]{2,1,0:T(8,128)(2,1)} %pair_ref.1, bf16[128,8]{1,0:T(8,128)(2,1)} %copy.13.weight_ref, bf16[4,256,64]{2,1,0:T(8,128)(2,1)} %copy.14.column_ref, bf16[8,512,256]{2,1,0:T(8,128)(2,1)} %x_ref.1, ...), custom_call_target="tpu_custom_call" | custom-call | tf_op jit(solution)/shard_map/row_attention/pallas_call | solution.py:736
  58.6 0.0 copy-done.3
  58.7 0.8 fusion.3
  59.5 0.0 copy-done.4
  59.5 0.7 copy.17.wfac_ref
  60.2 0.0 copy-done
  60.2 0.1 dynamic-slice_convert_fusion.2
  60.4 0.1 copy.16
  60.5 0.6 reshape.38.mask_ref
  61.1 47.6 %column_outer.1 = (bf16[4,2,512,256]{3,2,1,0:T(8,128)(2,1)}, bf16[4,8,8,512]{3,2,1,0:T(8,128)(2,1)}) custom-call(bf16[64,4,8,128]{3,2,1,0:T(8,128)(2,1)} %bitcast.17, bf16[64,16,256]{2,1,0:T(8,128)(2,1)} %get-tuple-element.8.res_ref, bf16[512,512]{1,0:T(8,128)(2,1)} %bitcast.13, bf16[4,2,256,128]{3,2,1,0:T(8,128)(2,1)} %get-tuple-element.9.wcol_ref, ...), custom_call_target="tpu_custom_call" | custom-call | tf_op jit(solution)/shard_map/column_outer/pallas_call | solution.py:783
  108.7 3.7 %copy.18 = bf16[256,2,4,2,256]{4,3,2,1,0:T(2,128)(2,1)S(1)} copy(bf16[256,2,4,2,256]{4,0,1,3,2:T(8,128)(2,1)} %bitcast.14) | data formatting | bytes 4194304 | tf_op jit(solution)/shard_map/transpose | solution.py:845
  112.4 0.0 copy-start.2
  112.4 0.0 copy-start.5
  112.5 2.2 %reshape.40 = bf16[512,8,256]{2,1,0:T(8,128)(2,1)} reshape(bf16[256,2,4,2,256]{4,3,2,1,0:T(2,128)(2,1)S(1)} %copy.18) | data formatting | bytes 4194304 | tf_op jit(solution)/shard_map/reshape | solution.py:846
  114.7 0.0 copy-done.2
  114.7 0.1 copy.19
  114.9 0.1 dynamic_slice.17
  115.0 0.1 dynamic_slice.16
  115.1 0.3 fusion
  115.3 0.3 copy-done.1
  115.6 0.9 add_convert_fusion
  (7 shorter events, 0.1 us)
Async XLA Ops:
  3.8 54.9 %copy-start.3 = (bf16[256,256]{1,0:T(8,128)(2,1)S(1)}, bf16[256,256]{1,0:T(8,128)(2,1)}, u32[]{:S(2)}) copy-start(bf16[256,256]{1,0:T(8,128)(2,1)} %param.17) | copy-start | bytes 393220
  5.5 54.0 %copy-start.4 = (bf16[256,64]{0,1:T(8,128)(2,1)S(1)}, bf16[256,64]{0,1:T(8,128)(2,1)}, u32[]{:S(2)}) copy-start(bf16[256,64]{0,1:T(8,128)(2,1)} %param.20) | copy-start | bytes 98308
  5.5 54.7 %copy-start = (s32[512,512]{1,0:T(8,128)S(1)}, s32[512,512]{1,0:T(8,128)}, u32[]{:S(2)}) copy-start(s32[512,512]{1,0:T(8,128)} %mask_ref.1) | copy-start | bytes 3145732
  112.4 2.2 %copy-start.2 = (bf16[4,8,8,512]{3,2,1,0:T(8,128)(2,1)S(1)}, bf16[4,8,8,512]{3,2,1,0:T(8,128)(2,1)}, u32[]{:S(2)}) copy-start(bf16[4,8,8,512]{3,2,1,0:T(8,128)(2,1)} %get-tuple-element.11) | copy-start | bytes 786436
  112.4 2.4 %copy-start.5 = (s32[512]{0:T(512)S(1)}, s32[512]{0:T(512)}, u32[]{:S(2)}) copy-start(s32[512]{0:T(512)} %param.14) | copy-start | bytes 6148
  114.7 0.9 copy-start.1

commit v7 on v6

--- a/solution.py
+++ b/solution.py
@@ -699,8 +699,16 @@
         arrived(pair_ref.at[slot], p_recv.at[slot])
 
 
-def whole(shape):
-    return pl.BlockSpec(shape, lambda *_: (0,) * len(shape))
+def assemble_kernel(in_ref, out_ref, rows_s):
+    for b in range(4):
+        for k in range(2):
+            for p in range(2):
+                for side in range(2):
+                    block = in_ref[b, k, p, :, side * 128 : side * 128 + 128].astype(F32)
+                    rows_s[side, pl.ds(p * 8 + b * 2 + k, 32, stride=16), :] = block
+    for side in range(2):
+        block = rows_s[side].reshape(64, 8, 128)
+        out_ref[:, :, side * 128 : side * 128 + 128] = block.astype(BF16)
 
 
 def per_device(
@@ -842,8 +850,15 @@
         outer_out,
     )
 
-    rows = jnp.transpose(gathered.reshape(4, 2, 2, 256, 256), (3, 2, 0, 1, 4))
-    updated_alignment = rows.reshape(SEQS, 8, 256)
+    updated_alignment = pl.pallas_call(
+        assemble_kernel,
+        grid=(8,),
+        in_specs=[pl.BlockSpec((4, 2, 2, 32, 256), lambda i: (0, 0, 0, i, 0))],
+        out_specs=pl.BlockSpec((64, 8, 256), lambda i: (i, 0, 0)),
+        out_shape=jax.ShapeDtypeStruct((SEQS, 8, 256), BF16),
+        scratch_shapes=[vmem((2, 512, 128), F32)],
+        name="assemble",
+    )(gathered.reshape(4, 2, 2, 256, 256))
 
     mask_rows = lax.dynamic_slice_in_dim(align_mask, dap * 8, 8, 1).astype(BF16)
     mask_cols = lax.dynamic_slice_in_dim(align_mask, branch * 128, 128, 1).astype(BF16)

time: 117 us -> 118 us (level)
  Pallas kernels: 101 us -> 107 us
  local copies, waits for them, and re-layouts: 12.9 us -> 6.97 us
    pallas_call x0 -> x1, Pallas kernels: none -> 6.67 us  [per_device(): pl.pallas_call(assemble_kernel, grid=(8,), in_specs=[pl.BlockSpec((4, 2,...]
    transpose x1 -> x0, local copies, waits for them, and re-layouts: 3.75 us -> none  [per_device(): rows = jnp.transpose(gathered.reshape(4, 2, 2, 256, 256), (3, 2, 0, 1, 4))]
    reshape x1 -> x0, local copies, waits for them, and re-layouts: 2.21 us -> none  [per_device(): updated_alignment = rows.reshape(SEQS, 8, 256)]
where the time goes in v7:
time: 118 us; the launch traced here: 117 us
  Pallas kernels  107 us (91%)
  local copies, waits for them, and re-layouts  6.97 us (6%)
  other arithmetic  1.93 us (2%)
    pallas_call x1, Pallas kernels, per_device(): pl.pallas_call(front_kernel, in_specs=[pl.BlockSpec(memory_space=vmem)] *...  53.1 us
    pallas_call x1, Pallas kernels, per_device(): pl.pallas_call(back_kernel, in_specs=[pl.BlockSpec(memory_space=vmem)] *...  47.5 us
    pallas_call x1, Pallas kernels, per_device(): pl.pallas_call(assemble_kernel, grid=(8,), in_specs=[pl.BlockSpec((4, 2,...  6.67 us
    unnamed x16, local copies, waits for them, and re-layouts  5.94 us

profile of v7, /device:TPU:32, one launch (start us, length us, event | category | flops | bytes accessed | tf_op | source)
XLA Modules:
  0.0 117.2 jit_solution(12493892997024494751)
XLA Ops:
  0.6 1.4 %copy.13.weight_ref = bf16[128,8]{1,0:T(8,128)(2,1)} copy(bf16[128,8]{0,1:T(8,128)(2,1)} %param.15) | data formatting | bytes 4096 | tf_op args[4]
  2.0 1.7 %copy.14.column_ref = bf16[4,256,64]{2,1,0:T(8,128)(2,1)} copy(bf16[4,256,64]{1,2,0:T(8,128)(2,1)} %param.18) | data formatting | bytes 262144 | tf_op args[7]
  3.8 1.8 %copy.15.row_ref = bf16[4,256,64]{2,1,0:T(8,128)(2,1)} copy(bf16[4,256,64]{1,2,0:T(8,128)(2,1)} %param.16) | data formatting | bytes 262144 | tf_op args[5]
  5.5 53.1 %row_attention.1 = (bf16[256,8,128]{2,1,0:T(8,128)(2,1)}, bf16[64,16,256]{2,1,0:T(8,128)(2,1)}, bf16[4,2,256,128]{3,2,1,0:T(8,128)(2,1)}) custom-call(bf16[8,128,128]{2,1,0:T(8,128)(2,1)} %pair_ref.1, bf16[128,8]{1,0:T(8,128)(2,1)} %copy.13.weight_ref, bf16[4,256,64]{2,1,0:T(8,128)(2,1)} %copy.14.column_ref, bf16[8,512,256]{2,1,0:T(8,128)(2,1)} %x_ref.1, ...), custom_call_target="tpu_custom_call" | custom-call | tf_op jit(solution)/shard_map/row_attention/pallas_call | solution.py:744
  58.6 0.0 copy-done.3
  58.7 0.8 fusion.3
  59.5 0.0 copy-done.4
  59.5 0.7 copy.17.wfac_ref
  60.2 0.0 copy-done
  60.2 0.1 dynamic-slice_convert_fusion.2
  60.4 0.1 copy.16
  60.5 0.6 reshape.35.mask_ref
  61.1 47.5 %column_outer.1 = (bf16[4,2,512,256]{3,2,1,0:T(8,128)(2,1)}, bf16[4,8,8,512]{3,2,1,0:T(8,128)(2,1)}) custom-call(bf16[64,4,8,128]{3,2,1,0:T(8,128)(2,1)} %bitcast.15, bf16[64,16,256]{2,1,0:T(8,128)(2,1)} %get-tuple-element.8.res_ref, bf16[512,512]{1,0:T(8,128)(2,1)} %bitcast.11, bf16[4,2,256,128]{3,2,1,0:T(8,128)(2,1)} %get-tuple-element.9.wcol_ref, ...), custom_call_target="tpu_custom_call" | custom-call | tf_op jit(solution)/shard_map/column_outer/pallas_call | solution.py:791
  108.7 0.0 copy-start.2
  108.7 0.0 copy-start.5
  108.7 6.7 %assemble.1 = bf16[512,8,256]{2,1,0:T(8,128)(2,1)} custom-call(bf16[4,2,2,256,256]{4,3,2,1,0:T(8,128)(2,1)} %bitcast.12), custom_call_target="tpu_custom_call" | custom-call | tf_op jit(solution)/shard_map/assemble/pallas_call | solution.py:853
  115.3 0.0 copy-done.2
  115.4 0.1 copy.18
  115.6 0.0 copy-done.5
  115.6 0.1 dynamic_slice.17
  115.7 0.1 dynamic_slice.16
  115.7 0.3 fusion
  116.0 0.3 copy-done.1
  116.3 0.9 add_convert_fusion
  (6 shorter events, 0.1 us)
Async XLA Ops:
  3.8 54.9 %copy-start.3 = (bf16[256,256]{1,0:T(8,128)(2,1)S(1)}, bf16[256,256]{1,0:T(8,128)(2,1)}, u32[]{:S(2)}) copy-start(bf16[256,256]{1,0:T(8,128)(2,1)} %param.17) | copy-start | bytes 393220
  5.5 54.0 %copy-start.4 = (bf16[256,64]{0,1:T(8,128)(2,1)S(1)}, bf16[256,64]{0,1:T(8,128)(2,1)}, u32[]{:S(2)}) copy-start(bf16[256,64]{0,1:T(8,128)(2,1)} %param.20) | copy-start | bytes 98308
  5.5 54.7 %copy-start = (s32[512,512]{1,0:T(8,128)S(1)}, s32[512,512]{1,0:T(8,128)}, u32[]{:S(2)}) copy-start(s32[512,512]{1,0:T(8,128)} %mask_ref.1) | copy-start | bytes 3145732
  108.7 6.7 %copy-start.2 = (bf16[4,8,8,512]{3,2,1,0:T(8,128)(2,1)S(1)}, bf16[4,8,8,512]{3,2,1,0:T(8,128)(2,1)}, u32[]{:S(2)}) copy-start(bf16[4,8,8,512]{3,2,1,0:T(8,128)(2,1)} %get-tuple-element.11) | copy-start | bytes 786436
  108.7 6.9 %copy-start.5 = (s32[512]{0:T(512)S(1)}, s32[512]{0:T(512)}, u32[]{:S(2)}) copy-start(s32[512]{0:T(512)} %param.14) | copy-start | bytes 6148
  115.3 0.9 copy-start.1
